TPU v7x, 32 devices: a whole 2x2x4 slice. The times are simulated.
32 devices in a mesh: grp: 4 (over x, core), dev: 8 (over z, y).
Axes of the slice: x: 2, y: 2, z: 4, core: 2. Of those that a mesh axis runs over, the one named last changes fastest.
Arguments:
- gradient: bfloat16 [8, 512, 2048], P('grp', 'dev'), may hold values from -400 to 400
- momentum: float32 [32, 512, 512], P(('grp', 'dev')), may hold values from -8 to 8
- master_weight: float32 [32, 512, 512], P(('grp', 'dev')), may hold values from -0.12 to 0.12
- owned_matrix: int32 [4, 2], replicated, may hold values from 0 to 1, each once within a row
- rollout_matrix: int32 [4, 8], P('grp'), may hold values from 0 to 7, each once within a row
Outputs:
- new_momentum: float32 [32, 512, 512], P(('grp', 'dev'))
- update: float32 [32, 512, 512], P(('grp', 'dev'))
- new_master: float32 [32, 512, 512], P(('grp', 'dev'))
- rollout_weight: bfloat16 [32, 512, 2048], P(('grp', 'dev'))
Inputs may be any that keep to these rules, and one draw needn't show every extreme that they name: Each row of owned_matrix lists every number 0 to 1 once. Each row of rollout_matrix lists every matrix 0 to 7 once.
All inputs are finite; a program needn't handle non-finite values.
Results may differ from a plain program's by a relative error of at most 0.001.
Values may be sent and summed in bfloat16 or wider, within the bound.
No kernel may reach another device: no remote copies, remote signals or barrier semaphores. Data moves between devices by JAX's collectives and lax.ppermute only.
A program may use at most 64 MiB of HBM per device.

v0:
```python
import functools
import math

import jax
import jax.numpy as jnp
from jax import lax
from jax.experimental import pallas as pl
from jax.experimental.pallas import tpu as pltpu
from jax.sharding import PartitionSpec as P

ITERS = 5
PACK = 4


momentum_decay = 0.95
learn_rate = 0.02
weight_decay = 0.1
first_coeff = 3.4445
second_coeff = -4.775
third_coeff = 2.0315
norm_epsilon = 1e-07


def from_partner(block, axis, bit):
    count = lax.axis_size(axis)
    route = []
    for low in range(count):
        high = low | 1 << bit
        if high != low and high < count:
            route += [(low, high), (high, low)]
    return lax.ppermute(block, axis, route)


def product(left, right, precision=lax.Precision.HIGHEST):
    return jnp.dot(left, right, precision=precision, preferred_element_type=jnp.float32)


def pack_upper(full):
    step = full.shape[0] // PACK
    rows = [full[i * step : (i + 1) * step, i * step :] for i in range(PACK)]
    return [
        jnp.concatenate([rows[0], rows[3]], axis=1),
        jnp.concatenate([rows[1], rows[2]], axis=1),
    ]


def gram_sum(slab_part, share_count):
    halves = pack_upper(product(slab_part, slab_part.T))
    moved = [jnp.zeros_like(half) for half in halves]
    bits = list(range(share_count.bit_length() - 1))
    orders = [bits, bits[::-1]]
    for turn in range(len(bits)):
        halves = [half + other for half, other in zip(halves, moved)] if turn else halves
        moved = [from_partner(half, "dev", order[turn]) for half, order in zip(halves, orders)]
    return halves, moved


def parts_of(value, count):
    parts = []
    for _ in range(count - 1):
        high = value.astype(jnp.bfloat16)
        parts.append(high)
        value = value - high.astype(jnp.float32)
    return parts + [value.astype(jnp.bfloat16)]


def split_product(left, right):
    count = len(left)
    total = None
    for order in range(count - 1, -1, -1):
        for i in range(order + 1):
            term = jnp.dot(left[i], right[order - i], preferred_element_type=jnp.float32)
            total = term if total is None else total + term
    return total


def newton_kernel(iters, scale, a0, a1, b0, b1, p_ref, w_ref, u_ref, n_ref, r_ref, gram, cur):
    rows = gram.shape[0]
    step = rows // PACK
    halves = [a0[...] + a1[...], b0[...] + b1[...]]
    bands = [
        halves[0][:, : 4 * step],
        halves[1][:, : 3 * step],
        halves[1][:, 3 * step :],
        halves[0][:, 4 * step :],
    ]
    eye = lax.broadcasted_iota(jnp.int32, (step, step), 0) == lax.broadcasted_iota(
        jnp.int32, (step, step), 1
    )
    diag = sum(jnp.where(eye, band[:, :step], 0.0) for band in bands)
    norm_sq = jnp.sum(jnp.sum(diag, axis=1, keepdims=True), axis=0, keepdims=True)
    factor = 1.0 / (jnp.sqrt(norm_sq) + norm_epsilon)
    square = factor * factor
    for i, band in enumerate(bands):
        scaled = band * square
        gram[i * step : (i + 1) * step, i * step :] = scaled
        for j in range(i + 1, PACK):
            gram[j * step : (j + 1) * step, i * step : (i + 1) * step] = scaled[
                :, (j - i) * step : (j - i + 1) * step
            ].T
    cur[...] = p_ref[...] * factor

    def mixed_of(a, a_parts):
        return second_coeff * a + third_coeff * split_product(a_parts[:2], a_parts[:2])

    def apply(mixed_parts):
        x = cur[...]
        return first_coeff * x + split_product(mixed_parts[:2], parts_of(x, 2))

    def advance(count):
        a = gram[...]
        a_parts = parts_of(a, count)
        mixed_parts = parts_of(mixed_of(a, a_parts if count == 2 else parts_of(a, 2)), count)
        half_way = first_coeff * a + split_product(mixed_parts, a_parts)
        gram[...] = first_coeff * half_way + split_product(parts_of(half_way, count), mixed_parts)
        cur[...] = apply(mixed_parts)

    advance(3)
    if iters > 2:
        lax.fori_loop(1, iters - 1, lambda _, none: (advance(2), none)[1], 0)
    a = gram[...]
    u = apply(parts_of(mixed_of(a, parts_of(a, 2)), 2)) * scale
    w = w_ref[...]
    new = w - learn_rate * (u + weight_decay * w)
    r_ref[...] = new.astype(r_ref.dtype)
    u_ref[...] = u
    n_ref[...] = new


def newton(halves, moved, nesterov, master, iters, scale):
    rows, cols = nesterov.shape
    vmem = pl.BlockSpec(memory_space=pltpu.VMEM)
    f32 = jax.ShapeDtypeStruct((rows, cols), jnp.float32)
    return pl.pallas_call(
        functools.partial(newton_kernel, iters, scale),
        out_shape=[f32, f32, jax.ShapeDtypeStruct((rows, cols), jnp.bfloat16)],
        in_specs=[vmem] * 6,
        out_specs=[vmem] * 3,
        scratch_shapes=[pltpu.VMEM((rows, rows), jnp.float32), pltpu.VMEM((rows, cols), jnp.float32)],
        cost_estimate=pl.CostEstimate(
            flops=2 * 60 * rows * rows * cols, bytes_accessed=24 * rows * cols, transcendentals=0
        ),
        compiler_params=pltpu.CompilerParams(vmem_limit_bytes=40 << 20),
    )(halves[0], moved[0], halves[1], moved[1], nesterov, master)


def flipped(block, axis, flip):
    return lax.ppermute(block, axis, [(i, i ^ flip) for i in range(lax.axis_size(axis))])


def choose(items, index):
    bit = 0
    while len(items) > 1:
        odd = (index >> bit) & 1 == 1
        items = [jnp.where(odd, items[i + 1], items[i]) for i in range(0, len(items), 2)]
        bit += 1
    return items[0]


def owner_of(owned_matrix, quads):
    ids = jnp.arange(quads, dtype=jnp.int32)
    return jnp.sum(
        jnp.where(owned_matrix[:, :, None] == ids[None, None, :], ids[None, :, None], 0), axis=1
    ).reshape(-1)


def wanted_slots(rollout_matrix, owned_matrix, share_count):
    quads = owned_matrix.shape[1]
    group = lax.axis_index("grp")
    place = lax.axis_index("dev")
    inverse = owner_of(owned_matrix, quads)
    mats = jnp.arange(inverse.shape[0], dtype=jnp.int32)
    targets = rollout_matrix[0]
    owner = jnp.sum(jnp.where(targets[:, None] == mats[None, :], inverse[None, :], 0), axis=1)
    slot = ((targets // quads) ^ group) * quads + (owner ^ (place // share_count))
    return [
        lax.dynamic_index_in_dim(slot, place ^ turn, 0, keepdims=False)
        for turn in range(share_count)
    ]


def lay_kernel(share_count, *refs):
    mine = lax.axis_index("dev") % share_count
    blocks, out, done = refs[:share_count], refs[-2], refs[-1]
    cols = blocks[0].shape[1]
    moves = []
    for turn, block in enumerate(blocks):
        start = pl.multiple_of((mine ^ turn) * cols, cols)
        moves.append(
            pltpu.make_async_copy(block, out.at[:, pl.ds(start, cols)], done.at[turn])
        )
    for move in moves:
        move.start()
    for move in moves:
        move.wait()


def lay(blocks):
    share_count = len(blocks)
    rows, cols = blocks[0].shape
    return pl.pallas_call(
        functools.partial(lay_kernel, share_count),
        out_shape=jax.ShapeDtypeStruct((rows, cols * share_count), blocks[0].dtype),
        in_specs=[pl.BlockSpec(memory_space=pltpu.VMEM)] * share_count,
        out_specs=pl.BlockSpec(memory_space=pltpu.HBM),
        scratch_shapes=[pltpu.SemaphoreType.DMA((share_count,))],
    )(*blocks)


def sync_two_halves(rounded, slots, share_count):
    group_count = lax.axis_size("grp")
    tables = []
    for start in (rounded, flipped(rounded, "dev", share_count)):
        table = {0: start}
        for bit in range(group_count.bit_length() - 2, -1, -1):
            for key in list(table):
                table[key | 1 << bit] = flipped(table[key], "grp", 1 << bit)
        tables.append(table)
    slabs = [table[key] for key in range(group_count) for table in tables]
    picked = [choose(slabs, slot) for slot in slots]
    return lay(
        [picked[0]] + [flipped(picked[turn], "dev", turn) for turn in range(1, share_count)]
    )


def sync_any(rounded, rollout_matrix, owned_matrix, row_block, columns):
    dev_count = lax.axis_size("dev")
    group_count = lax.axis_size("grp")
    quads = owned_matrix.shape[1]
    row_count, slab_cols = rounded.shape
    all_mats = group_count * quads
    slot_count = all_mats // dev_count
    own_rows = lax.all_to_all(
        rounded.reshape(dev_count, row_block, slab_cols),
        "dev",
        split_axis=0,
        concat_axis=2,
        tiled=True,
    )
    copies = lax.all_gather(own_rows, "grp", axis=0, tiled=True)
    blocks = copies.reshape(group_count, row_block, quads, columns)
    inverse_flat = owner_of(owned_matrix, quads)
    targets = rollout_matrix[0]
    global_ids = jnp.arange(all_mats, dtype=jnp.int32)
    target_group = targets // quads
    target_owner = jnp.sum(
        jnp.where(targets[:, None] == global_ids[None, :], inverse_flat[None, :], 0), axis=1
    )
    flat_owner = target_group * quads + target_owner
    chooser = (
        (flat_owner[:, None] == global_ids[None, :])
        .astype(jnp.bfloat16)
        .reshape(all_mats, group_count, quads)
    )
    outgoing = jnp.einsum(
        "pgq,grqc->prc", chooser, blocks, preferred_element_type=jnp.float32
    ).astype(jnp.bfloat16)
    landed = lax.all_to_all(
        outgoing.reshape(dev_count, slot_count, row_block, columns),
        "dev",
        split_axis=0,
        concat_axis=2,
        tiled=True,
    )
    return landed.reshape(slot_count, row_count, columns)


def shards(gradient, momentum, master_weight, owned_matrix, rollout_matrix):
    group = lax.axis_index("grp")
    dev_count = lax.axis_size("dev")
    group_count = lax.axis_size("grp")
    quads = gradient.shape[0]
    row_block = gradient.shape[1]
    columns = gradient.shape[2]
    slab_cols = momentum.shape[2]
    row_count = momentum.shape[1]
    share_count = columns // slab_cols
    two_halves = (
        quads == 2
        and dev_count == quads * share_count
        and not share_count & (share_count - 1)
        and not group_count & (group_count - 1)
    )
    mine = lax.dynamic_index_in_dim(owned_matrix, group, 0, keepdims=False)
    local_ids = jnp.arange(quads, dtype=jnp.int32)
    picker = (mine[:, None] == local_ids[None, :]).astype(jnp.bfloat16)
    ordered = jnp.einsum(
        "qm,mrc->rqc", picker, gradient, preferred_element_type=jnp.float32
    ).astype(jnp.bfloat16)
    arrived = lax.all_to_all(
        ordered.reshape(row_block, dev_count, slab_cols),
        "dev",
        split_axis=1,
        concat_axis=0,
        tiled=True,
    )
    grad_slab = arrived.reshape(row_count, slab_cols).astype(jnp.float32)
    new_moment = momentum_decay * momentum[0] + grad_slab
    nesterov = grad_slab + momentum_decay * new_moment
    if two_halves:
        slots = wanted_slots(rollout_matrix, owned_matrix, share_count)
        nesterov, slots = lax.optimization_barrier((nesterov, slots))
    halves, moved = gram_sum(nesterov, share_count)
    scale_factor = 0.2 * math.sqrt(max(row_count, columns))
    update, new_weight, rounded = newton(
        halves, moved, nesterov, master_weight[0], ITERS, scale_factor
    )
    if two_halves:
        rollout = sync_two_halves(rounded, slots, share_count)[None]
    else:
        rollout = sync_any(rounded, rollout_matrix, owned_matrix, row_block, columns)
    return (new_moment[None], update[None], new_weight[None], rollout)


def solution(mesh):
    placed = (
        P("grp", "dev", None),
        P(("grp", "dev"), None, None),
        P(("grp", "dev"), None, None),
        P(),
        P("grp", None),
    )
    return jax.shard_map(
        shards,
        mesh=mesh,
        in_specs=placed,
        out_specs=(
            P(("grp", "dev"), None, None),
            P(("grp", "dev"), None, None),
            P(("grp", "dev"), None, None),
            P(("grp", "dev"), None, None),
        ),
        check_vma=False,
    )
```

profile of v0, /device:TPU:0, one launch (start us, length us, event | category | flops | bytes accessed | tf_op | source)
XLA Modules:
  0.0 142.1 jit_solution(36996400521363706)
XLA Ops:
  0.7 0.9 dynamic-slice_reduce_fusion
  1.7 0.8 fusion
  2.6 0.9 copy.24
  3.6 7.3 %all-to-all-start = ((bf16[64,8,512]{2,0,1:T(8,128)(2,1)}), bf16[64,8,512]{2,0,1:T(8,128)(2,1)S(1)}, u32[]{:S(2)}, u32[]{:S(2)}) async-start(bf16[64,8,512]{2,0,1:T(8,128)(2,1)} %copy.24), calls=%async_computation | async-start | bytes 1048576 | tf_op jit(solution)/shard_map/all_to_all | solution.py:290
  11.3 0.7 fusion.8
  12.0 13.4 %all-to-all-done = bf16[64,8,512]{2,0,1:T(8,128)(2,1)S(1)} async-done(((bf16[64,8,512]{2,0,1:T(8,128)(2,1)}), bf16[64,8,512]{2,0,1:T(8,128)(2,1)S(1)}, u32[]{:S(2)}, u32[]{:S(2)}) %all-to-all-start) | async-done | bytes 524320 | tf_op jit(solution)/shard_map/all_to_all | solution.py:290
  25.4 0.2 bitcast_add_fusion.1.p_ref
  25.6 1.9 %fusion.9 = f32[512,512]{1,0:T(8,128)S(1)} fusion(f32[512,512]{1,0:T(8,128)S(1)} %bitcast_add_fusion.1.p_ref), kind=kOutput, calls=%fused_computation.29 | convolution fusion | flops 1610612736 | bytes 2097152 | tf_op jit(solution)/shard_map/dot_general | solution.py:35
  27.5 0.8 collective-permute-start.2
  28.4 0.8 collective-permute-start
  29.2 6.5 %collective-permute-done.2 = f32[128,640]{1,0:T(8,128)S(1)} collective-permute-done((f32[128,640]{1,0:T(8,128)S(1)}, f32[128,640]{1,0:T(8,128)S(1)}, u32[]{:S(2)}, u32[]{:S(2)}) %collective-permute-start.2) | collective-permute-done | bytes 327712 | tf_op jit(solution)/shard_map/ppermute | solution.py:31
  35.7 2.1 %collective-permute-start.3 = (f32[128,640]{1,0:T(8,128)S(1)}, f32[128,640]{1,0:T(8,128)S(1)}, u32[]{:S(2)}, u32[]{:S(2)}) collective-permute-start(f32[128,640]{1,0:T(8,128)S(1)} %fusion.6.b0), channel_id=1, source_target_pairs={{0,1},{1,0},{2,3},{3,2},{4,5},{5,4},{6,7},{7,6},{8,9},{9,8},{10,11... | collective-permute-start | bytes 983048 | tf_op jit(solution)/shard_map/ppermute | solution.py:31
  37.9 0.5 collective-permute-start.1
  38.4 5.6 %collective-permute-done.3.b1 = f32[128,640]{1,0:T(8,128)S(1)} collective-permute-done((f32[128,640]{1,0:T(8,128)S(1)}, f32[128,640]{1,0:T(8,128)S(1)}, u32[]{:S(2)}, u32[]{:S(2)}) %collective-permute-start.3) | collective-permute-done | bytes 327712 | tf_op jit(solution)/shard_map/ppermute | solution.py:31
  44.0 1.6 %collective-permute-done.1.a1 = f32[128,640]{1,0:T(8,128)S(1)} collective-permute-done((f32[128,640]{1,0:T(8,128)S(1)}, f32[128,640]{1,0:T(8,128)S(1)}, u32[]{:S(2)}, u32[]{:S(2)}) %collective-permute-start.1) | collective-permute-done | bytes 327712 | tf_op jit(solution)/shard_map/ppermute | solution.py:31
  45.6 19.1 %shard_map.84 = (f32[512,512]{1,0:T(8,128)}, f32[512,512]{1,0:T(8,128)}, bf16[512,512]{1,0:T(8,128)(2,1)S(1)}) custom-call(f32[128,640]{1,0:T(8,128)S(1)} %fusion.7.a0, f32[128,640]{1,0:T(8,128)S(1)} %collective-permute-done.1.a1, f32[128,640]{1,0:T(8,128)S(1)} %fusion.6.b0, f32[128,640]{1,0:T(8,128)S(1)} %collective-permute-done.3.b1, ...), custom_call_target="tpu_custom_call" | custom-call | flops 16106127360 | bytes 6291456 | tf_op jit(solution)/shard_map/pallas_call | solution.py:134
  64.7 2.4 %collective-permute-start.4 = (bf16[512,512]{1,0:T(8,128)(2,1)S(1)}, bf16[512,512]{1,0:T(8,128)(2,1)S(1)}, u32[]{:S(2)}, u32[]{:S(2)}) collective-permute-start(bf16[512,512]{1,0:T(8,128)(2,1)S(1)} %get-tuple-element.16), channel_id=1, source_target_pairs={{0,4},{1,5},{2,6},{3,7},{4,0},{5,1},{6,2},{7,3},{8,12},{9,13},{10,... | collective-permute-start | bytes 1572872 | tf_op jit(solution)/shard_map/ppermute | solution.py:148
  67.1 1.5 %collective-permute-start.7 = (bf16[512,512]{1,0:T(8,128)(2,1)S(1)}, bf16[512,512]{1,0:T(8,128)(2,1)}, u32[]{:S(2)}, u32[]{:S(2)}) collective-permute-start(bf16[512,512]{1,0:T(8,128)(2,1)S(1)} %get-tuple-element.16), channel_id=1, source_target_pairs={{0,16},{8,24},{16,0},{24,8},{1,17},{9,25},{17,1},{25,9},{2,18},{10... | collective-permute-start | bytes 1572872 | tf_op jit(solution)/shard_map/ppermute | solution.py:148
  68.6 20.1 %collective-permute-done.4 = bf16[512,512]{1,0:T(8,128)(2,1)S(1)} collective-permute-done((bf16[512,512]{1,0:T(8,128)(2,1)S(1)}, bf16[512,512]{1,0:T(8,128)(2,1)S(1)}, u32[]{:S(2)}, u32[]{:S(2)}) %collective-permute-start.4) | collective-permute-done | bytes 524320 | tf_op jit(solution)/shard_map/ppermute | solution.py:148
  88.7 1.5 %collective-permute-start.5 = (bf16[512,512]{1,0:T(8,128)(2,1)S(1)}, bf16[512,512]{1,0:T(8,128)(2,1)}, u32[]{:S(2)}, u32[]{:S(2)}) collective-permute-start(bf16[512,512]{1,0:T(8,128)(2,1)S(1)} %collective-permute-done.4), channel_id=1, source_target_pairs={{0,16},{8,24},{16,0},{24,8},{1,17},{9,25},{17,1},{25,9},{2,18},{10... | collective-permute-start | bytes 1572872 | tf_op jit(solution)/shard_map/ppermute | solution.py:148
  90.2 0.5 collective-permute-start.9
  90.7 11.3 %collective-permute-done.5 = bf16[512,512]{1,0:T(8,128)(2,1)} collective-permute-done((bf16[512,512]{1,0:T(8,128)(2,1)S(1)}, bf16[512,512]{1,0:T(8,128)(2,1)}, u32[]{:S(2)}, u32[]{:S(2)}) %collective-permute-start.5) | collective-permute-done | bytes 524320 | tf_op jit(solution)/shard_map/ppermute | solution.py:148
  109.9 2.2 %select_select_fusion = (bf16[512,512]{1,0:T(8,128)(2,1)S(1)}, bf16[512,512]{1,0:T(8,128)(2,1)S(1)}, bf16[512,512]{1,0:T(8,128)(2,1)S(1)}) fusion(bf16[512,512]{1,0:T(8,128)(2,1)S(1)} %collective-permute-done.4, bf16[512,512]{1,0:T(8,128)(2,1)S(1)} %get-tuple-element.16, bf16[512,512]{1,0:T(8,128)(2,1)} %collective-permute-done.9, ...), kind=kLoop, calls=%fused_computation.6 | loop fusion | flops 5505024 | bytes 5767177 | tf_op jit(solution)/shard_map/jit(_where)/select_n | solution.py:155
  112.2 1.3 collective-permute-start.11
  113.5 2.2 %collective-permute-start.13 = (bf16[512,512]{1,0:T(8,128)(2,1)S(1)}, bf16[512,512]{1,0:T(8,128)(2,1)}, u32[]{:S(2)}, u32[]{:S(2)}) collective-permute-start(bf16[512,512]{1,0:T(8,128)(2,1)S(1)} %get-tuple-element.20), channel_id=1, source_target_pairs={{0,3},{1,2},{2,1},{3,0},{4,7},{5,6},{6,5},{7,4},{8,11},{9,10},{10,... | collective-permute-start | bytes 1572872 | tf_op jit(solution)/shard_map/ppermute | solution.py:148
  115.7 1.1 bitcast_add_fusion
  116.8 2.3 %select_select_fusion.3.refs_0_ = bf16[512,512]{1,0:T(8,128)(2,1)} fusion(bf16[512,512]{1,0:T(8,128)(2,1)S(1)} %collective-permute-done.4, bf16[512,512]{1,0:T(8,128)(2,1)S(1)} %get-tuple-element.16, bf16[512,512]{1,0:T(8,128)(2,1)} %collective-permute-done.9, bf16[512,512]{1,0:T(8,128)(2,1)} %collective-permute-done.10, ...), kind=kLoop, calls=%fused_computation.9 | loop fusion | flops 1835008 | bytes 4718595 | tf_op jit(solution)/shard_map/jit(_where)/select_n | solution.py:155
  119.2 7.4 %collective-permute-done.11.refs_1_ = bf16[512,512]{1,0:T(8,128)(2,1)S(1)} collective-permute-done((bf16[512,512]{1,0:T(8,128)(2,1)S(1)}, bf16[512,512]{1,0:T(8,128)(2,1)S(1)}, u32[]{:S(2)}, u32[]{:S(2)}) %collective-permute-start.11) | collective-permute-done | bytes 524320 | tf_op jit(solution)/shard_map/ppermute | solution.py:148
  126.6 1.7 %collective-permute-done.12.refs_2_ = bf16[512,512]{1,0:T(8,128)(2,1)S(1)} collective-permute-done((bf16[512,512]{1,0:T(8,128)(2,1)S(1)}, bf16[512,512]{1,0:T(8,128)(2,1)S(1)}, u32[]{:S(2)}, u32[]{:S(2)}) %collective-permute-start.12) | collective-permute-done | bytes 524320 | tf_op jit(solution)/shard_map/ppermute | solution.py:148
  128.3 0.8 copy-done.4
  129.1 10.0 %collective-permute-done.13.refs_3_ = bf16[512,512]{1,0:T(8,128)(2,1)} collective-permute-done((bf16[512,512]{1,0:T(8,128)(2,1)S(1)}, bf16[512,512]{1,0:T(8,128)(2,1)}, u32[]{:S(2)}, u32[]{:S(2)}) %collective-permute-start.13) | collective-permute-done | bytes 524320 | tf_op jit(solution)/shard_map/ppermute | solution.py:148
  139.1 2.9 %shard_map.85 = bf16[512,2048]{1,0:T(8,128)(2,1)} custom-call(bf16[512,512]{1,0:T(8,128)(2,1)} %select_select_fusion.3.refs_0_, bf16[512,512]{1,0:T(8,128)(2,1)} %copy-done.3, bf16[512,512]{1,0:T(8,128)(2,1)} %copy-done.4, bf16[512,512]{1,0:T(8,128)(2,1)} %collective-permute-done.13.refs_3_), custom_call_target="tpu_custom_call" | custom-call | tf_op jit(solution)/shard_map/pallas_call | solution.py:201
  (37 shorter events, 0.9 us)
Async XLA Ops:
  0.6 1.1 copy-start
  2.5 8.4 %copy-start.5 = (s32[4,2]{0,1:T(2,128)S(1)}, s32[4,2]{0,1:T(2,128)}, u32[]{:S(2)}) copy-start(s32[4,2]{0,1:T(2,128)} %param.8) | copy-start | bytes 100
  2.5 8.6 %copy-start.6 = (s32[1,8]{1,0:T(1,128)S(1)}, s32[1,8]{1,0:T(1,128)}, u32[]{:S(2)}) copy-start(s32[1,8]{1,0:T(1,128)} %param.9) | copy-start | bytes 100
  2.5 22.9 %copy-start.2 = (f32[1,512,512]{2,1,0:T(8,128)S(1)}, f32[1,512,512]{2,1,0:T(8,128)}, u32[]{:S(2)}) copy-start(f32[1,512,512]{2,1,0:T(8,128)} %param.6) | copy-start | bytes 3145732
  3.6 21.8 %all-to-all-start = ((bf16[64,8,512]{2,0,1:T(8,128)(2,1)}), bf16[64,8,512]{2,0,1:T(8,128)(2,1)S(1)}, u32[]{:S(2)}, u32[]{:S(2)}) async-start(bf16[64,8,512]{2,0,1:T(8,128)(2,1)} %copy.24), calls=%async_computation | async-start | bytes 1048576 | tf_op jit(solution)/shard_map/all_to_all | solution.py:290
  27.5 18.1 %copy-start.1 = (f32[1,512,512]{2,1,0:T(8,128)S(1)}, f32[1,512,512]{2,1,0:T(8,128)}, u32[]{:S(2)}) copy-start(f32[1,512,512]{2,1,0:T(8,128)} %param.7) | copy-start | bytes 3145732
  27.5 8.2 %collective-permute-start.2 = (f32[128,640]{1,0:T(8,128)S(1)}, f32[128,640]{1,0:T(8,128)S(1)}, u32[]{:S(2)}, u32[]{:S(2)}) collective-permute-start(f32[128,640]{1,0:T(8,128)S(1)} %pad_maximum_fusion.1), channel_id=1, source_target_pairs={{0,2},{2,0},{1,3},{3,1},{4,6},{6,4},{5,7},{7,5},{8,10},{10,8},{9,1... | collective-permute-start | bytes 983048 | tf_op jit(solution)/shard_map/ppermute | solution.py:31
  28.4 9.5 %collective-permute-start = (f32[128,640]{1,0:T(8,128)S(1)}, f32[128,640]{1,0:T(8,128)S(1)}, u32[]{:S(2)}, u32[]{:S(2)}) collective-permute-start(f32[128,640]{1,0:T(8,128)S(1)} %pad_maximum_fusion), channel_id=1, source_target_pairs={{0,1},{1,0},{2,3},{3,2},{4,5},{5,4},{6,7},{7,6},{8,9},{9,8},{10,11... | collective-permute-start | bytes 983048 | tf_op jit(solution)/shard_map/ppermute | solution.py:31
  35.7 8.3 %collective-permute-start.3 = (f32[128,640]{1,0:T(8,128)S(1)}, f32[128,640]{1,0:T(8,128)S(1)}, u32[]{:S(2)}, u32[]{:S(2)}) collective-permute-start(f32[128,640]{1,0:T(8,128)S(1)} %fusion.6.b0), channel_id=1, source_target_pairs={{0,1},{1,0},{2,3},{3,2},{4,5},{5,4},{6,7},{7,6},{8,9},{9,8},{10,11... | collective-permute-start | bytes 983048 | tf_op jit(solution)/shard_map/ppermute | solution.py:31
  37.9 7.7 %collective-permute-start.1 = (f32[128,640]{1,0:T(8,128)S(1)}, f32[128,640]{1,0:T(8,128)S(1)}, u32[]{:S(2)}, u32[]{:S(2)}) collective-permute-start(f32[128,640]{1,0:T(8,128)S(1)} %fusion.7.a0), channel_id=1, source_target_pairs={{0,2},{2,0},{1,3},{3,1},{4,6},{6,4},{5,7},{7,5},{8,10},{10,8},{9,1... | collective-permute-start | bytes 983048 | tf_op jit(solution)/shard_map/ppermute | solution.py:31
  64.7 24.0 %collective-permute-start.4 = (bf16[512,512]{1,0:T(8,128)(2,1)S(1)}, bf16[512,512]{1,0:T(8,128)(2,1)S(1)}, u32[]{:S(2)}, u32[]{:S(2)}) collective-permute-start(bf16[512,512]{1,0:T(8,128)(2,1)S(1)} %get-tuple-element.16), channel_id=1, source_target_pairs={{0,4},{1,5},{2,6},{3,7},{4,0},{5,1},{6,2},{7,3},{8,12},{9,13},{10,... | collective-permute-start | bytes 1572872 | tf_op jit(solution)/shard_map/ppermute | solution.py:148
  67.1 23.6 %collective-permute-start.7 = (bf16[512,512]{1,0:T(8,128)(2,1)S(1)}, bf16[512,512]{1,0:T(8,128)(2,1)}, u32[]{:S(2)}, u32[]{:S(2)}) collective-permute-start(bf16[512,512]{1,0:T(8,128)(2,1)S(1)} %get-tuple-element.16), channel_id=1, source_target_pairs={{0,16},{8,24},{16,0},{24,8},{1,17},{9,25},{17,1},{25,9},{2,18},{10... | collective-permute-start | bytes 1572872 | tf_op jit(solution)/shard_map/ppermute | solution.py:148
  88.7 13.3 %collective-permute-start.5 = (bf16[512,512]{1,0:T(8,128)(2,1)S(1)}, bf16[512,512]{1,0:T(8,128)(2,1)}, u32[]{:S(2)}, u32[]{:S(2)}) collective-permute-start(bf16[512,512]{1,0:T(8,128)(2,1)S(1)} %collective-permute-done.4), channel_id=1, source_target_pairs={{0,16},{8,24},{16,0},{24,8},{1,17},{9,25},{17,1},{25,9},{2,18},{10... | collective-permute-start | bytes 1572872 | tf_op jit(solution)/shard_map/ppermute | solution.py:148
  90.2 19.7 %collective-permute-start.10 = (bf16[512,512]{1,0:T(8,128)(2,1)S(1)}, bf16[512,512]{1,0:T(8,128)(2,1)}, u32[]{:S(2)}, u32[]{:S(2)}) collective-permute-start(bf16[512,512]{1,0:T(8,128)(2,1)S(1)} %get-tuple-element.16), channel_id=1, source_target_pairs={{0,8},{8,0},{16,24},{24,16},{1,9},{9,1},{17,25},{25,17},{2,10},{10... | collective-permute-start | bytes 1572872 | tf_op jit(solution)/shard_map/ppermute | solution.py:148
  90.2 19.7 %collective-permute-start.9 = (bf16[512,512]{1,0:T(8,128)(2,1)S(1)}, bf16[512,512]{1,0:T(8,128)(2,1)}, u32[]{:S(2)}, u32[]{:S(2)}) collective-permute-start(bf16[512,512]{1,0:T(8,128)(2,1)S(1)} %collective-permute-done.4), channel_id=1, source_target_pairs={{0,8},{8,0},{16,24},{24,16},{1,9},{9,1},{17,25},{25,17},{2,10},{10... | collective-permute-start | bytes 1572872 | tf_op jit(solution)/shard_map/ppermute | solution.py:148
  90.7 19.2 %collective-permute-start.8 = (bf16[512,512]{1,0:T(8,128)(2,1)}, bf16[512,512]{1,0:T(8,128)(2,1)}, u32[]{:S(2)}, u32[]{:S(2)}) collective-permute-start(bf16[512,512]{1,0:T(8,128)(2,1)} %collective-permute-done.7), channel_id=1, source_target_pairs={{0,8},{8,0},{16,24},{24,16},{1,9},{9,1},{17,25},{25,17},{2,10},{10... | collective-permute-start | bytes 1572872 | tf_op jit(solution)/shard_map/ppermute | solution.py:148
  102.0 7.9 %collective-permute-start.6 = (bf16[512,512]{1,0:T(8,128)(2,1)}, bf16[512,512]{1,0:T(8,128)(2,1)}, u32[]{:S(2)}, u32[]{:S(2)}) collective-permute-start(bf16[512,512]{1,0:T(8,128)(2,1)} %collective-permute-done.5), channel_id=1, source_target_pairs={{0,8},{8,0},{16,24},{24,16},{1,9},{9,1},{17,25},{25,17},{2,10},{10... | collective-permute-start | bytes 1572872 | tf_op jit(solution)/shard_map/ppermute | solution.py:148
  112.2 14.4 %collective-permute-start.11 = (bf16[512,512]{1,0:T(8,128)(2,1)S(1)}, bf16[512,512]{1,0:T(8,128)(2,1)S(1)}, u32[]{:S(2)}, u32[]{:S(2)}) collective-permute-start(bf16[512,512]{1,0:T(8,128)(2,1)S(1)} %get-tuple-element.22), channel_id=1, source_target_pairs={{0,1},{1,0},{2,3},{3,2},{4,5},{5,4},{6,7},{7,6},{8,9},{9,8},{10,11... | collective-permute-start | bytes 1572872 | tf_op jit(solution)/shard_map/ppermute | solution.py:148
  113.5 14.8 %collective-permute-start.12 = (bf16[512,512]{1,0:T(8,128)(2,1)S(1)}, bf16[512,512]{1,0:T(8,128)(2,1)S(1)}, u32[]{:S(2)}, u32[]{:S(2)}) collective-permute-start(bf16[512,512]{1,0:T(8,128)(2,1)S(1)} %get-tuple-element.21), channel_id=1, source_target_pairs={{0,2},{1,3},{2,0},{3,1},{4,6},{5,7},{6,4},{7,5},{8,10},{9,11},{10,... | collective-permute-start | bytes 1572872 | tf_op jit(solution)/shard_map/ppermute | solution.py:148
  113.5 25.6 %collective-permute-start.13 = (bf16[512,512]{1,0:T(8,128)(2,1)S(1)}, bf16[512,512]{1,0:T(8,128)(2,1)}, u32[]{:S(2)}, u32[]{:S(2)}) collective-permute-start(bf16[512,512]{1,0:T(8,128)(2,1)S(1)} %get-tuple-element.20), channel_id=1, source_target_pairs={{0,3},{1,2},{2,1},{3,0},{4,7},{5,6},{6,5},{7,4},{8,11},{9,10},{10,... | collective-permute-start | bytes 1572872 | tf_op jit(solution)/shard_map/ppermute | solution.py:148
  126.6 1.7 %copy-start.3 = (bf16[512,512]{1,0:T(8,128)(2,1)}, bf16[512,512]{1,0:T(8,128)(2,1)S(1)}, u32[]{:S(2)}) copy-start(bf16[512,512]{1,0:T(8,128)(2,1)S(1)} %collective-permute-done.11.refs_1_) | copy-start | bytes 1572868
  128.3 0.8 copy-start.4
where the time goes:
time: 143 us; the launch traced here: 142 us
  waiting for transfers between devices  77.6 us (54%)
  Pallas kernels  22 us (15%)
  starting transfers between devices  20.9 us (15%)
  between operations  8.84 us (6%)
  other arithmetic  6.19 us (4%)
  local copies, waits for them, and re-layouts  3.88 us (3%)
  matrix products  2.62 us (2%)
    ppermute x10, waiting for transfers between devices, flipped(): lax.ppermute(block, axis, [(i, i ^ flip) for i in range(lax.axis_size(axi...  50.6 us
    pallas_call x1, Pallas kernels, newton(): pl.pallas_call(functools.partial(newton_kernel, iters, scale), out_shape=...  19.1 us
    ppermute x4, waiting for transfers between devices, from_partner(): return lax.ppermute(block, axis, route)  13.7 us
    all_to_all x1, waiting for transfers between devices, shards(): lax.all_to_all(ordered.reshape(row_block, dev_count, slab_cols), 'dev', s...  13.4 us
    ppermute x10, starting transfers between devices, flipped(): lax.ppermute(block, axis, [(i, i ^ flip) for i in range(lax.axis_size(axi...  9.42 us
    all_to_all x1, starting transfers between devices, shards(): lax.all_to_all(ordered.reshape(row_block, dev_count, slab_cols), 'dev', s...  7.31 us
    select_n x2, other arithmetic, choose(): jnp.where(odd, items[i + 1], items[i])  4.54 us
    ppermute x4, starting transfers between devices, from_partner(): return lax.ppermute(block, axis, route)  4.22 us
  transfers between devices with their start and end apart: 15, of which 9 were waited for; matrix products, arithmetic and copies ran while one was open for 3% of the time, Pallas kernels for 0%

commit v1 on v0

--- a/solution.py
+++ b/solution.py
@@ -8,8 +8,10 @@
 from jax.experimental.pallas import tpu as pltpu
 from jax.sharding import PartitionSpec as P
 
+
 ITERS = 5
 PACK = 4
+CHUNKS = 2
 
 
 momentum_decay = 0.95
@@ -74,7 +76,8 @@
     return total
 
 
-def newton_kernel(iters, scale, a0, a1, b0, b1, p_ref, w_ref, u_ref, n_ref, r_ref, gram, cur):
+def newton_kernel(iters, scale, a0, a1, b0, b1, p_ref, w_ref, u_ref, n_ref, r_ref, *rest):
+    pieces, (gram, cur) = rest[:-2], rest[-2:]
     rows = gram.shape[0]
     step = rows // PACK
     halves = [a0[...] + a1[...], b0[...] + b1[...]]
@@ -122,39 +125,37 @@
     u = apply(parts_of(mixed_of(a, parts_of(a, 2)), 2)) * scale
     w = w_ref[...]
     new = w - learn_rate * (u + weight_decay * w)
-    r_ref[...] = new.astype(r_ref.dtype)
+    rounded = new.astype(r_ref.dtype)
+    r_ref[...] = rounded
+    for i, piece in enumerate(pieces):
+        piece[...] = rounded[i * piece.shape[0] : (i + 1) * piece.shape[0]]
     u_ref[...] = u
     n_ref[...] = new
 
 
-def newton(halves, moved, nesterov, master, iters, scale):
+def newton(halves, moved, nesterov, master, iters, scale, chunks):
     rows, cols = nesterov.shape
     vmem = pl.BlockSpec(memory_space=pltpu.VMEM)
     f32 = jax.ShapeDtypeStruct((rows, cols), jnp.float32)
+    pieces = [jax.ShapeDtypeStruct((rows // chunks, cols), jnp.bfloat16) for _ in range(chunks)]
     return pl.pallas_call(
         functools.partial(newton_kernel, iters, scale),
-        out_shape=[f32, f32, jax.ShapeDtypeStruct((rows, cols), jnp.bfloat16)],
+        out_shape=[f32, f32, jax.ShapeDtypeStruct((rows, cols), jnp.bfloat16)] + pieces,
         in_specs=[vmem] * 6,
-        out_specs=[vmem] * 3,
-        scratch_shapes=[pltpu.VMEM((rows, rows), jnp.float32), pltpu.VMEM((rows, cols), jnp.float32)],
+        out_specs=[vmem] * (3 + chunks),
+        scratch_shapes=[
+            pltpu.VMEM((rows, rows), jnp.float32),
+            pltpu.VMEM((rows, cols), jnp.float32),
+        ],
         cost_estimate=pl.CostEstimate(
             flops=2 * 60 * rows * rows * cols, bytes_accessed=24 * rows * cols, transcendentals=0
         ),
-        compiler_params=pltpu.CompilerParams(vmem_limit_bytes=40 << 20),
+        compiler_params=pltpu.CompilerParams(vmem_limit_bytes=24 << 20),
     )(halves[0], moved[0], halves[1], moved[1], nesterov, master)
 
 
 def flipped(block, axis, flip):
     return lax.ppermute(block, axis, [(i, i ^ flip) for i in range(lax.axis_size(axis))])
-
-
-def choose(items, index):
-    bit = 0
-    while len(items) > 1:
-        odd = (index >> bit) & 1 == 1
-        items = [jnp.where(odd, items[i + 1], items[i]) for i in range(0, len(items), 2)]
-        bit += 1
-    return items[0]
 
 
 def owner_of(owned_matrix, quads):
@@ -173,54 +174,107 @@
     targets = rollout_matrix[0]
     owner = jnp.sum(jnp.where(targets[:, None] == mats[None, :], inverse[None, :], 0), axis=1)
     slot = ((targets // quads) ^ group) * quads + (owner ^ (place // share_count))
-    return [
-        lax.dynamic_index_in_dim(slot, place ^ turn, 0, keepdims=False)
-        for turn in range(share_count)
+    turns = place ^ jnp.arange(share_count, dtype=jnp.int32)
+    places = jnp.arange(slot.shape[0], dtype=jnp.int32)
+    return jnp.sum(jnp.where(turns[:, None] == places[None, :], slot[None, :], 0), axis=1)
+
+
+def pick_kernel(chunk, slots, *refs):
+    turns = slots.shape[0]
+    slabs, outs, done = refs[: -turns - 1], refs[-turns - 1 : -1], refs[-1]
+    rows = outs[0].shape[0]
+    views = [
+        slab if slab.shape[0] == rows else slab.at[pl.ds(chunk * rows, rows)] for slab in slabs
     ]
-
-
-def lay_kernel(share_count, *refs):
+    for turn in range(turns):
+        slot = slots[turn]
+        for index, view in enumerate(views):
+
+            @pl.when(slot == index)
+            def _(view=view, turn=turn):
+                pltpu.make_async_copy(view, outs[turn], done.at[turn]).start()
+
+    for turn in range(turns):
+        pltpu.make_async_copy(views[0], outs[turn], done.at[turn]).wait()
+
+
+def pick(slots, slabs, chunk, rows):
+    turns = slots.shape[0]
+    cols = slabs[0].shape[1]
+    block = jax.ShapeDtypeStruct((rows, cols), slabs[0].dtype)
+    return pl.pallas_call(
+        functools.partial(pick_kernel, chunk),
+        out_shape=[block] * turns,
+        in_specs=[pl.BlockSpec(memory_space=pltpu.SMEM)]
+        + [pl.BlockSpec(memory_space=pl.ANY)] * len(slabs),
+        out_specs=[pl.BlockSpec(memory_space=pltpu.VMEM)] * turns,
+        scratch_shapes=[pltpu.SemaphoreType.DMA((turns,))],
+        cost_estimate=pl.CostEstimate(
+            flops=0, bytes_accessed=4 * turns * rows * cols, transcendentals=0
+        ),
+        compiler_params=pltpu.CompilerParams(vmem_limit_bytes=8 << 20),
+    )(slots, *slabs)
+
+
+def lay_kernel(share_count, chunk, *refs):
     mine = lax.axis_index("dev") % share_count
     blocks, out, done = refs[:share_count], refs[-2], refs[-1]
-    cols = blocks[0].shape[1]
+    rows, cols = blocks[0].shape
     moves = []
     for turn, block in enumerate(blocks):
         start = pl.multiple_of((mine ^ turn) * cols, cols)
-        moves.append(
-            pltpu.make_async_copy(block, out.at[:, pl.ds(start, cols)], done.at[turn])
-        )
+        place = out.at[pl.ds(chunk * rows, rows), pl.ds(start, cols)]
+        moves.append(pltpu.make_async_copy(block, place, done.at[turn]))
     for move in moves:
         move.start()
     for move in moves:
         move.wait()
 
 
-def lay(blocks):
+def lay(blocks, chunk, chunks, before):
     share_count = len(blocks)
     rows, cols = blocks[0].shape
+    extra = [] if before is None else [before]
     return pl.pallas_call(
-        functools.partial(lay_kernel, share_count),
-        out_shape=jax.ShapeDtypeStruct((rows, cols * share_count), blocks[0].dtype),
-        in_specs=[pl.BlockSpec(memory_space=pltpu.VMEM)] * share_count,
+        functools.partial(lay_kernel, share_count, chunk),
+        out_shape=jax.ShapeDtypeStruct((rows * chunks, cols * share_count), blocks[0].dtype),
+        in_specs=[pl.BlockSpec(memory_space=pltpu.VMEM)] * share_count
+        + [pl.BlockSpec(memory_space=pltpu.HBM)] * len(extra),
         out_specs=pl.BlockSpec(memory_space=pltpu.HBM),
         scratch_shapes=[pltpu.SemaphoreType.DMA((share_count,))],
-    )(*blocks)
-
-
-def sync_two_halves(rounded, slots, share_count):
+        input_output_aliases={share_count: 0} if extra else {},
+        cost_estimate=pl.CostEstimate(
+            flops=0, bytes_accessed=4 * share_count * rows * cols, transcendentals=0
+        ),
+        compiler_params=pltpu.CompilerParams(vmem_limit_bytes=8 << 20),
+    )(*blocks, *extra)
+
+
+def spread(block):
     group_count = lax.axis_size("grp")
-    tables = []
-    for start in (rounded, flipped(rounded, "dev", share_count)):
-        table = {0: start}
-        for bit in range(group_count.bit_length() - 2, -1, -1):
-            for key in list(table):
-                table[key | 1 << bit] = flipped(table[key], "grp", 1 << bit)
-        tables.append(table)
-    slabs = [table[key] for key in range(group_count) for table in tables]
-    picked = [choose(slabs, slot) for slot in slots]
-    return lay(
-        [picked[0]] + [flipped(picked[turn], "dev", turn) for turn in range(1, share_count)]
-    )
+    table = {0: block}
+    for bit in range(group_count.bit_length() - 2, -1, -1):
+        for key in list(table):
+            table[key | 1 << bit] = flipped(table[key], "grp", 1 << bit)
+    return [table[key] for key in range(group_count)]
+
+
+def sync_two_halves(rounded, pieces, slots, share_count):
+    chunks = len(pieces)
+    rows = pieces[0].shape[0]
+    others = []
+    for piece in pieces:
+        others.append(flipped(piece, "dev", share_count))
+    mine = spread(rounded)
+    result = None
+    for chunk in range(chunks):
+        theirs = spread(others[chunk])
+        slabs = [slab for pair in zip(mine, theirs) for slab in pair]
+        blocks = list(pick(slots, slabs, chunk, rows))
+        for turn in range(1, share_count):
+            blocks[turn] = flipped(blocks[turn], "dev", turn)
+        result = lay(blocks, chunk, chunks, result)
+    return result
 
 
 def sync_any(rounded, rollout_matrix, owned_matrix, row_block, columns):
@@ -265,7 +319,7 @@
     return landed.reshape(slot_count, row_count, columns)
 
 
-def shards(gradient, momentum, master_weight, owned_matrix, rollout_matrix):
+def step(gradient, momentum, master_weight, owned_matrix, rollout_matrix):
     group = lax.axis_index("grp")
     dev_count = lax.axis_size("dev")
     group_count = lax.axis_size("grp")
@@ -302,11 +356,11 @@
         nesterov, slots = lax.optimization_barrier((nesterov, slots))
     halves, moved = gram_sum(nesterov, share_count)
     scale_factor = 0.2 * math.sqrt(max(row_count, columns))
-    update, new_weight, rounded = newton(
-        halves, moved, nesterov, master_weight[0], ITERS, scale_factor
+    update, new_weight, rounded, *pieces = newton(
+        halves, moved, nesterov, master_weight[0], ITERS, scale_factor, CHUNKS if two_halves else 0
     )
     if two_halves:
-        rollout = sync_two_halves(rounded, slots, share_count)[None]
+        rollout = sync_two_halves(rounded, pieces, slots, share_count)[None]
     else:
         rollout = sync_any(rounded, rollout_matrix, owned_matrix, row_block, columns)
     return (new_moment[None], update[None], new_weight[None], rollout)
@@ -321,7 +375,7 @@
         P("grp", None),
     )
     return jax.shard_map(
-        shards,
+        step,
         mesh=mesh,
         in_specs=placed,
         out_specs=(

time: 143 us -> 130 us (0.909)
  between operations: 8.84 us -> 0.86 us
  other arithmetic: 6.19 us -> 1.85 us
  local copies, waits for them, and re-layouts: 3.88 us -> 2.38 us
    select_n x2 -> x0, other arithmetic: 4.54 us -> none  [choose(): jnp.where(odd, items[i + 1], items[i])]
    ppermute x10 -> x17, starting transfers between devices: 9.42 us -> 12.7 us  [flipped(): lax.ppermute(block, axis, [(i, i ^ flip) for i in range(lax.axis_size(axi...]
    ppermute x10 -> x17, waiting for transfers between devices: 50.6 us -> 47.3 us  [flipped(): lax.ppermute(block, axis, [(i, i ^ flip) for i in range(lax.axis_size(axi...]
    ppermute x4, waiting for transfers between devices: 13.7 us -> 16.3 us  [from_partner(): return lax.ppermute(block, axis, route)]
    ppermute x4, starting transfers between devices: 4.22 us -> 1.74 us  [from_partner(): return lax.ppermute(block, axis, route)]
    pallas_call x1 -> x4, Pallas kernels: 2.86 us -> 3.67 us  [the longest x2 2.01 us: lay(): pl.pallas_call(functools.partial(lay_kernel, share_count, chunk), out_sha...]
  transfers between devices with their start and end apart: 15 -> 22, of which waited for: 9 -> 12; matrix products, arithmetic and copies ran while one was open for 3% -> 1% of each run, Pallas kernels for 0% -> 2%
where the time goes in v1:
time: 130 us
  waiting for transfers between devices  77.5 us (60%)
  Pallas kernels  22.6 us (17%)
  starting transfers between devices  21.7 us (17%)
  matrix products  2.62 us (2%)
  local copies, waits for them, and re-layouts  2.38 us (2%)
  other arithmetic  1.85 us (1%)
    ppermute x17, waiting for transfers between devices, flipped(): lax.ppermute(block, axis, [(i, i ^ flip) for i in range(lax.axis_size(axi...  47.3 us
    pallas_call x1, Pallas kernels, newton(): pl.pallas_call(functools.partial(newton_kernel, iters, scale), out_shape=...  19 us
    ppermute x4, waiting for transfers between devices, from_partner(): return lax.ppermute(block, axis, route)  16.3 us
    all_to_all x1, waiting for transfers between devices, step(): lax.all_to_all(ordered.reshape(row_block, dev_count, slab_cols), 'dev', s...  13.9 us
    ppermute x17, starting transfers between devices, flipped(): lax.ppermute(block, axis, [(i, i ^ flip) for i in range(lax.axis_size(axi...  12.7 us
    all_to_all x1, starting transfers between devices, step(): lax.all_to_all(ordered.reshape(row_block, dev_count, slab_cols), 'dev', s...  7.31 us
  transfers between devices with their start and end apart: 22, of which 12 were waited for; matrix products, arithmetic and copies ran while one was open for 1% of the time, Pallas kernels for 2%

profile of v1, /device:TPU:0, one launch (start us, length us, event | category | flops | bytes accessed | tf_op | source)
XLA Modules:
  0.0 129.6 jit_solution(6275069063992731252)
XLA Ops:
  0.7 0.9 dynamic-slice_reduce_fusion
  1.7 0.8 fusion
  2.6 0.9 copy.25
  3.6 7.3 %all-to-all-start = ((bf16[64,8,512]{2,0,1:T(8,128)(2,1)}), bf16[64,8,512]{2,0,1:T(8,128)(2,1)S(1)}, u32[]{:S(2)}, u32[]{:S(2)}) async-start(bf16[64,8,512]{2,0,1:T(8,128)(2,1)} %copy.25), calls=%async_computation | async-start | bytes 1048576 | tf_op jit(solution)/shard_map/all_to_all | solution.py:344
  11.5 13.9 %all-to-all-done = bf16[64,8,512]{2,0,1:T(8,128)(2,1)S(1)} async-done(((bf16[64,8,512]{2,0,1:T(8,128)(2,1)}), bf16[64,8,512]{2,0,1:T(8,128)(2,1)S(1)}, u32[]{:S(2)}, u32[]{:S(2)}) %all-to-all-start) | async-done | bytes 524320 | tf_op jit(solution)/shard_map/all_to_all | solution.py:344
  25.6 1.9 %fusion.9 = f32[512,512]{1,0:T(8,128)S(1)} fusion(f32[512,512]{1,0:T(8,128)S(1)} %bitcast_add_fusion.1.p_ref), kind=kOutput, calls=%fused_computation.28 | convolution fusion | flops 1610612736 | bytes 2097152 | tf_op jit(solution)/shard_map/dot_general | solution.py:37
  27.5 1.5 %collective-permute-start = (f32[128,640]{1,0:T(8,128)S(1)}, f32[128,640]{1,0:T(8,128)S(1)}, u32[]{:S(2)}, u32[]{:S(2)}) collective-permute-start(f32[128,640]{1,0:T(8,128)S(1)} %pad_maximum_fusion), channel_id=1, source_target_pairs={{0,1},{1,0},{2,3},{3,2},{4,5},{5,4},{6,7},{7,6},{8,9},{9,8},{10,11... | collective-permute-start | bytes 983048 | tf_op jit(solution)/shard_map/ppermute | solution.py:33
  29.2 6.8 %collective-permute-done = f32[128,640]{1,0:T(8,128)S(1)} collective-permute-done((f32[128,640]{1,0:T(8,128)S(1)}, f32[128,640]{1,0:T(8,128)S(1)}, u32[]{:S(2)}, u32[]{:S(2)}) %collective-permute-start) | collective-permute-done | bytes 327712 | tf_op jit(solution)/shard_map/ppermute | solution.py:33
  36.2 2.4 %collective-permute-done.2 = f32[128,640]{1,0:T(8,128)S(1)} collective-permute-done((f32[128,640]{1,0:T(8,128)S(1)}, f32[128,640]{1,0:T(8,128)S(1)}, u32[]{:S(2)}, u32[]{:S(2)}) %collective-permute-start.2) | collective-permute-done | bytes 327712 | tf_op jit(solution)/shard_map/ppermute | solution.py:33
  38.7 6.0 %collective-permute-done.1.a1 = f32[128,640]{1,0:T(8,128)S(1)} collective-permute-done((f32[128,640]{1,0:T(8,128)S(1)}, f32[128,640]{1,0:T(8,128)S(1)}, u32[]{:S(2)}, u32[]{:S(2)}) %collective-permute-start.1) | collective-permute-done | bytes 327712 | tf_op jit(solution)/shard_map/ppermute | solution.py:33
  44.7 1.1 collective-permute-done.3.b1
  45.7 19.0 %shard_map.84 = (f32[512,512]{1,0:T(8,128)}, f32[512,512]{1,0:T(8,128)}, bf16[512,512]{1,0:T(8,128)(2,1)S(1)}, bf16[256,512]{1,0:T(8,128)(2,1)S(1)}, bf16[256,512]{1,0:T(8,128)(2,1)S(1)}) custom-call(f32[128,640]{1,0:T(8,128)S(1)} %fusion.8.a0, f32[128,640]{1,0:T(8,128)S(1)} %collective-permute-done.1.a1, f32[128,640]{1,0:T(8,128)S(1)} %fusion.7.b0, ...), custom_call_target="tpu_custom_call" | custom-call | flops 16106127360 | bytes 6291456 | tf_op jit(solution)/shard_map/pallas_call | solution.py:141
  64.7 1.5 %collective-permute-start.7 = (bf16[512,512]{1,0:T(8,128)(2,1)S(1)}, bf16[512,512]{1,0:T(8,128)(2,1)S(1)}, u32[]{:S(2)}, u32[]{:S(2)}) collective-permute-start(bf16[512,512]{1,0:T(8,128)(2,1)S(1)} %get-tuple-element.23.refs_0_), channel_id=1, source_target_pairs={{0,16},{8,24},{16,0},{24,8},{1,17},{9,25},{17,1},{25,9},{2,18},{10... | collective-permute-start | bytes 1572872 | tf_op jit(solution)/shard_map/ppermute | solution.py:158
  66.2 2.0 %collective-permute-start.14 = (bf16[256,512]{1,0:T(8,128)(2,1)S(1)}, bf16[256,512]{1,0:T(8,128)(2,1)S(1)}, u32[]{:S(2)}, u32[]{:S(2)}) collective-permute-start(bf16[256,512]{1,0:T(8,128)(2,1)S(1)} %get-tuple-element.29), channel_id=1, source_target_pairs={{0,4},{1,5},{2,6},{3,7},{4,0},{5,1},{6,2},{7,3},{8,12},{9,13},{10,... | collective-permute-start | bytes 786440 | tf_op jit(solution)/shard_map/ppermute | solution.py:158
  68.2 0.9 collective-permute-start.4
  69.1 15.5 %collective-permute-done.14.refs_1_ = bf16[256,512]{1,0:T(8,128)(2,1)S(1)} collective-permute-done((bf16[256,512]{1,0:T(8,128)(2,1)S(1)}, bf16[256,512]{1,0:T(8,128)(2,1)S(1)}, u32[]{:S(2)}, u32[]{:S(2)}) %collective-permute-start.14) | collective-permute-done | bytes 262176 | tf_op jit(solution)/shard_map/ppermute | solution.py:158
  84.6 0.5 collective-permute-start.16
  85.1 4.1 %collective-permute-done.4.refs_1_ = bf16[256,512]{1,0:T(8,128)(2,1)S(1)} collective-permute-done((bf16[256,512]{1,0:T(8,128)(2,1)S(1)}, bf16[256,512]{1,0:T(8,128)(2,1)S(1)}, u32[]{:S(2)}, u32[]{:S(2)}) %collective-permute-start.4) | collective-permute-done | bytes 262176 | tf_op jit(solution)/shard_map/ppermute | solution.py:158
  89.2 0.5 collective-permute-start.8
  89.8 1.2 collective-permute-done.16.refs_5_
  91.0 5.6 %collective-permute-done.8.refs_5_ = bf16[256,512]{1,0:T(8,128)(2,1)S(1)} collective-permute-done((bf16[256,512]{1,0:T(8,128)(2,1)S(1)}, bf16[256,512]{1,0:T(8,128)(2,1)S(1)}, u32[]{:S(2)}, u32[]{:S(2)}) %collective-permute-start.8) | collective-permute-done | bytes 262176 | tf_op jit(solution)/shard_map/ppermute | solution.py:158
  97.1 0.8 shard_map.86
  97.9 2.6 %collective-permute-start.18 = (bf16[256,512]{1,0:T(8,128)(2,1)S(1)}, bf16[256,512]{1,0:T(8,128)(2,1)S(1)}, u32[]{:S(2)}, u32[]{:S(2)}) collective-permute-start(bf16[256,512]{1,0:T(8,128)(2,1)S(1)} %get-tuple-element.31), channel_id=1, source_target_pairs={{0,1},{1,0},{2,3},{3,2},{4,5},{5,4},{6,7},{7,6},{8,9},{9,8},{10,11... | collective-permute-start | bytes 786440 | tf_op jit(solution)/shard_map/ppermute | solution.py:158
  100.6 0.8 shard_map.85
  102.0 0.6 collective-permute-start.12
  102.5 2.5 %collective-permute-start.13 = (bf16[256,512]{1,0:T(8,128)(2,1)S(1)}, bf16[256,512]{1,0:T(8,128)(2,1)S(1)}, u32[]{:S(2)}, u32[]{:S(2)}) collective-permute-start(bf16[256,512]{1,0:T(8,128)(2,1)S(1)} %get-tuple-element.28), channel_id=1, source_target_pairs={{0,3},{1,2},{2,1},{3,0},{4,7},{5,6},{6,5},{7,4},{8,11},{9,10},{10,... | collective-permute-start | bytes 786440 | tf_op jit(solution)/shard_map/ppermute | solution.py:158
  105.0 2.8 %collective-permute-done.18.refs_1_ = bf16[256,512]{1,0:T(8,128)(2,1)S(1)} collective-permute-done((bf16[256,512]{1,0:T(8,128)(2,1)S(1)}, bf16[256,512]{1,0:T(8,128)(2,1)S(1)}, u32[]{:S(2)}, u32[]{:S(2)}) %collective-permute-start.18) | collective-permute-done | bytes 262176 | tf_op jit(solution)/shard_map/ppermute | solution.py:158
  108.2 1.1 bitcast_add_fusion
  109.3 13.1 %collective-permute-done.19.refs_2_ = bf16[256,512]{1,0:T(8,128)(2,1)S(1)} collective-permute-done((bf16[256,512]{1,0:T(8,128)(2,1)S(1)}, bf16[256,512]{1,0:T(8,128)(2,1)S(1)}, u32[]{:S(2)}, u32[]{:S(2)}) %collective-permute-start.19) | collective-permute-done | bytes 262176 | tf_op jit(solution)/shard_map/ppermute | solution.py:158
  122.4 5.1 %collective-permute-done.20.refs_3_ = bf16[256,512]{1,0:T(8,128)(2,1)S(1)} collective-permute-done((bf16[256,512]{1,0:T(8,128)(2,1)S(1)}, bf16[256,512]{1,0:T(8,128)(2,1)S(1)}, u32[]{:S(2)}, u32[]{:S(2)}) %collective-permute-start.20) | collective-permute-done | bytes 262176 | tf_op jit(solution)/shard_map/ppermute | solution.py:158
  127.5 1.0 shard_map.87.refs_4_
  128.6 1.0 shard_map.88
  (49 shorter events, 3.0 us)
Async XLA Ops:
  0.6 1.1 copy-start
  2.5 8.4 %copy-start.3 = (s32[4,2]{0,1:T(2,128)S(1)}, s32[4,2]{0,1:T(2,128)}, u32[]{:S(2)}) copy-start(s32[4,2]{0,1:T(2,128)} %param.8) | copy-start | bytes 100
  2.5 8.6 %copy-start.4 = (s32[1,8]{1,0:T(1,128)S(1)}, s32[1,8]{1,0:T(1,128)}, u32[]{:S(2)}) copy-start(s32[1,8]{1,0:T(1,128)} %param.9) | copy-start | bytes 100
  2.5 22.9 %copy-start.2 = (f32[1,512,512]{2,1,0:T(8,128)S(1)}, f32[1,512,512]{2,1,0:T(8,128)}, u32[]{:S(2)}) copy-start(f32[1,512,512]{2,1,0:T(8,128)} %param.6) | copy-start | bytes 3145732
  3.6 21.8 %all-to-all-start = ((bf16[64,8,512]{2,0,1:T(8,128)(2,1)}), bf16[64,8,512]{2,0,1:T(8,128)(2,1)S(1)}, u32[]{:S(2)}, u32[]{:S(2)}) async-start(bf16[64,8,512]{2,0,1:T(8,128)(2,1)} %copy.25), calls=%async_computation | async-start | bytes 1048576 | tf_op jit(solution)/shard_map/all_to_all | solution.py:344
  27.5 18.2 %copy-start.1 = (f32[1,512,512]{2,1,0:T(8,128)S(1)}, f32[1,512,512]{2,1,0:T(8,128)}, u32[]{:S(2)}) copy-start(f32[1,512,512]{2,1,0:T(8,128)} %param.7) | copy-start | bytes 3145732
  27.5 8.5 %collective-permute-start = (f32[128,640]{1,0:T(8,128)S(1)}, f32[128,640]{1,0:T(8,128)S(1)}, u32[]{:S(2)}, u32[]{:S(2)}) collective-permute-start(f32[128,640]{1,0:T(8,128)S(1)} %pad_maximum_fusion), channel_id=1, source_target_pairs={{0,1},{1,0},{2,3},{3,2},{4,5},{5,4},{6,7},{7,6},{8,9},{9,8},{10,11... | collective-permute-start | bytes 983048 | tf_op jit(solution)/shard_map/ppermute | solution.py:33
  29.1 9.4 %collective-permute-start.2 = (f32[128,640]{1,0:T(8,128)S(1)}, f32[128,640]{1,0:T(8,128)S(1)}, u32[]{:S(2)}, u32[]{:S(2)}) collective-permute-start(f32[128,640]{1,0:T(8,128)S(1)} %pad_maximum_fusion.1), channel_id=1, source_target_pairs={{0,2},{2,0},{1,3},{3,1},{4,6},{6,4},{5,7},{7,5},{8,10},{10,8},{9,1... | collective-permute-start | bytes 983048 | tf_op jit(solution)/shard_map/ppermute | solution.py:33
  36.1 8.6 %collective-permute-start.1 = (f32[128,640]{1,0:T(8,128)S(1)}, f32[128,640]{1,0:T(8,128)S(1)}, u32[]{:S(2)}, u32[]{:S(2)}) collective-permute-start(f32[128,640]{1,0:T(8,128)S(1)} %fusion.8.a0), channel_id=1, source_target_pairs={{0,2},{2,0},{1,3},{3,1},{4,6},{6,4},{5,7},{7,5},{8,10},{10,8},{9,1... | collective-permute-start | bytes 983048 | tf_op jit(solution)/shard_map/ppermute | solution.py:33
  38.6 7.1 %collective-permute-start.3 = (f32[128,640]{1,0:T(8,128)S(1)}, f32[128,640]{1,0:T(8,128)S(1)}, u32[]{:S(2)}, u32[]{:S(2)}) collective-permute-start(f32[128,640]{1,0:T(8,128)S(1)} %fusion.7.b0), channel_id=1, source_target_pairs={{0,1},{1,0},{2,3},{3,2},{4,5},{5,4},{6,7},{7,6},{8,9},{9,8},{10,11... | collective-permute-start | bytes 983048 | tf_op jit(solution)/shard_map/ppermute | solution.py:33
  64.7 20.5 %collective-permute-start.7 = (bf16[512,512]{1,0:T(8,128)(2,1)S(1)}, bf16[512,512]{1,0:T(8,128)(2,1)S(1)}, u32[]{:S(2)}, u32[]{:S(2)}) collective-permute-start(bf16[512,512]{1,0:T(8,128)(2,1)S(1)} %get-tuple-element.23.refs_0_), channel_id=1, source_target_pairs={{0,16},{8,24},{16,0},{24,8},{1,17},{9,25},{17,1},{25,9},{2,18},{10... | collective-permute-start | bytes 1572872 | tf_op jit(solution)/shard_map/ppermute | solution.py:158
  66.2 18.4 %collective-permute-start.14 = (bf16[256,512]{1,0:T(8,128)(2,1)S(1)}, bf16[256,512]{1,0:T(8,128)(2,1)S(1)}, u32[]{:S(2)}, u32[]{:S(2)}) collective-permute-start(bf16[256,512]{1,0:T(8,128)(2,1)S(1)} %get-tuple-element.29), channel_id=1, source_target_pairs={{0,4},{1,5},{2,6},{3,7},{4,0},{5,1},{6,2},{7,3},{8,12},{9,13},{10,... | collective-permute-start | bytes 786440 | tf_op jit(solution)/shard_map/ppermute | solution.py:158
  68.2 21.1 %collective-permute-start.4 = (bf16[256,512]{1,0:T(8,128)(2,1)S(1)}, bf16[256,512]{1,0:T(8,128)(2,1)S(1)}, u32[]{:S(2)}, u32[]{:S(2)}) collective-permute-start(bf16[256,512]{1,0:T(8,128)(2,1)S(1)} %get-tuple-element.24), channel_id=1, source_target_pairs={{0,4},{1,5},{2,6},{3,7},{4,0},{5,1},{6,2},{7,3},{8,12},{9,13},{10,... | collective-permute-start | bytes 786440 | tf_op jit(solution)/shard_map/ppermute | solution.py:158
  69.1 28.0 %collective-permute-start.5 = (bf16[512,512]{1,0:T(8,128)(2,1)S(1)}, bf16[512,512]{1,0:T(8,128)(2,1)S(1)}, u32[]{:S(2)}, u32[]{:S(2)}) collective-permute-start(bf16[512,512]{1,0:T(8,128)(2,1)S(1)} %get-tuple-element.23.refs_0_), channel_id=1, source_target_pairs={{0,8},{8,0},{16,24},{24,16},{1,9},{9,1},{17,25},{25,17},{2,10},{10... | collective-permute-start | bytes 1572872 | tf_op jit(solution)/shard_map/ppermute | solution.py:158
  84.6 6.4 %collective-permute-start.16 = (bf16[256,512]{1,0:T(8,128)(2,1)S(1)}, bf16[256,512]{1,0:T(8,128)(2,1)S(1)}, u32[]{:S(2)}, u32[]{:S(2)}) collective-permute-start(bf16[256,512]{1,0:T(8,128)(2,1)S(1)} %collective-permute-done.14.refs_1_), channel_id=1, source_target_pairs={{0,16},{8,24},{16,0},{24,8},{1,17},{9,25},{17,1},{25,9},{2,18},{10... | collective-permute-start | bytes 786440 | tf_op jit(solution)/shard_map/ppermute | solution.py:158
  85.1 12.0 %collective-permute-start.9 = (bf16[512,512]{1,0:T(8,128)(2,1)S(1)}, bf16[512,512]{1,0:T(8,128)(2,1)S(1)}, u32[]{:S(2)}, u32[]{:S(2)}) collective-permute-start(bf16[512,512]{1,0:T(8,128)(2,1)S(1)} %collective-permute-done.7.refs_4_), channel_id=1, source_target_pairs={{0,8},{8,0},{16,24},{24,16},{1,9},{9,1},{17,25},{25,17},{2,10},{10... | collective-permute-start | bytes 1572872 | tf_op jit(solution)/shard_map/ppermute | solution.py:158
  89.2 7.3 %collective-permute-start.8 = (bf16[256,512]{1,0:T(8,128)(2,1)S(1)}, bf16[256,512]{1,0:T(8,128)(2,1)S(1)}, u32[]{:S(2)}, u32[]{:S(2)}) collective-permute-start(bf16[256,512]{1,0:T(8,128)(2,1)S(1)} %collective-permute-done.4.refs_1_), channel_id=1, source_target_pairs={{0,16},{8,24},{16,0},{24,8},{1,17},{9,25},{17,1},{25,9},{2,18},{10... | collective-permute-start | bytes 786440 | tf_op jit(solution)/shard_map/ppermute | solution.py:158
  89.8 6.8 %collective-permute-start.15 = (bf16[256,512]{1,0:T(8,128)(2,1)S(1)}, bf16[256,512]{1,0:T(8,128)(2,1)S(1)}, u32[]{:S(2)}, u32[]{:S(2)}) collective-permute-start(bf16[256,512]{1,0:T(8,128)(2,1)S(1)} %collective-permute-done.14.refs_1_), channel_id=1, source_target_pairs={{0,8},{8,0},{16,24},{24,16},{1,9},{9,1},{17,25},{25,17},{2,10},{10... | collective-permute-start | bytes 786440 | tf_op jit(solution)/shard_map/ppermute | solution.py:158
  91.0 6.1 %collective-permute-start.17 = (bf16[256,512]{1,0:T(8,128)(2,1)S(1)}, bf16[256,512]{1,0:T(8,128)(2,1)S(1)}, u32[]{:S(2)}, u32[]{:S(2)}) collective-permute-start(bf16[256,512]{1,0:T(8,128)(2,1)S(1)} %collective-permute-done.16.refs_5_), channel_id=1, source_target_pairs={{0,8},{8,0},{16,24},{24,16},{1,9},{9,1},{17,25},{25,17},{2,10},{10... | collective-permute-start | bytes 786440 | tf_op jit(solution)/shard_map/ppermute | solution.py:158
  96.6 4.0 %collective-permute-start.6 = (bf16[256,512]{1,0:T(8,128)(2,1)S(1)}, bf16[256,512]{1,0:T(8,128)(2,1)S(1)}, u32[]{:S(2)}, u32[]{:S(2)}) collective-permute-start(bf16[256,512]{1,0:T(8,128)(2,1)S(1)} %collective-permute-done.4.refs_1_), channel_id=1, source_target_pairs={{0,8},{8,0},{16,24},{24,16},{1,9},{9,1},{17,25},{25,17},{2,10},{10... | collective-permute-start | bytes 786440 | tf_op jit(solution)/shard_map/ppermute | solution.py:158
  96.6 4.0 %collective-permute-start.10 = (bf16[256,512]{1,0:T(8,128)(2,1)S(1)}, bf16[256,512]{1,0:T(8,128)(2,1)S(1)}, u32[]{:S(2)}, u32[]{:S(2)}) collective-permute-start(bf16[256,512]{1,0:T(8,128)(2,1)S(1)} %collective-permute-done.8.refs_5_), channel_id=1, source_target_pairs={{0,8},{8,0},{16,24},{24,16},{1,9},{9,1},{17,25},{25,17},{2,10},{10... | collective-permute-start | bytes 786440 | tf_op jit(solution)/shard_map/ppermute | solution.py:158
  97.9 9.8 %collective-permute-start.18 = (bf16[256,512]{1,0:T(8,128)(2,1)S(1)}, bf16[256,512]{1,0:T(8,128)(2,1)S(1)}, u32[]{:S(2)}, u32[]{:S(2)}) collective-permute-start(bf16[256,512]{1,0:T(8,128)(2,1)S(1)} %get-tuple-element.31), channel_id=1, source_target_pairs={{0,1},{1,0},{2,3},{3,2},{4,5},{5,4},{6,7},{7,6},{8,9},{9,8},{10,11... | collective-permute-start | bytes 786440 | tf_op jit(solution)/shard_map/ppermute | solution.py:158
  101.4 27.1 %collective-permute-start.11 = (bf16[256,512]{1,0:T(8,128)(2,1)S(1)}, bf16[256,512]{1,0:T(8,128)(2,1)S(1)}, u32[]{:S(2)}, u32[]{:S(2)}) collective-permute-start(bf16[256,512]{1,0:T(8,128)(2,1)S(1)} %get-tuple-element.26), channel_id=1, source_target_pairs={{0,1},{1,0},{2,3},{3,2},{4,5},{5,4},{6,7},{7,6},{8,9},{9,8},{10,11... | collective-permute-start | bytes 786440 | tf_op jit(solution)/shard_map/ppermute | solution.py:158
  102.0 26.6 %collective-permute-start.12 = (bf16[256,512]{1,0:T(8,128)(2,1)S(1)}, bf16[256,512]{1,0:T(8,128)(2,1)S(1)}, u32[]{:S(2)}, u32[]{:S(2)}) collective-permute-start(bf16[256,512]{1,0:T(8,128)(2,1)S(1)} %get-tuple-element.27), channel_id=1, source_target_pairs={{0,2},{1,3},{2,0},{3,1},{4,6},{5,7},{6,4},{7,5},{8,10},{9,11},{10,... | collective-permute-start | bytes 786440 | tf_op jit(solution)/shard_map/ppermute | solution.py:158
  102.5 26.0 %collective-permute-start.13 = (bf16[256,512]{1,0:T(8,128)(2,1)S(1)}, bf16[256,512]{1,0:T(8,128)(2,1)S(1)}, u32[]{:S(2)}, u32[]{:S(2)}) collective-permute-start(bf16[256,512]{1,0:T(8,128)(2,1)S(1)} %get-tuple-element.28), channel_id=1, source_target_pairs={{0,3},{1,2},{2,1},{3,0},{4,7},{5,6},{6,5},{7,4},{8,11},{9,10},{10,... | collective-permute-start | bytes 786440 | tf_op jit(solution)/shard_map/ppermute | solution.py:158
  105.0 17.4 %collective-permute-start.19 = (bf16[256,512]{1,0:T(8,128)(2,1)S(1)}, bf16[256,512]{1,0:T(8,128)(2,1)S(1)}, u32[]{:S(2)}, u32[]{:S(2)}) collective-permute-start(bf16[256,512]{1,0:T(8,128)(2,1)S(1)} %get-tuple-element.32), channel_id=1, source_target_pairs={{0,2},{1,3},{2,0},{3,1},{4,6},{5,7},{6,4},{7,5},{8,10},{9,11},{10,... | collective-permute-start | bytes 786440 | tf_op jit(solution)/shard_map/ppermute | solution.py:158
  107.7 19.8 %collective-permute-start.20 = (bf16[256,512]{1,0:T(8,128)(2,1)S(1)}, bf16[256,512]{1,0:T(8,128)(2,1)S(1)}, u32[]{:S(2)}, u32[]{:S(2)}) collective-permute-start(bf16[256,512]{1,0:T(8,128)(2,1)S(1)} %get-tuple-element.33), channel_id=1, source_target_pairs={{0,3},{1,2},{2,1},{3,0},{4,7},{5,6},{6,5},{7,4},{8,11},{9,10},{10,... | collective-permute-start | bytes 786440 | tf_op jit(solution)/shard_map/ppermute | solution.py:158

commit v2 on v1

--- a/solution.py
+++ b/solution.py
@@ -33,21 +33,107 @@
     return lax.ppermute(block, axis, route)
 
 
-def product(left, right, precision=lax.Precision.HIGHEST):
-    return jnp.dot(left, right, precision=precision, preferred_element_type=jnp.float32)
-
-
-def pack_upper(full):
-    step = full.shape[0] // PACK
-    rows = [full[i * step : (i + 1) * step, i * step :] for i in range(PACK)]
-    return [
-        jnp.concatenate([rows[0], rows[3]], axis=1),
-        jnp.concatenate([rows[1], rows[2]], axis=1),
-    ]
-
-
-def gram_sum(slab_part, share_count):
-    halves = pack_upper(product(slab_part, slab_part.T))
+def parts_of(value, count):
+    parts = []
+    for _ in range(count - 1):
+        high = value.astype(jnp.bfloat16)
+        parts.append(high)
+        value = value - high.astype(jnp.float32)
+    return parts + [value.astype(jnp.bfloat16)]
+
+
+def split_product(left, right, turned=False):
+    count = len(left)
+    total = None
+    for order in range(count - 1, -1, -1):
+        for i in range(order + 1):
+            term = lax.dot_general(
+                left[i],
+                right[order - i],
+                (((1,), (1 if turned else 0,)), ((), ())),
+                preferred_element_type=jnp.float32,
+            )
+            total = term if total is None else total + term
+    return total
+
+
+def deal_kernel(share_count, owned, gradient, *refs):
+    outs, done = refs[:-1], refs[-1]
+    group = lax.axis_index("grp")
+    place = lax.axis_index("dev")
+    cols = outs[0].shape[1]
+    moves = []
+    for turn, out in enumerate(outs):
+        target = place ^ turn
+        column = pl.multiple_of((target % share_count) * cols, cols)
+        block = gradient.at[owned[group, target // share_count], :, pl.ds(column, cols)]
+        moves.append(pltpu.make_async_copy(block, out, done.at[turn]))
+    for move in moves:
+        move.start()
+    for move in moves:
+        move.wait()
+
+
+def deal(gradient, owned_matrix, share_count):
+    quads, rows, columns = gradient.shape
+    turns = quads * share_count
+    block = jax.ShapeDtypeStruct((rows, columns // share_count), gradient.dtype)
+    return pl.pallas_call(
+        functools.partial(deal_kernel, share_count),
+        out_shape=[block] * turns,
+        in_specs=[pl.BlockSpec(memory_space=pltpu.SMEM), pl.BlockSpec(memory_space=pl.ANY)],
+        out_specs=[pl.BlockSpec(memory_space=pltpu.VMEM)] * turns,
+        scratch_shapes=[pltpu.SemaphoreType.DMA((turns,))],
+        cost_estimate=pl.CostEstimate(
+            flops=0, bytes_accessed=4 * gradient.size, transcendentals=0
+        ),
+        compiler_params=pltpu.CompilerParams(vmem_limit_bytes=8 << 20),
+    )(owned_matrix, gradient)
+
+
+def gram_kernel(m_ref, *refs):
+    blocks, (nm_ref, p_ref, a_ref, b_ref) = refs[:-4], refs[-4:]
+    place = lax.axis_index("dev") if len(blocks) > 1 else 0
+    for turn, block in enumerate(blocks):
+        size = block.shape[0]
+        rows = pl.ds(pl.multiple_of((place ^ turn) * size, size), size)
+        grad = block[...].astype(jnp.float32)
+        moment = momentum_decay * m_ref[rows, :] + grad
+        nm_ref[rows, :] = moment
+        p_ref[rows, :] = grad + momentum_decay * moment
+    parts = parts_of(p_ref[...], 3)
+    step = p_ref.shape[0] // PACK
+
+    def band(i):
+        low = i * step
+        return split_product(
+            [part[low : low + step] for part in parts], [part[low:] for part in parts], turned=True
+        )
+
+    for ref, first, second in ((a_ref, 0, 3), (b_ref, 1, 2)):
+        width = (PACK - first) * step
+        ref[:, :width] = band(first)
+        ref[:, width:] = band(second)
+
+
+def gram_halves(momentum, blocks):
+    rows, cols = momentum.shape
+    vmem = pl.BlockSpec(memory_space=pltpu.VMEM)
+    f32 = jax.ShapeDtypeStruct((rows, cols), jnp.float32)
+    half = jax.ShapeDtypeStruct((rows // PACK, rows // PACK * (PACK + 1)), jnp.float32)
+    return pl.pallas_call(
+        gram_kernel,
+        out_shape=[f32, f32, half, half],
+        in_specs=[vmem] * (1 + len(blocks)),
+        out_specs=[vmem] * 4,
+        cost_estimate=pl.CostEstimate(
+            flops=8 * rows * rows * cols, bytes_accessed=16 * rows * cols, transcendentals=0
+        ),
+        compiler_params=pltpu.CompilerParams(vmem_limit_bytes=24 << 20),
+    )(momentum, *blocks)
+
+
+def gram_sum(halves, share_count):
     moved = [jnp.zeros_like(half) for half in halves]
     bits = list(range(share_count.bit_length() - 1))
     orders = [bits, bits[::-1]]
@@ -55,25 +141,6 @@
         halves = [half + other for half, other in zip(halves, moved)] if turn else halves
         moved = [from_partner(half, "dev", order[turn]) for half, order in zip(halves, orders)]
     return halves, moved
-
-
-def parts_of(value, count):
-    parts = []
-    for _ in range(count - 1):
-        high = value.astype(jnp.bfloat16)
-        parts.append(high)
-        value = value - high.astype(jnp.float32)
-    return parts + [value.astype(jnp.bfloat16)]
-
-
-def split_product(left, right):
-    count = len(left)
-    total = None
-    for order in range(count - 1, -1, -1):
-        for i in range(order + 1):
-            term = jnp.dot(left[i], right[order - i], preferred_element_type=jnp.float32)
-            total = term if total is None else total + term
-    return total
 
 
 def newton_kernel(iters, scale, a0, a1, b0, b1, p_ref, w_ref, u_ref, n_ref, r_ref, *rest):
@@ -335,26 +402,36 @@
         and not share_count & (share_count - 1)
         and not group_count & (group_count - 1)
     )
-    mine = lax.dynamic_index_in_dim(owned_matrix, group, 0, keepdims=False)
-    local_ids = jnp.arange(quads, dtype=jnp.int32)
-    picker = (mine[:, None] == local_ids[None, :]).astype(jnp.bfloat16)
-    ordered = jnp.einsum(
-        "qm,mrc->rqc", picker, gradient, preferred_element_type=jnp.float32
-    ).astype(jnp.bfloat16)
-    arrived = lax.all_to_all(
-        ordered.reshape(row_block, dev_count, slab_cols),
-        "dev",
-        split_axis=1,
-        concat_axis=0,
-        tiled=True,
-    )
-    grad_slab = arrived.reshape(row_count, slab_cols).astype(jnp.float32)
-    new_moment = momentum_decay * momentum[0] + grad_slab
-    nesterov = grad_slab + momentum_decay * new_moment
+    two_halves = (
+        quads == 2
+        and dev_count == quads * share_count
+        and not share_count & (share_count - 1)
+        and not group_count & (group_count - 1)
+    )
     if two_halves:
+        dealt = list(deal(gradient, owned_matrix, share_count))
+        for turn in [*range(share_count, dev_count), *range(1, share_count)]:
+            dealt[turn] = flipped(dealt[turn], "dev", turn)
         slots = wanted_slots(rollout_matrix, owned_matrix, share_count)
-        nesterov, slots = lax.optimization_barrier((nesterov, slots))
-    halves, moved = gram_sum(nesterov, share_count)
+    else:
+        mine = lax.dynamic_index_in_dim(owned_matrix, group, 0, keepdims=False)
+        local_ids = jnp.arange(quads, dtype=jnp.int32)
+        picker = (mine[:, None] == local_ids[None, :]).astype(jnp.bfloat16)
+        ordered = jnp.einsum(
+            "qm,mrc->rqc", picker, gradient, preferred_element_type=jnp.float32
+        ).astype(jnp.bfloat16)
+        arrived = lax.all_to_all(
+            ordered.reshape(row_block, dev_count, slab_cols),
+            "dev",
+            split_axis=1,
+            concat_axis=0,
+            tiled=True,
+        )
+        dealt = [arrived.reshape(row_count, slab_cols)]
+    new_moment, nesterov, *halves = gram_halves(momentum[0], dealt)
+    if two_halves:
+        halves, slots = lax.optimization_barrier((halves, slots))
+    halves, moved = gram_sum(halves, share_count)
     scale_factor = 0.2 * math.sqrt(max(row_count, columns))
     update, new_weight, rounded, *pieces = newton(
         halves, moved, nesterov, master_weight[0], ITERS, scale_factor, CHUNKS if two_halves else 0

time: 130 us -> 127 us (0.977)
  waiting for transfers between devices: 77.5 us -> 65.8 us
  starting transfers between devices: 21.7 us -> 28.4 us
  Pallas kernels: 22.6 us -> 26.2 us
  matrix products: 2.62 us -> 0 us
    all_to_all x1 -> x0, waiting for transfers between devices: 13.9 us -> none  [step(): lax.all_to_all(ordered.reshape(row_block, dev_count, slab_cols), 'dev', s...]
    ppermute x17 -> x24, starting transfers between devices: 12.7 us -> 24.2 us  [flipped(): lax.ppermute(block, axis, [(i, i ^ flip) for i in range(lax.axis_size(axi...]
    all_to_all x1 -> x0, starting transfers between devices: 7.31 us -> none  [step(): lax.all_to_all(ordered.reshape(row_block, dev_count, slab_cols), 'dev', s...]
    ppermute x17 -> x24, waiting for transfers between devices: 47.3 us -> 53.8 us  [flipped(): lax.ppermute(block, axis, [(i, i ^ flip) for i in range(lax.axis_size(axi...]
    ppermute x4, waiting for transfers between devices: 16.3 us -> 11.9 us  [from_partner(): return lax.ppermute(block, axis, route)]
    pallas_call x0 -> x2, Pallas kernels: none -> 3.58 us  [the longest x1 2.73 us: gram_halves(): pl.pallas_call(gram_kernel, out_shape=[f32, f32, half, half], in_specs=[v...]
    unnamed x10 -> x7, local copies, waits for them, and re-layouts: 0.15 us -> 3.04 us
    dot_general x2 -> x0, matrix products: 2.62 us -> none  [the longest x1 1.86 us: product(): jnp.dot(left, right, precision=precision, preferred_element_type=jnp.floa...]
  transfers between devices with their start and end apart: 22 -> 28, of which waited for: 12 -> 17; matrix products, arithmetic and copies ran while one was open for 1% -> 2% of each run, Pallas kernels for 2% -> 2%
where the time goes in v2:
time: 127 us
  waiting for transfers between devices  65.8 us (52%)
  starting transfers between devices  28.4 us (22%)
  Pallas kernels  26.2 us (21%)
  local copies, waits for them, and re-layouts  3.22 us (3%)
  other arithmetic  2.45 us (2%)
    ppermute x24, waiting for transfers between devices, flipped(): lax.ppermute(block, axis, [(i, i ^ flip) for i in range(lax.axis_size(axi...  53.8 us
    ppermute x24, starting transfers between devices, flipped(): lax.ppermute(block, axis, [(i, i ^ flip) for i in range(lax.axis_size(axi...  24.2 us
    pallas_call x1, Pallas kernels, newton(): pl.pallas_call(functools.partial(newton_kernel, iters, scale), out_shape=...  19 us
    ppermute x4, waiting for transfers between devices, from_partner(): return lax.ppermute(block, axis, route)  11.9 us
    ppermute x4, starting transfers between devices, from_partner(): return lax.ppermute(block, axis, route)  4.1 us
    unnamed x7, local copies, waits for them, and re-layouts  3.04 us
    pallas_call x1, Pallas kernels, gram_halves(): pl.pallas_call(gram_kernel, out_shape=[f32, f32, half, half], in_specs=[v...  2.73 us
  transfers between devices with their start and end apart: 28, of which 17 were waited for; matrix products, arithmetic and copies ran while one was open for 2% of the time, Pallas kernels for 2%

profile of v2, /device:TPU:0, one launch (start us, length us, event | category | flops | bytes accessed | tf_op | source)
XLA Modules:
  0.0 126.8 jit_solution(1485591262901630040)
XLA Ops:
  1.4 1.0 copy-done
  3.3 3.1 %collective-permute-start = (bf16[64,512]{1,0:T(8,128)(2,1)S(1)}, bf16[64,512]{1,0:T(8,128)(2,1)S(1)}, u32[]{:S(2)}, u32[]{:S(2)}) collective-permute-start(bf16[64,512]{1,0:T(8,128)(2,1)S(1)} %get-tuple-element.33), channel_id=1, source_target_pairs={{0,1},{1,0},{2,3},{3,2},{4,5},{5,4},{6,7},{7,6},{8,9},{9,8},{10,11... | collective-permute-start | bytes 196616 | tf_op jit(solution)/shard_map/ppermute | solution.py:225
  6.3 1.6 %collective-permute-start.1 = (bf16[64,512]{1,0:T(8,128)(2,1)S(1)}, bf16[64,512]{1,0:T(8,128)(2,1)S(1)}, u32[]{:S(2)}, u32[]{:S(2)}) collective-permute-start(bf16[64,512]{1,0:T(8,128)(2,1)S(1)} %get-tuple-element.34), channel_id=1, source_target_pairs={{0,2},{1,3},{2,0},{3,1},{4,6},{5,7},{6,4},{7,5},{8,10},{9,11},{10,... | collective-permute-start | bytes 196616 | tf_op jit(solution)/shard_map/ppermute | solution.py:225
  7.9 3.0 %collective-permute-start.3 = (bf16[64,512]{1,0:T(8,128)(2,1)S(1)}, bf16[64,512]{1,0:T(8,128)(2,1)S(1)}, u32[]{:S(2)}, u32[]{:S(2)}) collective-permute-start(bf16[64,512]{1,0:T(8,128)(2,1)S(1)} %get-tuple-element.36), channel_id=1, source_target_pairs={{0,4},{1,5},{2,6},{3,7},{4,0},{5,1},{6,2},{7,3},{8,12},{9,13},{10,... | collective-permute-start | bytes 196616 | tf_op jit(solution)/shard_map/ppermute | solution.py:225
  10.9 1.3 %collective-permute-start.4 = (bf16[64,512]{1,0:T(8,128)(2,1)S(1)}, bf16[64,512]{1,0:T(8,128)(2,1)S(1)}, u32[]{:S(2)}, u32[]{:S(2)}) collective-permute-start(bf16[64,512]{1,0:T(8,128)(2,1)S(1)} %get-tuple-element.37), channel_id=1, source_target_pairs={{0,5},{1,4},{2,7},{3,6},{4,1},{5,0},{6,3},{7,2},{8,13},{9,12},{10,... | collective-permute-start | bytes 196616 | tf_op jit(solution)/shard_map/ppermute | solution.py:225
  14.6 3.7 %collective-permute-start.5 = (bf16[64,512]{1,0:T(8,128)(2,1)S(1)}, bf16[64,512]{1,0:T(8,128)(2,1)S(1)}, u32[]{:S(2)}, u32[]{:S(2)}) collective-permute-start(bf16[64,512]{1,0:T(8,128)(2,1)S(1)} %get-tuple-element.38), channel_id=1, source_target_pairs={{0,6},{1,7},{2,4},{3,5},{4,2},{5,3},{6,0},{7,1},{8,14},{9,15},{10,... | collective-permute-start | bytes 196616 | tf_op jit(solution)/shard_map/ppermute | solution.py:225
  18.5 1.2 collective-permute-done.4.refs_5_
  19.7 1.1 collective-permute-done.5.refs_6_
  20.8 4.4 %collective-permute-done.6.refs_7_ = bf16[64,512]{1,0:T(8,128)(2,1)S(1)} collective-permute-done((bf16[64,512]{1,0:T(8,128)(2,1)S(1)}, bf16[64,512]{1,0:T(8,128)(2,1)S(1)}, u32[]{:S(2)}, u32[]{:S(2)}) %collective-permute-start.6) | collective-permute-done | bytes 65568 | tf_op jit(solution)/shard_map/ppermute | solution.py:225
  25.2 1.2 copy-done.1
  26.5 2.7 %shard_map.85 = (f32[512,512]{1,0:T(8,128)}, f32[512,512]{1,0:T(8,128)S(1)}, f32[128,640]{1,0:T(8,128)S(1)}, f32[128,640]{1,0:T(8,128)S(1)}) custom-call(f32[512,512]{1,0:T(8,128)S(1)} %bitcast.13, bf16[64,512]{1,0:T(8,128)(2,1)S(1)} %get-tuple-element.32.refs_0_, bf16[64,512]{1,0:T(8,128)(2,1)S(1)} %collective-permute-done.refs_1_, ...), custom_call_target="tpu_custom_call" | custom-call | flops 1073741824 | bytes 4194304 | tf_op jit(solution)/shard_map/pallas_call | solution.py:124
  29.8 6.5 %collective-permute-done.7 = f32[128,640]{1,0:T(8,128)S(1)} collective-permute-done((f32[128,640]{1,0:T(8,128)S(1)}, f32[128,640]{1,0:T(8,128)S(1)}, u32[]{:S(2)}, u32[]{:S(2)}) %collective-permute-start.7) | collective-permute-done | bytes 327712 | tf_op jit(solution)/shard_map/ppermute | solution.py:33
  37.4 2.9 %collective-permute-start.10 = (f32[128,640]{1,0:T(8,128)S(1)}, f32[128,640]{1,0:T(8,128)S(1)}, u32[]{:S(2)}, u32[]{:S(2)}) collective-permute-start(f32[128,640]{1,0:T(8,128)S(1)} %add.15.b0), channel_id=1, source_target_pairs={{0,1},{1,0},{2,3},{3,2},{4,5},{5,4},{6,7},{7,6},{8,9},{9,8},{10,11... | collective-permute-start | bytes 983048 | tf_op jit(solution)/shard_map/ppermute | solution.py:33
  40.3 3.6 %collective-permute-done.8.a1 = f32[128,640]{1,0:T(8,128)S(1)} collective-permute-done((f32[128,640]{1,0:T(8,128)S(1)}, f32[128,640]{1,0:T(8,128)S(1)}, u32[]{:S(2)}, u32[]{:S(2)}) %collective-permute-start.8) | collective-permute-done | bytes 327712 | tf_op jit(solution)/shard_map/ppermute | solution.py:33
  43.9 1.4 %collective-permute-done.10.b1 = f32[128,640]{1,0:T(8,128)S(1)} collective-permute-done((f32[128,640]{1,0:T(8,128)S(1)}, f32[128,640]{1,0:T(8,128)S(1)}, u32[]{:S(2)}, u32[]{:S(2)}) %collective-permute-start.10) | collective-permute-done | bytes 327712 | tf_op jit(solution)/shard_map/ppermute | solution.py:33
  45.3 19.0 %shard_map.86 = (f32[512,512]{1,0:T(8,128)}, f32[512,512]{1,0:T(8,128)}, bf16[512,512]{1,0:T(8,128)(2,1)S(1)}, bf16[256,512]{1,0:T(8,128)(2,1)S(1)}, bf16[256,512]{1,0:T(8,128)(2,1)S(1)}) custom-call(f32[128,640]{1,0:T(8,128)S(1)} %add.14.a0, f32[128,640]{1,0:T(8,128)S(1)} %collective-permute-done.8.a1, f32[128,640]{1,0:T(8,128)S(1)} %add.15.b0, ...), custom_call_target="tpu_custom_call" | custom-call | flops 16106127360 | bytes 6291456 | tf_op jit(solution)/shard_map/pallas_call | solution.py:208
  64.3 1.5 %collective-permute-start.14 = (bf16[512,512]{1,0:T(8,128)(2,1)S(1)}, bf16[512,512]{1,0:T(8,128)(2,1)S(1)}, u32[]{:S(2)}, u32[]{:S(2)}) collective-permute-start(bf16[512,512]{1,0:T(8,128)(2,1)S(1)} %get-tuple-element.49.refs_0_), channel_id=1, source_target_pairs={{0,16},{8,24},{16,0},{24,8},{1,17},{9,25},{17,1},{25,9},{2,18},{10... | collective-permute-start | bytes 1572872 | tf_op jit(solution)/shard_map/ppermute | solution.py:225
  65.8 2.2 %collective-permute-start.21 = (bf16[256,512]{1,0:T(8,128)(2,1)S(1)}, bf16[256,512]{1,0:T(8,128)(2,1)S(1)}, u32[]{:S(2)}, u32[]{:S(2)}) collective-permute-start(bf16[256,512]{1,0:T(8,128)(2,1)S(1)} %get-tuple-element.55), channel_id=1, source_target_pairs={{0,4},{1,5},{2,6},{3,7},{4,0},{5,1},{6,2},{7,3},{8,12},{9,13},{10,... | collective-permute-start | bytes 786440 | tf_op jit(solution)/shard_map/ppermute | solution.py:225
  68.8 15.6 %collective-permute-done.21.refs_1_ = bf16[256,512]{1,0:T(8,128)(2,1)S(1)} collective-permute-done((bf16[256,512]{1,0:T(8,128)(2,1)S(1)}, bf16[256,512]{1,0:T(8,128)(2,1)S(1)}, u32[]{:S(2)}, u32[]{:S(2)}) %collective-permute-start.21) | collective-permute-done | bytes 262176 | tf_op jit(solution)/shard_map/ppermute | solution.py:225
  84.9 4.1 %collective-permute-done.11.refs_1_ = bf16[256,512]{1,0:T(8,128)(2,1)S(1)} collective-permute-done((bf16[256,512]{1,0:T(8,128)(2,1)S(1)}, bf16[256,512]{1,0:T(8,128)(2,1)S(1)}, u32[]{:S(2)}, u32[]{:S(2)}) %collective-permute-start.11) | collective-permute-done | bytes 262176 | tf_op jit(solution)/shard_map/ppermute | solution.py:225
  89.4 1.4 %collective-permute-done.23.refs_5_ = bf16[256,512]{1,0:T(8,128)(2,1)S(1)} collective-permute-done((bf16[256,512]{1,0:T(8,128)(2,1)S(1)}, bf16[256,512]{1,0:T(8,128)(2,1)S(1)}, u32[]{:S(2)}, u32[]{:S(2)}) %collective-permute-start.23) | collective-permute-done | bytes 262176 | tf_op jit(solution)/shard_map/ppermute | solution.py:225
  91.3 5.0 %collective-permute-done.15.refs_5_ = bf16[256,512]{1,0:T(8,128)(2,1)S(1)} collective-permute-done((bf16[256,512]{1,0:T(8,128)(2,1)S(1)}, bf16[256,512]{1,0:T(8,128)(2,1)S(1)}, u32[]{:S(2)}, u32[]{:S(2)}) %collective-permute-start.15) | collective-permute-done | bytes 262176 | tf_op jit(solution)/shard_map/ppermute | solution.py:225
  97.2 1.2 collective-permute-start.25
  99.2 1.0 collective-permute-start.18
  101.2 1.6 %collective-permute-start.27 = (bf16[256,512]{1,0:T(8,128)(2,1)S(1)}, bf16[256,512]{1,0:T(8,128)(2,1)S(1)}, u32[]{:S(2)}, u32[]{:S(2)}) collective-permute-start(bf16[256,512]{1,0:T(8,128)(2,1)S(1)} %get-tuple-element.59), channel_id=1, source_target_pairs={{0,3},{1,2},{2,1},{3,0},{4,7},{5,6},{6,5},{7,4},{8,11},{9,10},{10,... | collective-permute-start | bytes 786440 | tf_op jit(solution)/shard_map/ppermute | solution.py:225
  103.2 3.2 %collective-permute-done.25.refs_1_ = bf16[256,512]{1,0:T(8,128)(2,1)S(1)} collective-permute-done((bf16[256,512]{1,0:T(8,128)(2,1)S(1)}, bf16[256,512]{1,0:T(8,128)(2,1)S(1)}, u32[]{:S(2)}, u32[]{:S(2)}) %collective-permute-start.25) | collective-permute-done | bytes 262176 | tf_op jit(solution)/shard_map/ppermute | solution.py:225
  107.0 2.4 %collective-permute-done.26.refs_2_ = bf16[256,512]{1,0:T(8,128)(2,1)S(1)} collective-permute-done((bf16[256,512]{1,0:T(8,128)(2,1)S(1)}, bf16[256,512]{1,0:T(8,128)(2,1)S(1)}, u32[]{:S(2)}, u32[]{:S(2)}) %collective-permute-start.26) | collective-permute-done | bytes 262176 | tf_op jit(solution)/shard_map/ppermute | solution.py:225
  109.4 6.2 %collective-permute-done.27.refs_3_ = bf16[256,512]{1,0:T(8,128)(2,1)S(1)} collective-permute-done((bf16[256,512]{1,0:T(8,128)(2,1)S(1)}, bf16[256,512]{1,0:T(8,128)(2,1)S(1)}, u32[]{:S(2)}, u32[]{:S(2)}) %collective-permute-start.27) | collective-permute-done | bytes 262176 | tf_op jit(solution)/shard_map/ppermute | solution.py:225
  115.6 1.0 shard_map.89.refs_4_
  117.2 3.4 %collective-permute-done.19.refs_2_ = bf16[256,512]{1,0:T(8,128)(2,1)S(1)} collective-permute-done((bf16[256,512]{1,0:T(8,128)(2,1)S(1)}, bf16[256,512]{1,0:T(8,128)(2,1)S(1)}, u32[]{:S(2)}, u32[]{:S(2)}) %collective-permute-start.19) | collective-permute-done | bytes 262176 | tf_op jit(solution)/shard_map/ppermute | solution.py:225
  120.6 5.1 %collective-permute-done.20.refs_3_ = bf16[256,512]{1,0:T(8,128)(2,1)S(1)} collective-permute-done((bf16[256,512]{1,0:T(8,128)(2,1)S(1)}, bf16[256,512]{1,0:T(8,128)(2,1)S(1)}, u32[]{:S(2)}, u32[]{:S(2)}) %collective-permute-start.20) | collective-permute-done | bytes 262176 | tf_op jit(solution)/shard_map/ppermute | solution.py:225
  125.8 1.0 shard_map.90
  (47 shorter events, 12.3 us)
Async XLA Ops:
  1.4 1.0 copy-start
  3.3 11.3 %collective-permute-start = (bf16[64,512]{1,0:T(8,128)(2,1)S(1)}, bf16[64,512]{1,0:T(8,128)(2,1)S(1)}, u32[]{:S(2)}, u32[]{:S(2)}) collective-permute-start(bf16[64,512]{1,0:T(8,128)(2,1)S(1)} %get-tuple-element.33), channel_id=1, source_target_pairs={{0,1},{1,0},{2,3},{3,2},{4,5},{5,4},{6,7},{7,6},{8,9},{9,8},{10,11... | collective-permute-start | bytes 196616 | tf_op jit(solution)/shard_map/ppermute | solution.py:225
  6.3 11.9 %collective-permute-start.1 = (bf16[64,512]{1,0:T(8,128)(2,1)S(1)}, bf16[64,512]{1,0:T(8,128)(2,1)S(1)}, u32[]{:S(2)}, u32[]{:S(2)}) collective-permute-start(bf16[64,512]{1,0:T(8,128)(2,1)S(1)} %get-tuple-element.34), channel_id=1, source_target_pairs={{0,2},{1,3},{2,0},{3,1},{4,6},{5,7},{6,4},{7,5},{8,10},{9,11},{10,... | collective-permute-start | bytes 196616 | tf_op jit(solution)/shard_map/ppermute | solution.py:225
  7.9 10.6 %collective-permute-start.2 = (bf16[64,512]{1,0:T(8,128)(2,1)S(1)}, bf16[64,512]{1,0:T(8,128)(2,1)S(1)}, u32[]{:S(2)}, u32[]{:S(2)}) collective-permute-start(bf16[64,512]{1,0:T(8,128)(2,1)S(1)} %get-tuple-element.35), channel_id=1, source_target_pairs={{0,3},{1,2},{2,1},{3,0},{4,7},{5,6},{6,5},{7,4},{8,11},{9,10},{10,... | collective-permute-start | bytes 196616 | tf_op jit(solution)/shard_map/ppermute | solution.py:225
  7.9 10.6 %collective-permute-start.3 = (bf16[64,512]{1,0:T(8,128)(2,1)S(1)}, bf16[64,512]{1,0:T(8,128)(2,1)S(1)}, u32[]{:S(2)}, u32[]{:S(2)}) collective-permute-start(bf16[64,512]{1,0:T(8,128)(2,1)S(1)} %get-tuple-element.36), channel_id=1, source_target_pairs={{0,4},{1,5},{2,6},{3,7},{4,0},{5,1},{6,2},{7,3},{8,12},{9,13},{10,... | collective-permute-start | bytes 196616 | tf_op jit(solution)/shard_map/ppermute | solution.py:225
  10.9 8.8 %collective-permute-start.4 = (bf16[64,512]{1,0:T(8,128)(2,1)S(1)}, bf16[64,512]{1,0:T(8,128)(2,1)S(1)}, u32[]{:S(2)}, u32[]{:S(2)}) collective-permute-start(bf16[64,512]{1,0:T(8,128)(2,1)S(1)} %get-tuple-element.37), channel_id=1, source_target_pairs={{0,5},{1,4},{2,7},{3,6},{4,1},{5,0},{6,3},{7,2},{8,13},{9,12},{10,... | collective-permute-start | bytes 196616 | tf_op jit(solution)/shard_map/ppermute | solution.py:225
  14.6 6.2 %collective-permute-start.5 = (bf16[64,512]{1,0:T(8,128)(2,1)S(1)}, bf16[64,512]{1,0:T(8,128)(2,1)S(1)}, u32[]{:S(2)}, u32[]{:S(2)}) collective-permute-start(bf16[64,512]{1,0:T(8,128)(2,1)S(1)} %get-tuple-element.38), channel_id=1, source_target_pairs={{0,6},{1,7},{2,4},{3,5},{4,2},{5,3},{6,0},{7,1},{8,14},{9,15},{10,... | collective-permute-start | bytes 196616 | tf_op jit(solution)/shard_map/ppermute | solution.py:225
  18.3 7.0 %collective-permute-start.6 = (bf16[64,512]{1,0:T(8,128)(2,1)S(1)}, bf16[64,512]{1,0:T(8,128)(2,1)S(1)}, u32[]{:S(2)}, u32[]{:S(2)}) collective-permute-start(bf16[64,512]{1,0:T(8,128)(2,1)S(1)} %get-tuple-element.39), channel_id=1, source_target_pairs={{0,7},{1,6},{2,5},{3,4},{4,3},{5,2},{6,1},{7,0},{8,15},{9,14},{10,... | collective-permute-start | bytes 196616 | tf_op jit(solution)/shard_map/ppermute | solution.py:225
  25.2 1.2 copy-start.1
  26.5 18.9 %copy-start.2 = (f32[1,512,512]{2,1,0:T(8,128)S(1)}, f32[1,512,512]{2,1,0:T(8,128)}, u32[]{:S(2)}) copy-start(f32[1,512,512]{2,1,0:T(8,128)} %param.7) | copy-start | bytes 3145732
  29.2 7.1 %collective-permute-start.7 = (f32[128,640]{1,0:T(8,128)S(1)}, f32[128,640]{1,0:T(8,128)S(1)}, u32[]{:S(2)}, u32[]{:S(2)}) collective-permute-start(f32[128,640]{1,0:T(8,128)S(1)} %get-tuple-element.43), channel_id=1, source_target_pairs={{0,1},{1,0},{2,3},{3,2},{4,5},{5,4},{6,7},{7,6},{8,9},{9,8},{10,11... | collective-permute-start | bytes 983048 | tf_op jit(solution)/shard_map/ppermute | solution.py:33
  29.8 7.5 %collective-permute-start.9 = (f32[128,640]{1,0:T(8,128)S(1)}, f32[128,640]{1,0:T(8,128)S(1)}, u32[]{:S(2)}, u32[]{:S(2)}) collective-permute-start(f32[128,640]{1,0:T(8,128)S(1)} %get-tuple-element.44), channel_id=1, source_target_pairs={{0,2},{2,0},{1,3},{3,1},{4,6},{6,4},{5,7},{7,5},{8,10},{10,8},{9,1... | collective-permute-start | bytes 983048 | tf_op jit(solution)/shard_map/ppermute | solution.py:33
  36.4 7.5 %collective-permute-start.8 = (f32[128,640]{1,0:T(8,128)S(1)}, f32[128,640]{1,0:T(8,128)S(1)}, u32[]{:S(2)}, u32[]{:S(2)}) collective-permute-start(f32[128,640]{1,0:T(8,128)S(1)} %add.14.a0), channel_id=1, source_target_pairs={{0,2},{2,0},{1,3},{3,1},{4,6},{6,4},{5,7},{7,5},{8,10},{10,8},{9,1... | collective-permute-start | bytes 983048 | tf_op jit(solution)/shard_map/ppermute | solution.py:33
  37.4 7.9 %collective-permute-start.10 = (f32[128,640]{1,0:T(8,128)S(1)}, f32[128,640]{1,0:T(8,128)S(1)}, u32[]{:S(2)}, u32[]{:S(2)}) collective-permute-start(f32[128,640]{1,0:T(8,128)S(1)} %add.15.b0), channel_id=1, source_target_pairs={{0,1},{1,0},{2,3},{3,2},{4,5},{5,4},{6,7},{7,6},{8,9},{9,8},{10,11... | collective-permute-start | bytes 983048 | tf_op jit(solution)/shard_map/ppermute | solution.py:33
  64.3 20.5 %collective-permute-start.14 = (bf16[512,512]{1,0:T(8,128)(2,1)S(1)}, bf16[512,512]{1,0:T(8,128)(2,1)S(1)}, u32[]{:S(2)}, u32[]{:S(2)}) collective-permute-start(bf16[512,512]{1,0:T(8,128)(2,1)S(1)} %get-tuple-element.49.refs_0_), channel_id=1, source_target_pairs={{0,16},{8,24},{16,0},{24,8},{1,17},{9,25},{17,1},{25,9},{2,18},{10... | collective-permute-start | bytes 1572872 | tf_op jit(solution)/shard_map/ppermute | solution.py:225
  65.8 18.5 %collective-permute-start.21 = (bf16[256,512]{1,0:T(8,128)(2,1)S(1)}, bf16[256,512]{1,0:T(8,128)(2,1)S(1)}, u32[]{:S(2)}, u32[]{:S(2)}) collective-permute-start(bf16[256,512]{1,0:T(8,128)(2,1)S(1)} %get-tuple-element.55), channel_id=1, source_target_pairs={{0,4},{1,5},{2,6},{3,7},{4,0},{5,1},{6,2},{7,3},{8,12},{9,13},{10,... | collective-permute-start | bytes 786440 | tf_op jit(solution)/shard_map/ppermute | solution.py:225
  68.0 22.8 %collective-permute-start.12 = (bf16[512,512]{1,0:T(8,128)(2,1)S(1)}, bf16[512,512]{1,0:T(8,128)(2,1)S(1)}, u32[]{:S(2)}, u32[]{:S(2)}) collective-permute-start(bf16[512,512]{1,0:T(8,128)(2,1)S(1)} %get-tuple-element.49.refs_0_), channel_id=1, source_target_pairs={{0,8},{8,0},{16,24},{24,16},{1,9},{9,1},{17,25},{25,17},{2,10},{10... | collective-permute-start | bytes 1572872 | tf_op jit(solution)/shard_map/ppermute | solution.py:225
  68.0 20.9 %collective-permute-start.11 = (bf16[256,512]{1,0:T(8,128)(2,1)S(1)}, bf16[256,512]{1,0:T(8,128)(2,1)S(1)}, u32[]{:S(2)}, u32[]{:S(2)}) collective-permute-start(bf16[256,512]{1,0:T(8,128)(2,1)S(1)} %get-tuple-element.50), channel_id=1, source_target_pairs={{0,4},{1,5},{2,6},{3,7},{4,0},{5,1},{6,2},{7,3},{8,12},{9,13},{10,... | collective-permute-start | bytes 786440 | tf_op jit(solution)/shard_map/ppermute | solution.py:225
  84.3 6.4 %collective-permute-start.23 = (bf16[256,512]{1,0:T(8,128)(2,1)S(1)}, bf16[256,512]{1,0:T(8,128)(2,1)S(1)}, u32[]{:S(2)}, u32[]{:S(2)}) collective-permute-start(bf16[256,512]{1,0:T(8,128)(2,1)S(1)} %collective-permute-done.21.refs_1_), channel_id=1, source_target_pairs={{0,16},{8,24},{16,0},{24,8},{1,17},{9,25},{17,1},{25,9},{2,18},{10... | collective-permute-start | bytes 786440 | tf_op jit(solution)/shard_map/ppermute | solution.py:225
  84.9 11.5 %collective-permute-start.16 = (bf16[512,512]{1,0:T(8,128)(2,1)S(1)}, bf16[512,512]{1,0:T(8,128)(2,1)S(1)}, u32[]{:S(2)}, u32[]{:S(2)}) collective-permute-start(bf16[512,512]{1,0:T(8,128)(2,1)S(1)} %collective-permute-done.14.refs_4_), channel_id=1, source_target_pairs={{0,8},{8,0},{16,24},{24,16},{1,9},{9,1},{17,25},{25,17},{2,10},{10... | collective-permute-start | bytes 1572872 | tf_op jit(solution)/shard_map/ppermute | solution.py:225
  88.9 7.4 %collective-permute-start.15 = (bf16[256,512]{1,0:T(8,128)(2,1)S(1)}, bf16[256,512]{1,0:T(8,128)(2,1)S(1)}, u32[]{:S(2)}, u32[]{:S(2)}) collective-permute-start(bf16[256,512]{1,0:T(8,128)(2,1)S(1)} %collective-permute-done.11.refs_1_), channel_id=1, source_target_pairs={{0,16},{8,24},{16,0},{24,8},{1,17},{9,25},{17,1},{25,9},{2,18},{10... | collective-permute-start | bytes 786440 | tf_op jit(solution)/shard_map/ppermute | solution.py:225
  89.4 6.9 %collective-permute-start.22 = (bf16[256,512]{1,0:T(8,128)(2,1)S(1)}, bf16[256,512]{1,0:T(8,128)(2,1)S(1)}, u32[]{:S(2)}, u32[]{:S(2)}) collective-permute-start(bf16[256,512]{1,0:T(8,128)(2,1)S(1)} %collective-permute-done.21.refs_1_), channel_id=1, source_target_pairs={{0,8},{8,0},{16,24},{24,16},{1,9},{9,1},{17,25},{25,17},{2,10},{10... | collective-permute-start | bytes 786440 | tf_op jit(solution)/shard_map/ppermute | solution.py:225
  90.8 5.5 %collective-permute-start.24 = (bf16[256,512]{1,0:T(8,128)(2,1)S(1)}, bf16[256,512]{1,0:T(8,128)(2,1)S(1)}, u32[]{:S(2)}, u32[]{:S(2)}) collective-permute-start(bf16[256,512]{1,0:T(8,128)(2,1)S(1)} %collective-permute-done.23.refs_5_), channel_id=1, source_target_pairs={{0,8},{8,0},{16,24},{24,16},{1,9},{9,1},{17,25},{25,17},{2,10},{10... | collective-permute-start | bytes 786440 | tf_op jit(solution)/shard_map/ppermute | solution.py:225
  90.8 7.6 %collective-permute-start.13 = (bf16[256,512]{1,0:T(8,128)(2,1)S(1)}, bf16[256,512]{1,0:T(8,128)(2,1)S(1)}, u32[]{:S(2)}, u32[]{:S(2)}) collective-permute-start(bf16[256,512]{1,0:T(8,128)(2,1)S(1)} %collective-permute-done.11.refs_1_), channel_id=1, source_target_pairs={{0,8},{8,0},{16,24},{24,16},{1,9},{9,1},{17,25},{25,17},{2,10},{10... | collective-permute-start | bytes 786440 | tf_op jit(solution)/shard_map/ppermute | solution.py:225
  96.3 2.0 %collective-permute-start.17 = (bf16[256,512]{1,0:T(8,128)(2,1)S(1)}, bf16[256,512]{1,0:T(8,128)(2,1)S(1)}, u32[]{:S(2)}, u32[]{:S(2)}) collective-permute-start(bf16[256,512]{1,0:T(8,128)(2,1)S(1)} %collective-permute-done.15.refs_5_), channel_id=1, source_target_pairs={{0,8},{8,0},{16,24},{24,16},{1,9},{9,1},{17,25},{25,17},{2,10},{10... | collective-permute-start | bytes 786440 | tf_op jit(solution)/shard_map/ppermute | solution.py:225
  97.2 9.2 %collective-permute-start.25 = (bf16[256,512]{1,0:T(8,128)(2,1)S(1)}, bf16[256,512]{1,0:T(8,128)(2,1)S(1)}, u32[]{:S(2)}, u32[]{:S(2)}) collective-permute-start(bf16[256,512]{1,0:T(8,128)(2,1)S(1)} %get-tuple-element.57), channel_id=1, source_target_pairs={{0,1},{1,0},{2,3},{3,2},{4,5},{5,4},{6,7},{7,6},{8,9},{9,8},{10,11... | collective-permute-start | bytes 786440 | tf_op jit(solution)/shard_map/ppermute | solution.py:225
  99.2 18.0 %collective-permute-start.18 = (bf16[256,512]{1,0:T(8,128)(2,1)S(1)}, bf16[256,512]{1,0:T(8,128)(2,1)S(1)}, u32[]{:S(2)}, u32[]{:S(2)}) collective-permute-start(bf16[256,512]{1,0:T(8,128)(2,1)S(1)} %get-tuple-element.52), channel_id=1, source_target_pairs={{0,1},{1,0},{2,3},{3,2},{4,5},{5,4},{6,7},{7,6},{8,9},{9,8},{10,11... | collective-permute-start | bytes 786440 | tf_op jit(solution)/shard_map/ppermute | solution.py:225
  100.2 9.2 %collective-permute-start.26 = (bf16[256,512]{1,0:T(8,128)(2,1)S(1)}, bf16[256,512]{1,0:T(8,128)(2,1)S(1)}, u32[]{:S(2)}, u32[]{:S(2)}) collective-permute-start(bf16[256,512]{1,0:T(8,128)(2,1)S(1)} %get-tuple-element.58), channel_id=1, source_target_pairs={{0,2},{1,3},{2,0},{3,1},{4,6},{5,7},{6,4},{7,5},{8,10},{9,11},{10,... | collective-permute-start | bytes 786440 | tf_op jit(solution)/shard_map/ppermute | solution.py:225
  101.2 14.4 %collective-permute-start.27 = (bf16[256,512]{1,0:T(8,128)(2,1)S(1)}, bf16[256,512]{1,0:T(8,128)(2,1)S(1)}, u32[]{:S(2)}, u32[]{:S(2)}) collective-permute-start(bf16[256,512]{1,0:T(8,128)(2,1)S(1)} %get-tuple-element.59), channel_id=1, source_target_pairs={{0,3},{1,2},{2,1},{3,0},{4,7},{5,6},{6,5},{7,4},{8,11},{9,10},{10,... | collective-permute-start | bytes 786440 | tf_op jit(solution)/shard_map/ppermute | solution.py:225
  102.8 17.9 %collective-permute-start.19 = (bf16[256,512]{1,0:T(8,128)(2,1)S(1)}, bf16[256,512]{1,0:T(8,128)(2,1)S(1)}, u32[]{:S(2)}, u32[]{:S(2)}) collective-permute-start(bf16[256,512]{1,0:T(8,128)(2,1)S(1)} %get-tuple-element.53), channel_id=1, source_target_pairs={{0,2},{1,3},{2,0},{3,1},{4,6},{5,7},{6,4},{7,5},{8,10},{9,11},{10,... | collective-permute-start | bytes 786440 | tf_op jit(solution)/shard_map/ppermute | solution.py:225
  106.4 19.3 %collective-permute-start.20 = (bf16[256,512]{1,0:T(8,128)(2,1)S(1)}, bf16[256,512]{1,0:T(8,128)(2,1)S(1)}, u32[]{:S(2)}, u32[]{:S(2)}) collective-permute-start(bf16[256,512]{1,0:T(8,128)(2,1)S(1)} %get-tuple-element.54), channel_id=1, source_target_pairs={{0,3},{1,2},{2,1},{3,0},{4,7},{5,6},{6,5},{7,4},{8,11},{9,10},{10,... | collective-permute-start | bytes 786440 | tf_op jit(solution)/shard_map/ppermute | solution.py:225

commit v3 on v2

--- a/solution.py
+++ b/solution.py
@@ -11,6 +11,7 @@
 
 ITERS = 5
 PACK = 4
+STRIP = 8
 CHUNKS = 2
 
 
@@ -40,6 +41,10 @@
         parts.append(high)
         value = value - high.astype(jnp.float32)
     return parts + [value.astype(jnp.bfloat16)]
+
+
+def square_indices(size):
+    return [lax.broadcasted_iota(jnp.int32, (size, size), axis) for axis in range(2)]
 
 
 def split_product(left, right, turned=False):
@@ -55,6 +60,14 @@
             )
             total = term if total is None else total + term
     return total
+
+
+def even_product(left, right):
+    half = left[0].shape[0] // 2
+    top = split_product([part[:half] for part in left], right)
+    low = split_product([part[half:] for part in left], [part[:, half:] for part in right])
+    bottom = jnp.concatenate([top[:, half:].T, low], axis=1)
+    return jnp.concatenate([top, bottom], axis=0)
 
 
 def deal_kernel(share_count, owned, gradient, *refs):
@@ -103,6 +116,7 @@
         p_ref[rows, :] = grad + momentum_decay * moment
     parts = parts_of(p_ref[...], 3)
     step = p_ref.shape[0] // PACK
+    row, col = square_indices(step)
 
     def band(i):
         low = i * step
@@ -111,16 +125,22 @@
         )
 
     for ref, first, second in ((a_ref, 0, 3), (b_ref, 1, 2)):
-        width = (PACK - first) * step
-        ref[:, :width] = band(first)
-        ref[:, width:] = band(second)
+        one, two = band(first), band(second)
+        ref[:step, :step] = jnp.where(row <= col, one[:, :step], two[:, :step])
+        middle = (PACK - first) * step
+        ref[:step, step:middle] = one[:, step:]
+        if second < PACK - 1:
+            ref[:step, middle:] = two[:, step:]
+        ref[step:, :] = jnp.zeros((STRIP, ref.shape[1]), jnp.float32)
+        diagonal = jnp.sum(jnp.where(row == col, two[:, :step], 0.0), axis=0, keepdims=True)
+        ref[step:, :step] = jnp.broadcast_to(diagonal, (STRIP, step))
 
 
 def gram_halves(momentum, blocks):
     rows, cols = momentum.shape
     vmem = pl.BlockSpec(memory_space=pltpu.VMEM)
     f32 = jax.ShapeDtypeStruct((rows, cols), jnp.float32)
-    half = jax.ShapeDtypeStruct((rows // PACK, rows // PACK * (PACK + 1)), jnp.float32)
+    half = jax.ShapeDtypeStruct((rows // PACK + STRIP, rows), jnp.float32)
     return pl.pallas_call(
         gram_kernel,
         out_shape=[f32, f32, half, half],
@@ -148,30 +168,38 @@
     rows = gram.shape[0]
     step = rows // PACK
     halves = [a0[...] + a1[...], b0[...] + b1[...]]
-    bands = [
-        halves[0][:, : 4 * step],
-        halves[1][:, : 3 * step],
-        halves[1][:, 3 * step :],
-        halves[0][:, 4 * step :],
-    ]
-    eye = lax.broadcasted_iota(jnp.int32, (step, step), 0) == lax.broadcasted_iota(
-        jnp.int32, (step, step), 1
-    )
-    diag = sum(jnp.where(eye, band[:, :step], 0.0) for band in bands)
-    norm_sq = jnp.sum(jnp.sum(diag, axis=1, keepdims=True), axis=0, keepdims=True)
+    row, col = square_indices(step)
+    diagonals, norm_sq = [None] * PACK, 0.0
+    for half, first, second in zip(halves, (0, 1), (3, 2)):
+        block = half[:step, :step]
+        upper, lower = jnp.where(row < col, block, 0.0), jnp.where(row > col, block, 0.0)
+        one = jnp.where(row == col, block, 0.0)
+        two = jnp.where(row == col, half[step : step + 1, :step], 0.0)
+        both = jnp.sum(one + two, axis=1, keepdims=True)
+        norm_sq = norm_sq + jnp.sum(both, axis=0, keepdims=True)
+        diagonals[first] = upper + upper.T + one
+        diagonals[second] = lower + lower.T + two
     factor = 1.0 / (jnp.sqrt(norm_sq) + norm_epsilon)
     square = factor * factor
+    middle = [(PACK - i) * step for i in range(PACK)]
+    bands = [
+        halves[0][:step, step : middle[0]],
+        halves[1][:step, step : middle[1]],
+        halves[1][:step, middle[1] :],
+    ]
+    for i, diagonal in enumerate(diagonals):
+        gram[i * step : (i + 1) * step, i * step : (i + 1) * step] = diagonal * square
     for i, band in enumerate(bands):
         scaled = band * square
-        gram[i * step : (i + 1) * step, i * step :] = scaled
+        gram[i * step : (i + 1) * step, (i + 1) * step :] = scaled
         for j in range(i + 1, PACK):
             gram[j * step : (j + 1) * step, i * step : (i + 1) * step] = scaled[
-                :, (j - i) * step : (j - i + 1) * step
+                :, (j - i - 1) * step : (j - i) * step
             ].T
     cur[...] = p_ref[...] * factor
 
     def mixed_of(a, a_parts):
-        return second_coeff * a + third_coeff * split_product(a_parts[:2], a_parts[:2])
+        return second_coeff * a + third_coeff * even_product(a_parts[:2], a_parts[:2])
 
     def apply(mixed_parts):
         x = cur[...]
@@ -181,8 +209,10 @@
         a = gram[...]
         a_parts = parts_of(a, count)
         mixed_parts = parts_of(mixed_of(a, a_parts if count == 2 else parts_of(a, 2)), count)
-        half_way = first_coeff * a + split_product(mixed_parts, a_parts)
-        gram[...] = first_coeff * half_way + split_product(parts_of(half_way, count), mixed_parts)
+        half_way = first_coeff * a + even_product(mixed_parts, a_parts)
+        gram[...] = first_coeff * half_way + even_product(
+            parts_of(half_way, count), mixed_parts
+        )
         cur[...] = apply(mixed_parts)
 
     advance(3)

time: 127 us -> 125 us (0.984)
  Pallas kernels: 26.2 us -> 24.7 us
    pallas_call x1, Pallas kernels: 19 us -> 17.4 us  [newton(): pl.pallas_call(functools.partial(newton_kernel, iters, scale), out_shape=...]
  transfers between devices with their start and end apart: 28 -> 28, of which waited for: 17 -> 16; matrix products, arithmetic and copies ran while one was open for 2% -> 2% of each run, Pallas kernels for 2% -> 2%
where the time goes in v3:
time: 125 us
  waiting for transfers between devices  65.9 us (53%)
  starting transfers between devices  27.7 us (22%)
  Pallas kernels  24.7 us (20%)
  local copies, waits for them, and re-layouts  3.22 us (3%)
  other arithmetic  2.46 us (2%)
    ppermute x24, waiting for transfers between devices, flipped(): lax.ppermute(block, axis, [(i, i ^ flip) for i in range(lax.axis_size(axi...  54 us
    ppermute x24, starting transfers between devices, flipped(): lax.ppermute(block, axis, [(i, i ^ flip) for i in range(lax.axis_size(axi...  24.1 us
    pallas_call x1, Pallas kernels, newton(): pl.pallas_call(functools.partial(newton_kernel, iters, scale), out_shape=...  17.4 us
    ppermute x4, waiting for transfers between devices, from_partner(): return lax.ppermute(block, axis, route)  11.9 us
    ppermute x4, starting transfers between devices, from_partner(): return lax.ppermute(block, axis, route)  3.59 us
    unnamed x7, local copies, waits for them, and re-layouts  3.04 us
    pallas_call x1, Pallas kernels, gram_halves(): pl.pallas_call(gram_kernel, out_shape=[f32, f32, half, half], in_specs=[v...  2.74 us
  transfers between devices with their start and end apart: 28, of which 16 were waited for; matrix products, arithmetic and copies ran while one was open for 2% of the time, Pallas kernels for 2%

profile of v3, /device:TPU:0, one launch (start us, length us, event | category | flops | bytes accessed | tf_op | source)
XLA Modules:
  0.0 124.9 jit_solution(13055192735979223383)
XLA Ops:
  1.4 1.0 copy-done
  3.3 3.1 %collective-permute-start = (bf16[64,512]{1,0:T(8,128)(2,1)S(1)}, bf16[64,512]{1,0:T(8,128)(2,1)S(1)}, u32[]{:S(2)}, u32[]{:S(2)}) collective-permute-start(bf16[64,512]{1,0:T(8,128)(2,1)S(1)} %get-tuple-element.33), channel_id=1, source_target_pairs={{0,1},{1,0},{2,3},{3,2},{4,5},{5,4},{6,7},{7,6},{8,9},{9,8},{10,11... | collective-permute-start | bytes 196616 | tf_op jit(solution)/shard_map/ppermute | solution.py:255
  6.3 1.6 %collective-permute-start.1 = (bf16[64,512]{1,0:T(8,128)(2,1)S(1)}, bf16[64,512]{1,0:T(8,128)(2,1)S(1)}, u32[]{:S(2)}, u32[]{:S(2)}) collective-permute-start(bf16[64,512]{1,0:T(8,128)(2,1)S(1)} %get-tuple-element.34), channel_id=1, source_target_pairs={{0,2},{1,3},{2,0},{3,1},{4,6},{5,7},{6,4},{7,5},{8,10},{9,11},{10,... | collective-permute-start | bytes 196616 | tf_op jit(solution)/shard_map/ppermute | solution.py:255
  7.9 3.0 %collective-permute-start.3 = (bf16[64,512]{1,0:T(8,128)(2,1)S(1)}, bf16[64,512]{1,0:T(8,128)(2,1)S(1)}, u32[]{:S(2)}, u32[]{:S(2)}) collective-permute-start(bf16[64,512]{1,0:T(8,128)(2,1)S(1)} %get-tuple-element.36), channel_id=1, source_target_pairs={{0,4},{1,5},{2,6},{3,7},{4,0},{5,1},{6,2},{7,3},{8,12},{9,13},{10,... | collective-permute-start | bytes 196616 | tf_op jit(solution)/shard_map/ppermute | solution.py:255
  10.9 1.3 %collective-permute-start.4 = (bf16[64,512]{1,0:T(8,128)(2,1)S(1)}, bf16[64,512]{1,0:T(8,128)(2,1)S(1)}, u32[]{:S(2)}, u32[]{:S(2)}) collective-permute-start(bf16[64,512]{1,0:T(8,128)(2,1)S(1)} %get-tuple-element.37), channel_id=1, source_target_pairs={{0,5},{1,4},{2,7},{3,6},{4,1},{5,0},{6,3},{7,2},{8,13},{9,12},{10,... | collective-permute-start | bytes 196616 | tf_op jit(solution)/shard_map/ppermute | solution.py:255
  14.6 3.7 %collective-permute-start.5 = (bf16[64,512]{1,0:T(8,128)(2,1)S(1)}, bf16[64,512]{1,0:T(8,128)(2,1)S(1)}, u32[]{:S(2)}, u32[]{:S(2)}) collective-permute-start(bf16[64,512]{1,0:T(8,128)(2,1)S(1)} %get-tuple-element.38), channel_id=1, source_target_pairs={{0,6},{1,7},{2,4},{3,5},{4,2},{5,3},{6,0},{7,1},{8,14},{9,15},{10,... | collective-permute-start | bytes 196616 | tf_op jit(solution)/shard_map/ppermute | solution.py:255
  18.5 1.2 collective-permute-done.4.refs_5_
  19.7 1.1 collective-permute-done.5.refs_6_
  20.8 4.4 %collective-permute-done.6.refs_7_ = bf16[64,512]{1,0:T(8,128)(2,1)S(1)} collective-permute-done((bf16[64,512]{1,0:T(8,128)(2,1)S(1)}, bf16[64,512]{1,0:T(8,128)(2,1)S(1)}, u32[]{:S(2)}, u32[]{:S(2)}) %collective-permute-start.6) | collective-permute-done | bytes 65568 | tf_op jit(solution)/shard_map/ppermute | solution.py:255
  25.2 1.2 copy-done.1
  26.5 2.7 %shard_map.85 = (f32[512,512]{1,0:T(8,128)}, f32[512,512]{1,0:T(8,128)S(1)}, f32[136,512]{1,0:T(8,128)S(1)}, f32[136,512]{1,0:T(8,128)S(1)}) custom-call(f32[512,512]{1,0:T(8,128)S(1)} %bitcast.13, bf16[64,512]{1,0:T(8,128)(2,1)S(1)} %get-tuple-element.32.refs_0_, bf16[64,512]{1,0:T(8,128)(2,1)S(1)} %collective-permute-done.refs_1_, ...), custom_call_target="tpu_custom_call" | custom-call | flops 1073741824 | bytes 4194304 | tf_op jit(solution)/shard_map/pallas_call | solution.py:144
  29.8 6.0 %collective-permute-done.7 = f32[136,512]{1,0:T(8,128)S(1)} collective-permute-done((f32[136,512]{1,0:T(8,128)S(1)}, f32[136,512]{1,0:T(8,128)S(1)}, u32[]{:S(2)}, u32[]{:S(2)}) %collective-permute-start.7) | collective-permute-done | bytes 278560 | tf_op jit(solution)/shard_map/ppermute | solution.py:34
  36.0 1.4 %collective-permute-done.9 = f32[136,512]{1,0:T(8,128)S(1)} collective-permute-done((f32[136,512]{1,0:T(8,128)S(1)}, f32[136,512]{1,0:T(8,128)S(1)}, u32[]{:S(2)}, u32[]{:S(2)}) %collective-permute-start.9) | collective-permute-done | bytes 278560 | tf_op jit(solution)/shard_map/ppermute | solution.py:34
  37.4 2.9 %collective-permute-start.10 = (f32[136,512]{1,0:T(8,128)S(1)}, f32[136,512]{1,0:T(8,128)S(1)}, u32[]{:S(2)}, u32[]{:S(2)}) collective-permute-start(f32[136,512]{1,0:T(8,128)S(1)} %add.15.b0), channel_id=1, source_target_pairs={{0,1},{1,0},{2,3},{3,2},{4,5},{5,4},{6,7},{7,6},{8,9},{9,8},{10,11... | collective-permute-start | bytes 835592 | tf_op jit(solution)/shard_map/ppermute | solution.py:34
  40.3 2.2 %collective-permute-done.8.a1 = f32[136,512]{1,0:T(8,128)S(1)} collective-permute-done((f32[136,512]{1,0:T(8,128)S(1)}, f32[136,512]{1,0:T(8,128)S(1)}, u32[]{:S(2)}, u32[]{:S(2)}) %collective-permute-start.8) | collective-permute-done | bytes 278560 | tf_op jit(solution)/shard_map/ppermute | solution.py:34
  42.5 2.3 %collective-permute-done.10.b1 = f32[136,512]{1,0:T(8,128)S(1)} collective-permute-done((f32[136,512]{1,0:T(8,128)S(1)}, f32[136,512]{1,0:T(8,128)S(1)}, u32[]{:S(2)}, u32[]{:S(2)}) %collective-permute-start.10) | collective-permute-done | bytes 278560 | tf_op jit(solution)/shard_map/ppermute | solution.py:34
  44.8 17.4 %shard_map.86 = (f32[512,512]{1,0:T(8,128)}, f32[512,512]{1,0:T(8,128)}, bf16[512,512]{1,0:T(8,128)(2,1)S(1)}, bf16[256,512]{1,0:T(8,128)(2,1)S(1)}, bf16[256,512]{1,0:T(8,128)(2,1)S(1)}) custom-call(f32[136,512]{1,0:T(8,128)S(1)} %add.14.a0, f32[136,512]{1,0:T(8,128)S(1)} %collective-permute-done.8.a1, f32[136,512]{1,0:T(8,128)S(1)} %add.15.b0, ...), custom_call_target="tpu_custom_call" | custom-call | flops 16106127360 | bytes 6291456 | tf_op jit(solution)/shard_map/pallas_call | solution.py:238
  62.2 1.6 %collective-permute-start.14 = (bf16[512,512]{1,0:T(8,128)(2,1)S(1)}, bf16[512,512]{1,0:T(8,128)(2,1)S(1)}, u32[]{:S(2)}, u32[]{:S(2)}) collective-permute-start(bf16[512,512]{1,0:T(8,128)(2,1)S(1)} %get-tuple-element.49.refs_0_), channel_id=1, source_target_pairs={{0,16},{8,24},{16,0},{24,8},{1,17},{9,25},{17,1},{25,9},{2,18},{10... | collective-permute-start | bytes 1572872 | tf_op jit(solution)/shard_map/ppermute | solution.py:255
  64.3 2.4 %collective-permute-start.11 = (bf16[256,512]{1,0:T(8,128)(2,1)S(1)}, bf16[256,512]{1,0:T(8,128)(2,1)S(1)}, u32[]{:S(2)}, u32[]{:S(2)}) collective-permute-start(bf16[256,512]{1,0:T(8,128)(2,1)S(1)} %get-tuple-element.50), channel_id=1, source_target_pairs={{0,4},{1,5},{2,6},{3,7},{4,0},{5,1},{6,2},{7,3},{8,12},{9,13},{10,... | collective-permute-start | bytes 786440 | tf_op jit(solution)/shard_map/ppermute | solution.py:255
  66.8 14.9 %collective-permute-done.21.refs_1_ = bf16[256,512]{1,0:T(8,128)(2,1)S(1)} collective-permute-done((bf16[256,512]{1,0:T(8,128)(2,1)S(1)}, bf16[256,512]{1,0:T(8,128)(2,1)S(1)}, u32[]{:S(2)}, u32[]{:S(2)}) %collective-permute-start.21) | collective-permute-done | bytes 262176 | tf_op jit(solution)/shard_map/ppermute | solution.py:255
  82.1 3.1 %collective-permute-done.11.refs_1_ = bf16[256,512]{1,0:T(8,128)(2,1)S(1)} collective-permute-done((bf16[256,512]{1,0:T(8,128)(2,1)S(1)}, bf16[256,512]{1,0:T(8,128)(2,1)S(1)}, u32[]{:S(2)}, u32[]{:S(2)}) %collective-permute-start.11) | collective-permute-done | bytes 262176 | tf_op jit(solution)/shard_map/ppermute | solution.py:255
  85.8 4.3 %collective-permute-done.23.refs_5_ = bf16[256,512]{1,0:T(8,128)(2,1)S(1)} collective-permute-done((bf16[256,512]{1,0:T(8,128)(2,1)S(1)}, bf16[256,512]{1,0:T(8,128)(2,1)S(1)}, u32[]{:S(2)}, u32[]{:S(2)}) %collective-permute-start.23) | collective-permute-done | bytes 262176 | tf_op jit(solution)/shard_map/ppermute | solution.py:255
  90.6 3.0 %collective-permute-done.15.refs_5_ = bf16[256,512]{1,0:T(8,128)(2,1)S(1)} collective-permute-done((bf16[256,512]{1,0:T(8,128)(2,1)S(1)}, bf16[256,512]{1,0:T(8,128)(2,1)S(1)}, u32[]{:S(2)}, u32[]{:S(2)}) %collective-permute-start.15) | collective-permute-done | bytes 262176 | tf_op jit(solution)/shard_map/ppermute | solution.py:255
  94.5 1.8 %collective-permute-start.25 = (bf16[256,512]{1,0:T(8,128)(2,1)S(1)}, bf16[256,512]{1,0:T(8,128)(2,1)S(1)}, u32[]{:S(2)}, u32[]{:S(2)}) collective-permute-start(bf16[256,512]{1,0:T(8,128)(2,1)S(1)} %get-tuple-element.57), channel_id=1, source_target_pairs={{0,1},{1,0},{2,3},{3,2},{4,5},{5,4},{6,7},{7,6},{8,9},{9,8},{10,11... | collective-permute-start | bytes 786440 | tf_op jit(solution)/shard_map/ppermute | solution.py:255
  97.8 2.9 %collective-permute-start.27 = (bf16[256,512]{1,0:T(8,128)(2,1)S(1)}, bf16[256,512]{1,0:T(8,128)(2,1)S(1)}, u32[]{:S(2)}, u32[]{:S(2)}) collective-permute-start(bf16[256,512]{1,0:T(8,128)(2,1)S(1)} %get-tuple-element.59), channel_id=1, source_target_pairs={{0,3},{1,2},{2,1},{3,0},{4,7},{5,6},{6,5},{7,4},{8,11},{9,10},{10,... | collective-permute-start | bytes 786440 | tf_op jit(solution)/shard_map/ppermute | solution.py:255
  100.7 3.0 %collective-permute-done.25.refs_1_ = bf16[256,512]{1,0:T(8,128)(2,1)S(1)} collective-permute-done((bf16[256,512]{1,0:T(8,128)(2,1)S(1)}, bf16[256,512]{1,0:T(8,128)(2,1)S(1)}, u32[]{:S(2)}, u32[]{:S(2)}) %collective-permute-start.25) | collective-permute-done | bytes 262176 | tf_op jit(solution)/shard_map/ppermute | solution.py:255
  103.7 3.3 %collective-permute-done.26.refs_2_ = bf16[256,512]{1,0:T(8,128)(2,1)S(1)} collective-permute-done((bf16[256,512]{1,0:T(8,128)(2,1)S(1)}, bf16[256,512]{1,0:T(8,128)(2,1)S(1)}, u32[]{:S(2)}, u32[]{:S(2)}) %collective-permute-start.26) | collective-permute-done | bytes 262176 | tf_op jit(solution)/shard_map/ppermute | solution.py:255
  107.0 6.5 %collective-permute-done.27.refs_3_ = bf16[256,512]{1,0:T(8,128)(2,1)S(1)} collective-permute-done((bf16[256,512]{1,0:T(8,128)(2,1)S(1)}, bf16[256,512]{1,0:T(8,128)(2,1)S(1)}, u32[]{:S(2)}, u32[]{:S(2)}) %collective-permute-start.27) | collective-permute-done | bytes 262176 | tf_op jit(solution)/shard_map/ppermute | solution.py:255
  113.5 1.0 shard_map.89.refs_4_
  114.5 3.7 %collective-permute-done.19.refs_2_ = bf16[256,512]{1,0:T(8,128)(2,1)S(1)} collective-permute-done((bf16[256,512]{1,0:T(8,128)(2,1)S(1)}, bf16[256,512]{1,0:T(8,128)(2,1)S(1)}, u32[]{:S(2)}, u32[]{:S(2)}) %collective-permute-start.19) | collective-permute-done | bytes 262176 | tf_op jit(solution)/shard_map/ppermute | solution.py:255
  118.3 5.4 %collective-permute-done.20.refs_3_ = bf16[256,512]{1,0:T(8,128)(2,1)S(1)} collective-permute-done((bf16[256,512]{1,0:T(8,128)(2,1)S(1)}, bf16[256,512]{1,0:T(8,128)(2,1)S(1)}, u32[]{:S(2)}, u32[]{:S(2)}) %collective-permute-start.20) | collective-permute-done | bytes 262176 | tf_op jit(solution)/shard_map/ppermute | solution.py:255
  123.7 1.0 shard_map.90
  (47 shorter events, 9.4 us)
Async XLA Ops:
  1.4 1.0 copy-start
  3.3 11.3 %collective-permute-start = (bf16[64,512]{1,0:T(8,128)(2,1)S(1)}, bf16[64,512]{1,0:T(8,128)(2,1)S(1)}, u32[]{:S(2)}, u32[]{:S(2)}) collective-permute-start(bf16[64,512]{1,0:T(8,128)(2,1)S(1)} %get-tuple-element.33), channel_id=1, source_target_pairs={{0,1},{1,0},{2,3},{3,2},{4,5},{5,4},{6,7},{7,6},{8,9},{9,8},{10,11... | collective-permute-start | bytes 196616 | tf_op jit(solution)/shard_map/ppermute | solution.py:255
  6.3 11.9 %collective-permute-start.1 = (bf16[64,512]{1,0:T(8,128)(2,1)S(1)}, bf16[64,512]{1,0:T(8,128)(2,1)S(1)}, u32[]{:S(2)}, u32[]{:S(2)}) collective-permute-start(bf16[64,512]{1,0:T(8,128)(2,1)S(1)} %get-tuple-element.34), channel_id=1, source_target_pairs={{0,2},{1,3},{2,0},{3,1},{4,6},{5,7},{6,4},{7,5},{8,10},{9,11},{10,... | collective-permute-start | bytes 196616 | tf_op jit(solution)/shard_map/ppermute | solution.py:255
  7.9 10.6 %collective-permute-start.2 = (bf16[64,512]{1,0:T(8,128)(2,1)S(1)}, bf16[64,512]{1,0:T(8,128)(2,1)S(1)}, u32[]{:S(2)}, u32[]{:S(2)}) collective-permute-start(bf16[64,512]{1,0:T(8,128)(2,1)S(1)} %get-tuple-element.35), channel_id=1, source_target_pairs={{0,3},{1,2},{2,1},{3,0},{4,7},{5,6},{6,5},{7,4},{8,11},{9,10},{10,... | collective-permute-start | bytes 196616 | tf_op jit(solution)/shard_map/ppermute | solution.py:255
  7.9 10.6 %collective-permute-start.3 = (bf16[64,512]{1,0:T(8,128)(2,1)S(1)}, bf16[64,512]{1,0:T(8,128)(2,1)S(1)}, u32[]{:S(2)}, u32[]{:S(2)}) collective-permute-start(bf16[64,512]{1,0:T(8,128)(2,1)S(1)} %get-tuple-element.36), channel_id=1, source_target_pairs={{0,4},{1,5},{2,6},{3,7},{4,0},{5,1},{6,2},{7,3},{8,12},{9,13},{10,... | collective-permute-start | bytes 196616 | tf_op jit(solution)/shard_map/ppermute | solution.py:255
  10.9 8.8 %collective-permute-start.4 = (bf16[64,512]{1,0:T(8,128)(2,1)S(1)}, bf16[64,512]{1,0:T(8,128)(2,1)S(1)}, u32[]{:S(2)}, u32[]{:S(2)}) collective-permute-start(bf16[64,512]{1,0:T(8,128)(2,1)S(1)} %get-tuple-element.37), channel_id=1, source_target_pairs={{0,5},{1,4},{2,7},{3,6},{4,1},{5,0},{6,3},{7,2},{8,13},{9,12},{10,... | collective-permute-start | bytes 196616 | tf_op jit(solution)/shard_map/ppermute | solution.py:255
  14.6 6.2 %collective-permute-start.5 = (bf16[64,512]{1,0:T(8,128)(2,1)S(1)}, bf16[64,512]{1,0:T(8,128)(2,1)S(1)}, u32[]{:S(2)}, u32[]{:S(2)}) collective-permute-start(bf16[64,512]{1,0:T(8,128)(2,1)S(1)} %get-tuple-element.38), channel_id=1, source_target_pairs={{0,6},{1,7},{2,4},{3,5},{4,2},{5,3},{6,0},{7,1},{8,14},{9,15},{10,... | collective-permute-start | bytes 196616 | tf_op jit(solution)/shard_map/ppermute | solution.py:255
  18.3 7.0 %collective-permute-start.6 = (bf16[64,512]{1,0:T(8,128)(2,1)S(1)}, bf16[64,512]{1,0:T(8,128)(2,1)S(1)}, u32[]{:S(2)}, u32[]{:S(2)}) collective-permute-start(bf16[64,512]{1,0:T(8,128)(2,1)S(1)} %get-tuple-element.39), channel_id=1, source_target_pairs={{0,7},{1,6},{2,5},{3,4},{4,3},{5,2},{6,1},{7,0},{8,15},{9,14},{10,... | collective-permute-start | bytes 196616 | tf_op jit(solution)/shard_map/ppermute | solution.py:255
  25.2 1.2 copy-start.1
  26.5 18.3 %copy-start.2 = (f32[1,512,512]{2,1,0:T(8,128)S(1)}, f32[1,512,512]{2,1,0:T(8,128)}, u32[]{:S(2)}) copy-start(f32[1,512,512]{2,1,0:T(8,128)} %param.7) | copy-start | bytes 3145732
  29.2 6.6 %collective-permute-start.7 = (f32[136,512]{1,0:T(8,128)S(1)}, f32[136,512]{1,0:T(8,128)S(1)}, u32[]{:S(2)}, u32[]{:S(2)}) collective-permute-start(f32[136,512]{1,0:T(8,128)S(1)} %get-tuple-element.43), channel_id=1, source_target_pairs={{0,1},{1,0},{2,3},{3,2},{4,5},{5,4},{6,7},{7,6},{8,9},{9,8},{10,11... | collective-permute-start | bytes 835592 | tf_op jit(solution)/shard_map/ppermute | solution.py:34
  29.8 7.5 %collective-permute-start.9 = (f32[136,512]{1,0:T(8,128)S(1)}, f32[136,512]{1,0:T(8,128)S(1)}, u32[]{:S(2)}, u32[]{:S(2)}) collective-permute-start(f32[136,512]{1,0:T(8,128)S(1)} %get-tuple-element.44), channel_id=1, source_target_pairs={{0,2},{2,0},{1,3},{3,1},{4,6},{6,4},{5,7},{7,5},{8,10},{10,8},{9,1... | collective-permute-start | bytes 835592 | tf_op jit(solution)/shard_map/ppermute | solution.py:34
  35.9 6.6 %collective-permute-start.8 = (f32[136,512]{1,0:T(8,128)S(1)}, f32[136,512]{1,0:T(8,128)S(1)}, u32[]{:S(2)}, u32[]{:S(2)}) collective-permute-start(f32[136,512]{1,0:T(8,128)S(1)} %add.14.a0), channel_id=1, source_target_pairs={{0,2},{2,0},{1,3},{3,1},{4,6},{6,4},{5,7},{7,5},{8,10},{10,8},{9,1... | collective-permute-start | bytes 835592 | tf_op jit(solution)/shard_map/ppermute | solution.py:34
  37.4 7.4 %collective-permute-start.10 = (f32[136,512]{1,0:T(8,128)S(1)}, f32[136,512]{1,0:T(8,128)S(1)}, u32[]{:S(2)}, u32[]{:S(2)}) collective-permute-start(f32[136,512]{1,0:T(8,128)S(1)} %add.15.b0), channel_id=1, source_target_pairs={{0,1},{1,0},{2,3},{3,2},{4,5},{5,4},{6,7},{7,6},{8,9},{9,8},{10,11... | collective-permute-start | bytes 835592 | tf_op jit(solution)/shard_map/ppermute | solution.py:34
  62.2 19.9 %collective-permute-start.14 = (bf16[512,512]{1,0:T(8,128)(2,1)S(1)}, bf16[512,512]{1,0:T(8,128)(2,1)S(1)}, u32[]{:S(2)}, u32[]{:S(2)}) collective-permute-start(bf16[512,512]{1,0:T(8,128)(2,1)S(1)} %get-tuple-element.49.refs_0_), channel_id=1, source_target_pairs={{0,16},{8,24},{16,0},{24,8},{1,17},{9,25},{17,1},{25,9},{2,18},{10... | collective-permute-start | bytes 1572872 | tf_op jit(solution)/shard_map/ppermute | solution.py:255
  63.8 17.8 %collective-permute-start.21 = (bf16[256,512]{1,0:T(8,128)(2,1)S(1)}, bf16[256,512]{1,0:T(8,128)(2,1)S(1)}, u32[]{:S(2)}, u32[]{:S(2)}) collective-permute-start(bf16[256,512]{1,0:T(8,128)(2,1)S(1)} %get-tuple-element.55), channel_id=1, source_target_pairs={{0,4},{1,5},{2,6},{3,7},{4,0},{5,1},{6,2},{7,3},{8,12},{9,13},{10,... | collective-permute-start | bytes 786440 | tf_op jit(solution)/shard_map/ppermute | solution.py:255
  64.3 25.8 %collective-permute-start.12 = (bf16[512,512]{1,0:T(8,128)(2,1)S(1)}, bf16[512,512]{1,0:T(8,128)(2,1)S(1)}, u32[]{:S(2)}, u32[]{:S(2)}) collective-permute-start(bf16[512,512]{1,0:T(8,128)(2,1)S(1)} %get-tuple-element.49.refs_0_), channel_id=1, source_target_pairs={{0,8},{8,0},{16,24},{24,16},{1,9},{9,1},{17,25},{25,17},{2,10},{10... | collective-permute-start | bytes 1572872 | tf_op jit(solution)/shard_map/ppermute | solution.py:255
  64.3 20.9 %collective-permute-start.11 = (bf16[256,512]{1,0:T(8,128)(2,1)S(1)}, bf16[256,512]{1,0:T(8,128)(2,1)S(1)}, u32[]{:S(2)}, u32[]{:S(2)}) collective-permute-start(bf16[256,512]{1,0:T(8,128)(2,1)S(1)} %get-tuple-element.50), channel_id=1, source_target_pairs={{0,4},{1,5},{2,6},{3,7},{4,0},{5,1},{6,2},{7,3},{8,12},{9,13},{10,... | collective-permute-start | bytes 786440 | tf_op jit(solution)/shard_map/ppermute | solution.py:255
  81.6 8.5 %collective-permute-start.23 = (bf16[256,512]{1,0:T(8,128)(2,1)S(1)}, bf16[256,512]{1,0:T(8,128)(2,1)S(1)}, u32[]{:S(2)}, u32[]{:S(2)}) collective-permute-start(bf16[256,512]{1,0:T(8,128)(2,1)S(1)} %collective-permute-done.21.refs_1_), channel_id=1, source_target_pairs={{0,16},{8,24},{16,0},{24,8},{1,17},{9,25},{17,1},{25,9},{2,18},{10... | collective-permute-start | bytes 786440 | tf_op jit(solution)/shard_map/ppermute | solution.py:255
  82.1 11.5 %collective-permute-start.16 = (bf16[512,512]{1,0:T(8,128)(2,1)S(1)}, bf16[512,512]{1,0:T(8,128)(2,1)S(1)}, u32[]{:S(2)}, u32[]{:S(2)}) collective-permute-start(bf16[512,512]{1,0:T(8,128)(2,1)S(1)} %collective-permute-done.14.refs_4_), channel_id=1, source_target_pairs={{0,8},{8,0},{16,24},{24,16},{1,9},{9,1},{17,25},{25,17},{2,10},{10... | collective-permute-start | bytes 1572872 | tf_op jit(solution)/shard_map/ppermute | solution.py:255
  85.2 8.4 %collective-permute-start.15 = (bf16[256,512]{1,0:T(8,128)(2,1)S(1)}, bf16[256,512]{1,0:T(8,128)(2,1)S(1)}, u32[]{:S(2)}, u32[]{:S(2)}) collective-permute-start(bf16[256,512]{1,0:T(8,128)(2,1)S(1)} %collective-permute-done.11.refs_1_), channel_id=1, source_target_pairs={{0,16},{8,24},{16,0},{24,8},{1,17},{9,25},{17,1},{25,9},{2,18},{10... | collective-permute-start | bytes 786440 | tf_op jit(solution)/shard_map/ppermute | solution.py:255
  85.8 7.8 %collective-permute-start.22 = (bf16[256,512]{1,0:T(8,128)(2,1)S(1)}, bf16[256,512]{1,0:T(8,128)(2,1)S(1)}, u32[]{:S(2)}, u32[]{:S(2)}) collective-permute-start(bf16[256,512]{1,0:T(8,128)(2,1)S(1)} %collective-permute-done.21.refs_1_), channel_id=1, source_target_pairs={{0,8},{8,0},{16,24},{24,16},{1,9},{9,1},{17,25},{25,17},{2,10},{10... | collective-permute-start | bytes 786440 | tf_op jit(solution)/shard_map/ppermute | solution.py:255
  90.1 3.5 %collective-permute-start.24 = (bf16[256,512]{1,0:T(8,128)(2,1)S(1)}, bf16[256,512]{1,0:T(8,128)(2,1)S(1)}, u32[]{:S(2)}, u32[]{:S(2)}) collective-permute-start(bf16[256,512]{1,0:T(8,128)(2,1)S(1)} %collective-permute-done.23.refs_5_), channel_id=1, source_target_pairs={{0,8},{8,0},{16,24},{24,16},{1,9},{9,1},{17,25},{25,17},{2,10},{10... | collective-permute-start | bytes 786440 | tf_op jit(solution)/shard_map/ppermute | solution.py:255
  90.1 6.2 %collective-permute-start.13 = (bf16[256,512]{1,0:T(8,128)(2,1)S(1)}, bf16[256,512]{1,0:T(8,128)(2,1)S(1)}, u32[]{:S(2)}, u32[]{:S(2)}) collective-permute-start(bf16[256,512]{1,0:T(8,128)(2,1)S(1)} %collective-permute-done.11.refs_1_), channel_id=1, source_target_pairs={{0,8},{8,0},{16,24},{24,16},{1,9},{9,1},{17,25},{25,17},{2,10},{10... | collective-permute-start | bytes 786440 | tf_op jit(solution)/shard_map/ppermute | solution.py:255
  93.6 2.7 %collective-permute-start.17 = (bf16[256,512]{1,0:T(8,128)(2,1)S(1)}, bf16[256,512]{1,0:T(8,128)(2,1)S(1)}, u32[]{:S(2)}, u32[]{:S(2)}) collective-permute-start(bf16[256,512]{1,0:T(8,128)(2,1)S(1)} %collective-permute-done.15.refs_5_), channel_id=1, source_target_pairs={{0,8},{8,0},{16,24},{24,16},{1,9},{9,1},{17,25},{25,17},{2,10},{10... | collective-permute-start | bytes 786440 | tf_op jit(solution)/shard_map/ppermute | solution.py:255
  94.5 9.2 %collective-permute-start.25 = (bf16[256,512]{1,0:T(8,128)(2,1)S(1)}, bf16[256,512]{1,0:T(8,128)(2,1)S(1)}, u32[]{:S(2)}, u32[]{:S(2)}) collective-permute-start(bf16[256,512]{1,0:T(8,128)(2,1)S(1)} %get-tuple-element.57), channel_id=1, source_target_pairs={{0,1},{1,0},{2,3},{3,2},{4,5},{5,4},{6,7},{7,6},{8,9},{9,8},{10,11... | collective-permute-start | bytes 786440 | tf_op jit(solution)/shard_map/ppermute | solution.py:255
  97.2 17.4 %collective-permute-start.18 = (bf16[256,512]{1,0:T(8,128)(2,1)S(1)}, bf16[256,512]{1,0:T(8,128)(2,1)S(1)}, u32[]{:S(2)}, u32[]{:S(2)}) collective-permute-start(bf16[256,512]{1,0:T(8,128)(2,1)S(1)} %get-tuple-element.52), channel_id=1, source_target_pairs={{0,1},{1,0},{2,3},{3,2},{4,5},{5,4},{6,7},{7,6},{8,9},{9,8},{10,11... | collective-permute-start | bytes 786440 | tf_op jit(solution)/shard_map/ppermute | solution.py:255
  97.8 9.2 %collective-permute-start.26 = (bf16[256,512]{1,0:T(8,128)(2,1)S(1)}, bf16[256,512]{1,0:T(8,128)(2,1)S(1)}, u32[]{:S(2)}, u32[]{:S(2)}) collective-permute-start(bf16[256,512]{1,0:T(8,128)(2,1)S(1)} %get-tuple-element.58), channel_id=1, source_target_pairs={{0,2},{1,3},{2,0},{3,1},{4,6},{5,7},{6,4},{7,5},{8,10},{9,11},{10,... | collective-permute-start | bytes 786440 | tf_op jit(solution)/shard_map/ppermute | solution.py:255
  97.8 15.7 %collective-permute-start.27 = (bf16[256,512]{1,0:T(8,128)(2,1)S(1)}, bf16[256,512]{1,0:T(8,128)(2,1)S(1)}, u32[]{:S(2)}, u32[]{:S(2)}) collective-permute-start(bf16[256,512]{1,0:T(8,128)(2,1)S(1)} %get-tuple-element.59), channel_id=1, source_target_pairs={{0,3},{1,2},{2,1},{3,0},{4,7},{5,6},{6,5},{7,4},{8,11},{9,10},{10,... | collective-permute-start | bytes 786440 | tf_op jit(solution)/shard_map/ppermute | solution.py:255
  100.7 17.6 %collective-permute-start.19 = (bf16[256,512]{1,0:T(8,128)(2,1)S(1)}, bf16[256,512]{1,0:T(8,128)(2,1)S(1)}, u32[]{:S(2)}, u32[]{:S(2)}) collective-permute-start(bf16[256,512]{1,0:T(8,128)(2,1)S(1)} %get-tuple-element.53), channel_id=1, source_target_pairs={{0,2},{1,3},{2,0},{3,1},{4,6},{5,7},{6,4},{7,5},{8,10},{9,11},{10,... | collective-permute-start | bytes 786440 | tf_op jit(solution)/shard_map/ppermute | solution.py:255
  103.7 20.0 %collective-permute-start.20 = (bf16[256,512]{1,0:T(8,128)(2,1)S(1)}, bf16[256,512]{1,0:T(8,128)(2,1)S(1)}, u32[]{:S(2)}, u32[]{:S(2)}) collective-permute-start(bf16[256,512]{1,0:T(8,128)(2,1)S(1)} %get-tuple-element.54), channel_id=1, source_target_pairs={{0,3},{1,2},{2,1},{3,0},{4,7},{5,6},{6,5},{7,4},{8,11},{9,10},{10,... | collective-permute-start | bytes 786440 | tf_op jit(solution)/shard_map/ppermute | solution.py:255

commit v4 on v3

--- a/solution.py
+++ b/solution.py
@@ -49,17 +49,14 @@
 
 def split_product(left, right, turned=False):
     count = len(left)
-    total = None
-    for order in range(count - 1, -1, -1):
-        for i in range(order + 1):
-            term = lax.dot_general(
-                left[i],
-                right[order - i],
-                (((1,), (1 if turned else 0,)), ((), ())),
-                preferred_element_type=jnp.float32,
-            )
-            total = term if total is None else total + term
-    return total
+    terms = [(i, order - i) for order in range(count - 1, -1, -1) for i in range(order + 1)]
+    axis = 1 if turned else 0
+    return lax.dot_general(
+        jnp.concatenate([left[i] for i, _ in terms], axis=1),
+        jnp.concatenate([right[j] for _, j in terms], axis=axis),
+        (((1,), (axis,)), ((), ())),
+        preferred_element_type=jnp.float32,
+    )
 
 
 def even_product(left, right):
@@ -163,7 +160,7 @@
     return halves, moved
 
 
-def newton_kernel(iters, scale, a0, a1, b0, b1, p_ref, w_ref, u_ref, n_ref, r_ref, *rest):
+def newton_kernel(iters, scale, a0, a1, b0, b1, p_ref, w_ref, u_ref, r_ref, *rest):
     pieces, (gram, cur) = rest[:-2], rest[-2:]
     rows = gram.shape[0]
     step = rows // PACK
@@ -227,7 +224,6 @@
     for i, piece in enumerate(pieces):
         piece[...] = rounded[i * piece.shape[0] : (i + 1) * piece.shape[0]]
     u_ref[...] = u
-    n_ref[...] = new
 
 
 def newton(halves, moved, nesterov, master, iters, scale, chunks):
@@ -237,9 +233,9 @@
     pieces = [jax.ShapeDtypeStruct((rows // chunks, cols), jnp.bfloat16) for _ in range(chunks)]
     return pl.pallas_call(
         functools.partial(newton_kernel, iters, scale),
-        out_shape=[f32, f32, jax.ShapeDtypeStruct((rows, cols), jnp.bfloat16)] + pieces,
+        out_shape=[f32, jax.ShapeDtypeStruct((rows, cols), jnp.bfloat16)] + pieces,
         in_specs=[vmem] * 6,
-        out_specs=[vmem] * (3 + chunks),
+        out_specs=[vmem] * (2 + chunks),
         scratch_shapes=[
             pltpu.VMEM((rows, rows), jnp.float32),
             pltpu.VMEM((rows, cols), jnp.float32),
@@ -463,9 +459,11 @@
         halves, slots = lax.optimization_barrier((halves, slots))
     halves, moved = gram_sum(halves, share_count)
     scale_factor = 0.2 * math.sqrt(max(row_count, columns))
-    update, new_weight, rounded, *pieces = newton(
+    update, rounded, *pieces = newton(
         halves, moved, nesterov, master_weight[0], ITERS, scale_factor, CHUNKS if two_halves else 0
     )
+    master = master_weight[0]
+    new_weight = master - learn_rate * (update + weight_decay * master)
     if two_halves:
         rollout = sync_two_halves(rounded, pieces, slots, share_count)[None]
     else:

time: 125 us -> 121 us (0.968)
  waiting for transfers between devices: 65.9 us -> 62.4 us
  Pallas kernels: 24.7 us -> 22.9 us
    ppermute x24, waiting for transfers between devices: 54 us -> 50.5 us  [flipped(): lax.ppermute(block, axis, [(i, i ^ flip) for i in range(lax.axis_size(axi...]
    pallas_call x1, Pallas kernels: 17.4 us -> 15.7 us  [newton(): pl.pallas_call(functools.partial(newton_kernel, iters, scale), out_shape=...]
    unnamed x7 -> x9, local copies, waits for them, and re-layouts: 3.04 us -> 3.04 us
  transfers between devices with their start and end apart: 28 -> 28, of which waited for: 16 -> 17; matrix products, arithmetic and copies ran while one was open for 2% -> 3% of each run, Pallas kernels for 2% -> 2%
where the time goes in v4:
time: 121 us
  waiting for transfers between devices  62.4 us (52%)
  starting transfers between devices  27.7 us (23%)
  Pallas kernels  22.9 us (19%)
  other arithmetic  3.68 us (3%)
  local copies, waits for them, and re-layouts  3.22 us (3%)
    ppermute x24, waiting for transfers between devices, flipped(): lax.ppermute(block, axis, [(i, i ^ flip) for i in range(lax.axis_size(axi...  50.5 us
    ppermute x24, starting transfers between devices, flipped(): lax.ppermute(block, axis, [(i, i ^ flip) for i in range(lax.axis_size(axi...  24 us
    pallas_call x1, Pallas kernels, newton(): pl.pallas_call(functools.partial(newton_kernel, iters, scale), out_shape=...  15.7 us
    ppermute x4, waiting for transfers between devices, from_partner(): return lax.ppermute(block, axis, route)  11.8 us
    ppermute x4, starting transfers between devices, from_partner(): return lax.ppermute(block, axis, route)  3.66 us
    unnamed x9, local copies, waits for them, and re-layouts  3.04 us
    pallas_call x1, Pallas kernels, gram_halves(): pl.pallas_call(gram_kernel, out_shape=[f32, f32, half, half], in_specs=[v...  2.71 us
  transfers between devices with their start and end apart: 28, of which 17 were waited for; matrix products, arithmetic and copies ran while one was open for 3% of the time, Pallas kernels for 2%

profile of v4, /device:TPU:0, one launch (start us, length us, event | category | flops | bytes accessed | tf_op | source)
XLA Modules:
  0.0 120.7 jit_solution(9188089074623445842)
XLA Ops:
  1.4 1.0 copy-done.1
  3.3 3.1 %collective-permute-start = (bf16[64,512]{1,0:T(8,128)(2,1)S(1)}, bf16[64,512]{1,0:T(8,128)(2,1)S(1)}, u32[]{:S(2)}, u32[]{:S(2)}) collective-permute-start(bf16[64,512]{1,0:T(8,128)(2,1)S(1)} %get-tuple-element.32), channel_id=1, source_target_pairs={{0,1},{1,0},{2,3},{3,2},{4,5},{5,4},{6,7},{7,6},{8,9},{9,8},{10,11... | collective-permute-start | bytes 196616 | tf_op jit(solution)/shard_map/ppermute | solution.py:251
  6.3 1.6 %collective-permute-start.1 = (bf16[64,512]{1,0:T(8,128)(2,1)S(1)}, bf16[64,512]{1,0:T(8,128)(2,1)S(1)}, u32[]{:S(2)}, u32[]{:S(2)}) collective-permute-start(bf16[64,512]{1,0:T(8,128)(2,1)S(1)} %get-tuple-element.33), channel_id=1, source_target_pairs={{0,2},{1,3},{2,0},{3,1},{4,6},{5,7},{6,4},{7,5},{8,10},{9,11},{10,... | collective-permute-start | bytes 196616 | tf_op jit(solution)/shard_map/ppermute | solution.py:251
  7.9 3.0 %collective-permute-start.3 = (bf16[64,512]{1,0:T(8,128)(2,1)S(1)}, bf16[64,512]{1,0:T(8,128)(2,1)S(1)}, u32[]{:S(2)}, u32[]{:S(2)}) collective-permute-start(bf16[64,512]{1,0:T(8,128)(2,1)S(1)} %get-tuple-element.35), channel_id=1, source_target_pairs={{0,4},{1,5},{2,6},{3,7},{4,0},{5,1},{6,2},{7,3},{8,12},{9,13},{10,... | collective-permute-start | bytes 196616 | tf_op jit(solution)/shard_map/ppermute | solution.py:251
  10.9 1.3 %collective-permute-start.4 = (bf16[64,512]{1,0:T(8,128)(2,1)S(1)}, bf16[64,512]{1,0:T(8,128)(2,1)S(1)}, u32[]{:S(2)}, u32[]{:S(2)}) collective-permute-start(bf16[64,512]{1,0:T(8,128)(2,1)S(1)} %get-tuple-element.36), channel_id=1, source_target_pairs={{0,5},{1,4},{2,7},{3,6},{4,1},{5,0},{6,3},{7,2},{8,13},{9,12},{10,... | collective-permute-start | bytes 196616 | tf_op jit(solution)/shard_map/ppermute | solution.py:251
  14.6 3.7 %collective-permute-start.5 = (bf16[64,512]{1,0:T(8,128)(2,1)S(1)}, bf16[64,512]{1,0:T(8,128)(2,1)S(1)}, u32[]{:S(2)}, u32[]{:S(2)}) collective-permute-start(bf16[64,512]{1,0:T(8,128)(2,1)S(1)} %get-tuple-element.37), channel_id=1, source_target_pairs={{0,6},{1,7},{2,4},{3,5},{4,2},{5,3},{6,0},{7,1},{8,14},{9,15},{10,... | collective-permute-start | bytes 196616 | tf_op jit(solution)/shard_map/ppermute | solution.py:251
  18.5 1.2 %collective-permute-done.4.refs_5_ = bf16[64,512]{1,0:T(8,128)(2,1)S(1)} collective-permute-done((bf16[64,512]{1,0:T(8,128)(2,1)S(1)}, bf16[64,512]{1,0:T(8,128)(2,1)S(1)}, u32[]{:S(2)}, u32[]{:S(2)}) %collective-permute-start.4) | collective-permute-done | bytes 65568 | tf_op jit(solution)/shard_map/ppermute | solution.py:251
  19.7 1.1 collective-permute-done.5.refs_6_
  20.8 4.4 %collective-permute-done.6.refs_7_ = bf16[64,512]{1,0:T(8,128)(2,1)S(1)} collective-permute-done((bf16[64,512]{1,0:T(8,128)(2,1)S(1)}, bf16[64,512]{1,0:T(8,128)(2,1)S(1)}, u32[]{:S(2)}, u32[]{:S(2)}) %collective-permute-start.6) | collective-permute-done | bytes 65568 | tf_op jit(solution)/shard_map/ppermute | solution.py:251
  25.2 1.2 %copy-done.2 = f32[1,512,512]{2,1,0:T(8,128)S(1)} copy-done((f32[1,512,512]{2,1,0:T(8,128)S(1)}, f32[1,512,512]{2,1,0:T(8,128)}, u32[]{:S(2)}) %copy-start.2) | copy-done | bytes 1048600
  26.5 2.7 %shard_map.85 = (f32[512,512]{1,0:T(8,128)}, f32[512,512]{1,0:T(8,128)S(1)}, f32[136,512]{1,0:T(8,128)S(1)}, f32[136,512]{1,0:T(8,128)S(1)}) custom-call(f32[512,512]{1,0:T(8,128)S(1)} %bitcast.16, bf16[64,512]{1,0:T(8,128)(2,1)S(1)} %get-tuple-element.31.refs_0_, bf16[64,512]{1,0:T(8,128)(2,1)S(1)} %collective-permute-done.refs_1_, ...), custom_call_target="tpu_custom_call" | custom-call | flops 1073741824 | bytes 4194304 | tf_op jit(solution)/shard_map/pallas_call | solution.py:141
  29.7 6.0 %collective-permute-done.7 = f32[136,512]{1,0:T(8,128)S(1)} collective-permute-done((f32[136,512]{1,0:T(8,128)S(1)}, f32[136,512]{1,0:T(8,128)S(1)}, u32[]{:S(2)}, u32[]{:S(2)}) %collective-permute-start.7) | collective-permute-done | bytes 278560 | tf_op jit(solution)/shard_map/ppermute | solution.py:34
  35.9 1.3 %collective-permute-done.9 = f32[136,512]{1,0:T(8,128)S(1)} collective-permute-done((f32[136,512]{1,0:T(8,128)S(1)}, f32[136,512]{1,0:T(8,128)S(1)}, u32[]{:S(2)}, u32[]{:S(2)}) %collective-permute-start.9) | collective-permute-done | bytes 278560 | tf_op jit(solution)/shard_map/ppermute | solution.py:34
  37.3 3.0 %collective-permute-start.10 = (f32[136,512]{1,0:T(8,128)S(1)}, f32[136,512]{1,0:T(8,128)S(1)}, u32[]{:S(2)}, u32[]{:S(2)}) collective-permute-start(f32[136,512]{1,0:T(8,128)S(1)} %add.18.b0), channel_id=1, source_target_pairs={{0,1},{1,0},{2,3},{3,2},{4,5},{5,4},{6,7},{7,6},{8,9},{9,8},{10,11... | collective-permute-start | bytes 835592 | tf_op jit(solution)/shard_map/ppermute | solution.py:34
  40.2 2.2 %collective-permute-done.8.a1 = f32[136,512]{1,0:T(8,128)S(1)} collective-permute-done((f32[136,512]{1,0:T(8,128)S(1)}, f32[136,512]{1,0:T(8,128)S(1)}, u32[]{:S(2)}, u32[]{:S(2)}) %collective-permute-start.8) | collective-permute-done | bytes 278560 | tf_op jit(solution)/shard_map/ppermute | solution.py:34
  42.4 2.3 %collective-permute-done.10.b1 = f32[136,512]{1,0:T(8,128)S(1)} collective-permute-done((f32[136,512]{1,0:T(8,128)S(1)}, f32[136,512]{1,0:T(8,128)S(1)}, u32[]{:S(2)}, u32[]{:S(2)}) %collective-permute-start.10) | collective-permute-done | bytes 278560 | tf_op jit(solution)/shard_map/ppermute | solution.py:34
  44.8 15.7 %shard_map.86 = (f32[512,512]{1,0:T(8,128)}, bf16[512,512]{1,0:T(8,128)(2,1)S(1)}, bf16[256,512]{1,0:T(8,128)(2,1)S(1)}, bf16[256,512]{1,0:T(8,128)(2,1)S(1)}) custom-call(f32[136,512]{1,0:T(8,128)S(1)} %add.17.a0, f32[136,512]{1,0:T(8,128)S(1)} %collective-permute-done.8.a1, f32[136,512]{1,0:T(8,128)S(1)} %add.18.b0, ...), custom_call_target="tpu_custom_call" | custom-call | flops 16106127360 | bytes 6291456 | tf_op jit(solution)/shard_map/pallas_call | solution.py:234
  60.5 1.5 %collective-permute-start.14 = (bf16[512,512]{1,0:T(8,128)(2,1)S(1)}, bf16[512,512]{1,0:T(8,128)(2,1)S(1)}, u32[]{:S(2)}, u32[]{:S(2)}) collective-permute-start(bf16[512,512]{1,0:T(8,128)(2,1)S(1)} %get-tuple-element.47.refs_0_), channel_id=1, source_target_pairs={{0,16},{8,24},{16,0},{24,8},{1,17},{9,25},{17,1},{25,9},{2,18},{10... | collective-permute-start | bytes 1572872 | tf_op jit(solution)/shard_map/ppermute | solution.py:251
  62.6 2.3 %collective-permute-start.11 = (bf16[256,512]{1,0:T(8,128)(2,1)S(1)}, bf16[256,512]{1,0:T(8,128)(2,1)S(1)}, u32[]{:S(2)}, u32[]{:S(2)}) collective-permute-start(bf16[256,512]{1,0:T(8,128)(2,1)S(1)} %get-tuple-element.48), channel_id=1, source_target_pairs={{0,4},{1,5},{2,6},{3,7},{4,0},{5,1},{6,2},{7,3},{8,12},{9,13},{10,... | collective-permute-start | bytes 786440 | tf_op jit(solution)/shard_map/ppermute | solution.py:251
  64.9 14.9 %collective-permute-done.21.refs_1_ = bf16[256,512]{1,0:T(8,128)(2,1)S(1)} collective-permute-done((bf16[256,512]{1,0:T(8,128)(2,1)S(1)}, bf16[256,512]{1,0:T(8,128)(2,1)S(1)}, u32[]{:S(2)}, u32[]{:S(2)}) %collective-permute-start.21) | collective-permute-done | bytes 262176 | tf_op jit(solution)/shard_map/ppermute | solution.py:251
  80.4 3.1 %collective-permute-done.11.refs_1_ = bf16[256,512]{1,0:T(8,128)(2,1)S(1)} collective-permute-done((bf16[256,512]{1,0:T(8,128)(2,1)S(1)}, bf16[256,512]{1,0:T(8,128)(2,1)S(1)}, u32[]{:S(2)}, u32[]{:S(2)}) %collective-permute-start.11) | collective-permute-done | bytes 262176 | tf_op jit(solution)/shard_map/ppermute | solution.py:251
  84.1 4.2 %collective-permute-done.23.refs_5_ = bf16[256,512]{1,0:T(8,128)(2,1)S(1)} collective-permute-done((bf16[256,512]{1,0:T(8,128)(2,1)S(1)}, bf16[256,512]{1,0:T(8,128)(2,1)S(1)}, u32[]{:S(2)}, u32[]{:S(2)}) %collective-permute-start.23) | collective-permute-done | bytes 262176 | tf_op jit(solution)/shard_map/ppermute | solution.py:251
  88.8 3.1 %collective-permute-done.15.refs_5_ = bf16[256,512]{1,0:T(8,128)(2,1)S(1)} collective-permute-done((bf16[256,512]{1,0:T(8,128)(2,1)S(1)}, bf16[256,512]{1,0:T(8,128)(2,1)S(1)}, u32[]{:S(2)}, u32[]{:S(2)}) %collective-permute-start.15) | collective-permute-done | bytes 262176 | tf_op jit(solution)/shard_map/ppermute | solution.py:251
  92.7 1.8 %collective-permute-start.25 = (bf16[256,512]{1,0:T(8,128)(2,1)S(1)}, bf16[256,512]{1,0:T(8,128)(2,1)S(1)}, u32[]{:S(2)}, u32[]{:S(2)}) collective-permute-start(bf16[256,512]{1,0:T(8,128)(2,1)S(1)} %get-tuple-element.55), channel_id=1, source_target_pairs={{0,1},{1,0},{2,3},{3,2},{4,5},{5,4},{6,7},{7,6},{8,9},{9,8},{10,11... | collective-permute-start | bytes 786440 | tf_op jit(solution)/shard_map/ppermute | solution.py:251
  94.5 1.7 %collective-permute-start.27 = (bf16[256,512]{1,0:T(8,128)(2,1)S(1)}, bf16[256,512]{1,0:T(8,128)(2,1)S(1)}, u32[]{:S(2)}, u32[]{:S(2)}) collective-permute-start(bf16[256,512]{1,0:T(8,128)(2,1)S(1)} %get-tuple-element.57), channel_id=1, source_target_pairs={{0,3},{1,2},{2,1},{3,0},{4,7},{5,6},{6,5},{7,4},{8,11},{9,10},{10,... | collective-permute-start | bytes 786440 | tf_op jit(solution)/shard_map/ppermute | solution.py:251
  97.1 1.8 %collective-permute-start.18 = (bf16[256,512]{1,0:T(8,128)(2,1)S(1)}, bf16[256,512]{1,0:T(8,128)(2,1)S(1)}, u32[]{:S(2)}, u32[]{:S(2)}) collective-permute-start(bf16[256,512]{1,0:T(8,128)(2,1)S(1)} %get-tuple-element.50), channel_id=1, source_target_pairs={{0,1},{1,0},{2,3},{3,2},{4,5},{5,4},{6,7},{7,6},{8,9},{9,8},{10,11... | collective-permute-start | bytes 786440 | tf_op jit(solution)/shard_map/ppermute | solution.py:251
  98.9 3.0 %collective-permute-done.25.refs_1_ = bf16[256,512]{1,0:T(8,128)(2,1)S(1)} collective-permute-done((bf16[256,512]{1,0:T(8,128)(2,1)S(1)}, bf16[256,512]{1,0:T(8,128)(2,1)S(1)}, u32[]{:S(2)}, u32[]{:S(2)}) %collective-permute-start.25) | collective-permute-done | bytes 262176 | tf_op jit(solution)/shard_map/ppermute | solution.py:251
  102.0 1.2 %subtract_bitcast_fusion = f32[1,512,512]{2,1,0:T(8,128)} fusion(f32[512,512]{1,0:T(8,128)S(1)} %copy-done.3, f32[1,512,512]{2,1,0:T(8,128)S(1)} %copy-done), kind=kLoop, calls=%fused_computation | loop fusion | flops 1048576 | bytes 3145728 | tf_op jit(solution)/shard_map/broadcast_in_dim | solution.py:471
  103.7 5.4 %collective-permute-done.27.refs_3_ = bf16[256,512]{1,0:T(8,128)(2,1)S(1)} collective-permute-done((bf16[256,512]{1,0:T(8,128)(2,1)S(1)}, bf16[256,512]{1,0:T(8,128)(2,1)S(1)}, u32[]{:S(2)}, u32[]{:S(2)}) %collective-permute-start.27) | collective-permute-done | bytes 262176 | tf_op jit(solution)/shard_map/ppermute | solution.py:251
  110.1 2.7 %collective-permute-done.18.refs_1_ = bf16[256,512]{1,0:T(8,128)(2,1)S(1)} collective-permute-done((bf16[256,512]{1,0:T(8,128)(2,1)S(1)}, bf16[256,512]{1,0:T(8,128)(2,1)S(1)}, u32[]{:S(2)}, u32[]{:S(2)}) %collective-permute-start.18) | collective-permute-done | bytes 262176 | tf_op jit(solution)/shard_map/ppermute | solution.py:251
  112.7 2.3 %collective-permute-done.19.refs_2_ = bf16[256,512]{1,0:T(8,128)(2,1)S(1)} collective-permute-done((bf16[256,512]{1,0:T(8,128)(2,1)S(1)}, bf16[256,512]{1,0:T(8,128)(2,1)S(1)}, u32[]{:S(2)}, u32[]{:S(2)}) %collective-permute-start.19) | collective-permute-done | bytes 262176 | tf_op jit(solution)/shard_map/ppermute | solution.py:251
  115.0 4.7 %collective-permute-done.20.refs_3_ = bf16[256,512]{1,0:T(8,128)(2,1)S(1)} collective-permute-done((bf16[256,512]{1,0:T(8,128)(2,1)S(1)}, bf16[256,512]{1,0:T(8,128)(2,1)S(1)}, u32[]{:S(2)}, u32[]{:S(2)}) %collective-permute-start.20) | collective-permute-done | bytes 262176 | tf_op jit(solution)/shard_map/ppermute | solution.py:251
  (50 shorter events, 11.4 us)
Async XLA Ops:
  1.4 1.0 copy-start.1
  3.3 11.3 %collective-permute-start = (bf16[64,512]{1,0:T(8,128)(2,1)S(1)}, bf16[64,512]{1,0:T(8,128)(2,1)S(1)}, u32[]{:S(2)}, u32[]{:S(2)}) collective-permute-start(bf16[64,512]{1,0:T(8,128)(2,1)S(1)} %get-tuple-element.32), channel_id=1, source_target_pairs={{0,1},{1,0},{2,3},{3,2},{4,5},{5,4},{6,7},{7,6},{8,9},{9,8},{10,11... | collective-permute-start | bytes 196616 | tf_op jit(solution)/shard_map/ppermute | solution.py:251
  6.3 11.9 %collective-permute-start.1 = (bf16[64,512]{1,0:T(8,128)(2,1)S(1)}, bf16[64,512]{1,0:T(8,128)(2,1)S(1)}, u32[]{:S(2)}, u32[]{:S(2)}) collective-permute-start(bf16[64,512]{1,0:T(8,128)(2,1)S(1)} %get-tuple-element.33), channel_id=1, source_target_pairs={{0,2},{1,3},{2,0},{3,1},{4,6},{5,7},{6,4},{7,5},{8,10},{9,11},{10,... | collective-permute-start | bytes 196616 | tf_op jit(solution)/shard_map/ppermute | solution.py:251
  7.9 10.6 %collective-permute-start.2 = (bf16[64,512]{1,0:T(8,128)(2,1)S(1)}, bf16[64,512]{1,0:T(8,128)(2,1)S(1)}, u32[]{:S(2)}, u32[]{:S(2)}) collective-permute-start(bf16[64,512]{1,0:T(8,128)(2,1)S(1)} %get-tuple-element.34), channel_id=1, source_target_pairs={{0,3},{1,2},{2,1},{3,0},{4,7},{5,6},{6,5},{7,4},{8,11},{9,10},{10,... | collective-permute-start | bytes 196616 | tf_op jit(solution)/shard_map/ppermute | solution.py:251
  7.9 10.6 %collective-permute-start.3 = (bf16[64,512]{1,0:T(8,128)(2,1)S(1)}, bf16[64,512]{1,0:T(8,128)(2,1)S(1)}, u32[]{:S(2)}, u32[]{:S(2)}) collective-permute-start(bf16[64,512]{1,0:T(8,128)(2,1)S(1)} %get-tuple-element.35), channel_id=1, source_target_pairs={{0,4},{1,5},{2,6},{3,7},{4,0},{5,1},{6,2},{7,3},{8,12},{9,13},{10,... | collective-permute-start | bytes 196616 | tf_op jit(solution)/shard_map/ppermute | solution.py:251
  10.9 8.8 %collective-permute-start.4 = (bf16[64,512]{1,0:T(8,128)(2,1)S(1)}, bf16[64,512]{1,0:T(8,128)(2,1)S(1)}, u32[]{:S(2)}, u32[]{:S(2)}) collective-permute-start(bf16[64,512]{1,0:T(8,128)(2,1)S(1)} %get-tuple-element.36), channel_id=1, source_target_pairs={{0,5},{1,4},{2,7},{3,6},{4,1},{5,0},{6,3},{7,2},{8,13},{9,12},{10,... | collective-permute-start | bytes 196616 | tf_op jit(solution)/shard_map/ppermute | solution.py:251
  14.6 6.2 %collective-permute-start.5 = (bf16[64,512]{1,0:T(8,128)(2,1)S(1)}, bf16[64,512]{1,0:T(8,128)(2,1)S(1)}, u32[]{:S(2)}, u32[]{:S(2)}) collective-permute-start(bf16[64,512]{1,0:T(8,128)(2,1)S(1)} %get-tuple-element.37), channel_id=1, source_target_pairs={{0,6},{1,7},{2,4},{3,5},{4,2},{5,3},{6,0},{7,1},{8,14},{9,15},{10,... | collective-permute-start | bytes 196616 | tf_op jit(solution)/shard_map/ppermute | solution.py:251
  18.3 7.0 %collective-permute-start.6 = (bf16[64,512]{1,0:T(8,128)(2,1)S(1)}, bf16[64,512]{1,0:T(8,128)(2,1)S(1)}, u32[]{:S(2)}, u32[]{:S(2)}) collective-permute-start(bf16[64,512]{1,0:T(8,128)(2,1)S(1)} %get-tuple-element.38), channel_id=1, source_target_pairs={{0,7},{1,6},{2,5},{3,4},{4,3},{5,2},{6,1},{7,0},{8,15},{9,14},{10,... | collective-permute-start | bytes 196616 | tf_op jit(solution)/shard_map/ppermute | solution.py:251
  25.2 1.2 %copy-start.2 = (f32[1,512,512]{2,1,0:T(8,128)S(1)}, f32[1,512,512]{2,1,0:T(8,128)}, u32[]{:S(2)}) copy-start(f32[1,512,512]{2,1,0:T(8,128)} %param.6) | copy-start | bytes 3145732
  26.5 18.3 %copy-start = (f32[1,512,512]{2,1,0:T(8,128)S(1)}, f32[1,512,512]{2,1,0:T(8,128)}, u32[]{:S(2)}) copy-start(f32[1,512,512]{2,1,0:T(8,128)} %param.7) | copy-start | bytes 3145732
  29.2 6.6 %collective-permute-start.7 = (f32[136,512]{1,0:T(8,128)S(1)}, f32[136,512]{1,0:T(8,128)S(1)}, u32[]{:S(2)}, u32[]{:S(2)}) collective-permute-start(f32[136,512]{1,0:T(8,128)S(1)} %get-tuple-element.42), channel_id=1, source_target_pairs={{0,1},{1,0},{2,3},{3,2},{4,5},{5,4},{6,7},{7,6},{8,9},{9,8},{10,11... | collective-permute-start | bytes 835592 | tf_op jit(solution)/shard_map/ppermute | solution.py:34
  29.7 7.5 %collective-permute-start.9 = (f32[136,512]{1,0:T(8,128)S(1)}, f32[136,512]{1,0:T(8,128)S(1)}, u32[]{:S(2)}, u32[]{:S(2)}) collective-permute-start(f32[136,512]{1,0:T(8,128)S(1)} %get-tuple-element.43), channel_id=1, source_target_pairs={{0,2},{2,0},{1,3},{3,1},{4,6},{6,4},{5,7},{7,5},{8,10},{10,8},{9,1... | collective-permute-start | bytes 835592 | tf_op jit(solution)/shard_map/ppermute | solution.py:34
  35.8 6.6 %collective-permute-start.8 = (f32[136,512]{1,0:T(8,128)S(1)}, f32[136,512]{1,0:T(8,128)S(1)}, u32[]{:S(2)}, u32[]{:S(2)}) collective-permute-start(f32[136,512]{1,0:T(8,128)S(1)} %add.17.a0), channel_id=1, source_target_pairs={{0,2},{2,0},{1,3},{3,1},{4,6},{6,4},{5,7},{7,5},{8,10},{10,8},{9,1... | collective-permute-start | bytes 835592 | tf_op jit(solution)/shard_map/ppermute | solution.py:34
  37.3 7.5 %collective-permute-start.10 = (f32[136,512]{1,0:T(8,128)S(1)}, f32[136,512]{1,0:T(8,128)S(1)}, u32[]{:S(2)}, u32[]{:S(2)}) collective-permute-start(f32[136,512]{1,0:T(8,128)S(1)} %add.18.b0), channel_id=1, source_target_pairs={{0,1},{1,0},{2,3},{3,2},{4,5},{5,4},{6,7},{7,6},{8,9},{9,8},{10,11... | collective-permute-start | bytes 835592 | tf_op jit(solution)/shard_map/ppermute | solution.py:34
  60.5 19.9 %collective-permute-start.14 = (bf16[512,512]{1,0:T(8,128)(2,1)S(1)}, bf16[512,512]{1,0:T(8,128)(2,1)S(1)}, u32[]{:S(2)}, u32[]{:S(2)}) collective-permute-start(bf16[512,512]{1,0:T(8,128)(2,1)S(1)} %get-tuple-element.47.refs_0_), channel_id=1, source_target_pairs={{0,16},{8,24},{16,0},{24,8},{1,17},{9,25},{17,1},{25,9},{2,18},{10... | collective-permute-start | bytes 1572872 | tf_op jit(solution)/shard_map/ppermute | solution.py:251
  62.0 17.8 %collective-permute-start.21 = (bf16[256,512]{1,0:T(8,128)(2,1)S(1)}, bf16[256,512]{1,0:T(8,128)(2,1)S(1)}, u32[]{:S(2)}, u32[]{:S(2)}) collective-permute-start(bf16[256,512]{1,0:T(8,128)(2,1)S(1)} %get-tuple-element.53), channel_id=1, source_target_pairs={{0,4},{1,5},{2,6},{3,7},{4,0},{5,1},{6,2},{7,3},{8,12},{9,13},{10,... | collective-permute-start | bytes 786440 | tf_op jit(solution)/shard_map/ppermute | solution.py:251
  62.6 25.7 %collective-permute-start.12 = (bf16[512,512]{1,0:T(8,128)(2,1)S(1)}, bf16[512,512]{1,0:T(8,128)(2,1)S(1)}, u32[]{:S(2)}, u32[]{:S(2)}) collective-permute-start(bf16[512,512]{1,0:T(8,128)(2,1)S(1)} %get-tuple-element.47.refs_0_), channel_id=1, source_target_pairs={{0,8},{8,0},{16,24},{24,16},{1,9},{9,1},{17,25},{25,17},{2,10},{10... | collective-permute-start | bytes 1572872 | tf_op jit(solution)/shard_map/ppermute | solution.py:251
  62.6 20.9 %collective-permute-start.11 = (bf16[256,512]{1,0:T(8,128)(2,1)S(1)}, bf16[256,512]{1,0:T(8,128)(2,1)S(1)}, u32[]{:S(2)}, u32[]{:S(2)}) collective-permute-start(bf16[256,512]{1,0:T(8,128)(2,1)S(1)} %get-tuple-element.48), channel_id=1, source_target_pairs={{0,4},{1,5},{2,6},{3,7},{4,0},{5,1},{6,2},{7,3},{8,12},{9,13},{10,... | collective-permute-start | bytes 786440 | tf_op jit(solution)/shard_map/ppermute | solution.py:251
  79.9 8.4 %collective-permute-start.23 = (bf16[256,512]{1,0:T(8,128)(2,1)S(1)}, bf16[256,512]{1,0:T(8,128)(2,1)S(1)}, u32[]{:S(2)}, u32[]{:S(2)}) collective-permute-start(bf16[256,512]{1,0:T(8,128)(2,1)S(1)} %collective-permute-done.21.refs_1_), channel_id=1, source_target_pairs={{0,16},{8,24},{16,0},{24,8},{1,17},{9,25},{17,1},{25,9},{2,18},{10... | collective-permute-start | bytes 786440 | tf_op jit(solution)/shard_map/ppermute | solution.py:251
  80.4 11.5 %collective-permute-start.16 = (bf16[512,512]{1,0:T(8,128)(2,1)S(1)}, bf16[512,512]{1,0:T(8,128)(2,1)S(1)}, u32[]{:S(2)}, u32[]{:S(2)}) collective-permute-start(bf16[512,512]{1,0:T(8,128)(2,1)S(1)} %collective-permute-done.14.refs_4_), channel_id=1, source_target_pairs={{0,8},{8,0},{16,24},{24,16},{1,9},{9,1},{17,25},{25,17},{2,10},{10... | collective-permute-start | bytes 1572872 | tf_op jit(solution)/shard_map/ppermute | solution.py:251
  83.5 8.4 %collective-permute-start.15 = (bf16[256,512]{1,0:T(8,128)(2,1)S(1)}, bf16[256,512]{1,0:T(8,128)(2,1)S(1)}, u32[]{:S(2)}, u32[]{:S(2)}) collective-permute-start(bf16[256,512]{1,0:T(8,128)(2,1)S(1)} %collective-permute-done.11.refs_1_), channel_id=1, source_target_pairs={{0,16},{8,24},{16,0},{24,8},{1,17},{9,25},{17,1},{25,9},{2,18},{10... | collective-permute-start | bytes 786440 | tf_op jit(solution)/shard_map/ppermute | solution.py:251
  84.1 7.8 %collective-permute-start.22 = (bf16[256,512]{1,0:T(8,128)(2,1)S(1)}, bf16[256,512]{1,0:T(8,128)(2,1)S(1)}, u32[]{:S(2)}, u32[]{:S(2)}) collective-permute-start(bf16[256,512]{1,0:T(8,128)(2,1)S(1)} %collective-permute-done.21.refs_1_), channel_id=1, source_target_pairs={{0,8},{8,0},{16,24},{24,16},{1,9},{9,1},{17,25},{25,17},{2,10},{10... | collective-permute-start | bytes 786440 | tf_op jit(solution)/shard_map/ppermute | solution.py:251
  88.2 3.6 %collective-permute-start.24 = (bf16[256,512]{1,0:T(8,128)(2,1)S(1)}, bf16[256,512]{1,0:T(8,128)(2,1)S(1)}, u32[]{:S(2)}, u32[]{:S(2)}) collective-permute-start(bf16[256,512]{1,0:T(8,128)(2,1)S(1)} %collective-permute-done.23.refs_5_), channel_id=1, source_target_pairs={{0,8},{8,0},{16,24},{24,16},{1,9},{9,1},{17,25},{25,17},{2,10},{10... | collective-permute-start | bytes 786440 | tf_op jit(solution)/shard_map/ppermute | solution.py:251
  88.2 8.0 %collective-permute-start.13 = (bf16[256,512]{1,0:T(8,128)(2,1)S(1)}, bf16[256,512]{1,0:T(8,128)(2,1)S(1)}, u32[]{:S(2)}, u32[]{:S(2)}) collective-permute-start(bf16[256,512]{1,0:T(8,128)(2,1)S(1)} %collective-permute-done.11.refs_1_), channel_id=1, source_target_pairs={{0,8},{8,0},{16,24},{24,16},{1,9},{9,1},{17,25},{25,17},{2,10},{10... | collective-permute-start | bytes 786440 | tf_op jit(solution)/shard_map/ppermute | solution.py:251
  91.8 4.4 %collective-permute-start.17 = (bf16[256,512]{1,0:T(8,128)(2,1)S(1)}, bf16[256,512]{1,0:T(8,128)(2,1)S(1)}, u32[]{:S(2)}, u32[]{:S(2)}) collective-permute-start(bf16[256,512]{1,0:T(8,128)(2,1)S(1)} %collective-permute-done.15.refs_5_), channel_id=1, source_target_pairs={{0,8},{8,0},{16,24},{24,16},{1,9},{9,1},{17,25},{25,17},{2,10},{10... | collective-permute-start | bytes 786440 | tf_op jit(solution)/shard_map/ppermute | solution.py:251
  92.7 9.3 %copy-start.3 = (f32[512,512]{1,0:T(8,128)S(1)}, f32[512,512]{1,0:T(8,128)}, u32[]{:S(2)}) copy-start(f32[512,512]{1,0:T(8,128)} %get-tuple-element.45) | copy-start | bytes 3145732
  92.7 9.2 %collective-permute-start.25 = (bf16[256,512]{1,0:T(8,128)(2,1)S(1)}, bf16[256,512]{1,0:T(8,128)(2,1)S(1)}, u32[]{:S(2)}, u32[]{:S(2)}) collective-permute-start(bf16[256,512]{1,0:T(8,128)(2,1)S(1)} %get-tuple-element.55), channel_id=1, source_target_pairs={{0,1},{1,0},{2,3},{3,2},{4,5},{5,4},{6,7},{7,6},{8,9},{9,8},{10,11... | collective-permute-start | bytes 786440 | tf_op jit(solution)/shard_map/ppermute | solution.py:251
  94.5 9.2 %collective-permute-start.26 = (bf16[256,512]{1,0:T(8,128)(2,1)S(1)}, bf16[256,512]{1,0:T(8,128)(2,1)S(1)}, u32[]{:S(2)}, u32[]{:S(2)}) collective-permute-start(bf16[256,512]{1,0:T(8,128)(2,1)S(1)} %get-tuple-element.56), channel_id=1, source_target_pairs={{0,2},{1,3},{2,0},{3,1},{4,6},{5,7},{6,4},{7,5},{8,10},{9,11},{10,... | collective-permute-start | bytes 786440 | tf_op jit(solution)/shard_map/ppermute | solution.py:251
  94.5 14.5 %collective-permute-start.27 = (bf16[256,512]{1,0:T(8,128)(2,1)S(1)}, bf16[256,512]{1,0:T(8,128)(2,1)S(1)}, u32[]{:S(2)}, u32[]{:S(2)}) collective-permute-start(bf16[256,512]{1,0:T(8,128)(2,1)S(1)} %get-tuple-element.57), channel_id=1, source_target_pairs={{0,3},{1,2},{2,1},{3,0},{4,7},{5,6},{6,5},{7,4},{8,11},{9,10},{10,... | collective-permute-start | bytes 786440 | tf_op jit(solution)/shard_map/ppermute | solution.py:251
  97.1 15.6 %collective-permute-start.18 = (bf16[256,512]{1,0:T(8,128)(2,1)S(1)}, bf16[256,512]{1,0:T(8,128)(2,1)S(1)}, u32[]{:S(2)}, u32[]{:S(2)}) collective-permute-start(bf16[256,512]{1,0:T(8,128)(2,1)S(1)} %get-tuple-element.50), channel_id=1, source_target_pairs={{0,1},{1,0},{2,3},{3,2},{4,5},{5,4},{6,7},{7,6},{8,9},{9,8},{10,11... | collective-permute-start | bytes 786440 | tf_op jit(solution)/shard_map/ppermute | solution.py:251
  98.9 16.1 %collective-permute-start.19 = (bf16[256,512]{1,0:T(8,128)(2,1)S(1)}, bf16[256,512]{1,0:T(8,128)(2,1)S(1)}, u32[]{:S(2)}, u32[]{:S(2)}) collective-permute-start(bf16[256,512]{1,0:T(8,128)(2,1)S(1)} %get-tuple-element.51), channel_id=1, source_target_pairs={{0,2},{1,3},{2,0},{3,1},{4,6},{5,7},{6,4},{7,5},{8,10},{9,11},{10,... | collective-permute-start | bytes 786440 | tf_op jit(solution)/shard_map/ppermute | solution.py:251
  102.0 17.7 %collective-permute-start.20 = (bf16[256,512]{1,0:T(8,128)(2,1)S(1)}, bf16[256,512]{1,0:T(8,128)(2,1)S(1)}, u32[]{:S(2)}, u32[]{:S(2)}) collective-permute-start(bf16[256,512]{1,0:T(8,128)(2,1)S(1)} %get-tuple-element.52), channel_id=1, source_target_pairs={{0,3},{1,2},{2,1},{3,0},{4,7},{5,6},{6,5},{7,4},{8,11},{9,10},{10,... | collective-permute-start | bytes 786440 | tf_op jit(solution)/shard_map/ppermute | solution.py:251

commit v5 on v4

--- a/solution.py
+++ b/solution.py
@@ -76,7 +76,7 @@
     for turn, out in enumerate(outs):
         target = place ^ turn
         column = pl.multiple_of((target % share_count) * cols, cols)
-        block = gradient.at[owned[group, target // share_count], :, pl.ds(column, cols)]
+        block = gradient.at[owned[target // share_count, group], :, pl.ds(column, cols)]
         moves.append(pltpu.make_async_copy(block, out, done.at[turn]))
     for move in moves:
         move.start()
@@ -98,7 +98,7 @@
             flops=0, bytes_accessed=4 * gradient.size, transcendentals=0
         ),
         compiler_params=pltpu.CompilerParams(vmem_limit_bytes=8 << 20),
-    )(owned_matrix, gradient)
+    )(owned_matrix.T, gradient)
 
 
 def gram_kernel(m_ref, *refs):
@@ -205,7 +205,7 @@
     def advance(count):
         a = gram[...]
         a_parts = parts_of(a, count)
-        mixed_parts = parts_of(mixed_of(a, a_parts if count == 2 else parts_of(a, 2)), count)
+        mixed_parts = parts_of(mixed_of(a, a_parts), count)
         half_way = first_coeff * a + even_product(mixed_parts, a_parts)
         gram[...] = first_coeff * half_way + even_product(
             parts_of(half_way, count), mixed_parts

time: 121 us -> 121 us (level)
    unnamed x9 -> x10, local copies, waits for them, and re-layouts: 3.04 us -> 2.95 us
where the time goes in v5:
time: 121 us
  waiting for transfers between devices  62.5 us (52%)
  starting transfers between devices  27.6 us (23%)
  Pallas kernels  22.9 us (19%)
  other arithmetic  3.69 us (3%)
  local copies, waits for them, and re-layouts  3.13 us (3%)
    ppermute x24, waiting for transfers between devices, flipped(): lax.ppermute(block, axis, [(i, i ^ flip) for i in range(lax.axis_size(axi...  50.6 us
    ppermute x24, starting transfers between devices, flipped(): lax.ppermute(block, axis, [(i, i ^ flip) for i in range(lax.axis_size(axi...  23.9 us
    pallas_call x1, Pallas kernels, newton(): pl.pallas_call(functools.partial(newton_kernel, iters, scale), out_shape=...  15.7 us
    ppermute x4, waiting for transfers between devices, from_partner(): return lax.ppermute(block, axis, route)  11.9 us
    ppermute x4, starting transfers between devices, from_partner(): return lax.ppermute(block, axis, route)  3.61 us
    unnamed x10, local copies, waits for them, and re-layouts  2.95 us
    pallas_call x1, Pallas kernels, gram_halves(): pl.pallas_call(gram_kernel, out_shape=[f32, f32, half, half], in_specs=[v...  2.72 us
  transfers between devices with their start and end apart: 28, of which 17 were waited for; matrix products, arithmetic and copies ran while one was open for 3% of the time, Pallas kernels for 2%

profile of v5, /device:TPU:0, one launch (start us, length us, event | category | flops | bytes accessed | tf_op | source)
XLA Modules:
  0.0 120.5 jit_solution(9343780815933084388)
XLA Ops:
  0.6 1.0 copy-done.1
  3.2 3.1 %collective-permute-start = (bf16[64,512]{1,0:T(8,128)(2,1)S(1)}, bf16[64,512]{1,0:T(8,128)(2,1)S(1)}, u32[]{:S(2)}, u32[]{:S(2)}) collective-permute-start(bf16[64,512]{1,0:T(8,128)(2,1)S(1)} %get-tuple-element.32), channel_id=1, source_target_pairs={{0,1},{1,0},{2,3},{3,2},{4,5},{5,4},{6,7},{7,6},{8,9},{9,8},{10,11... | collective-permute-start | bytes 196616 | tf_op jit(solution)/shard_map/ppermute | solution.py:251
  6.2 1.6 %collective-permute-start.1 = (bf16[64,512]{1,0:T(8,128)(2,1)S(1)}, bf16[64,512]{1,0:T(8,128)(2,1)S(1)}, u32[]{:S(2)}, u32[]{:S(2)}) collective-permute-start(bf16[64,512]{1,0:T(8,128)(2,1)S(1)} %get-tuple-element.33), channel_id=1, source_target_pairs={{0,2},{1,3},{2,0},{3,1},{4,6},{5,7},{6,4},{7,5},{8,10},{9,11},{10,... | collective-permute-start | bytes 196616 | tf_op jit(solution)/shard_map/ppermute | solution.py:251
  7.8 3.0 %collective-permute-start.3 = (bf16[64,512]{1,0:T(8,128)(2,1)S(1)}, bf16[64,512]{1,0:T(8,128)(2,1)S(1)}, u32[]{:S(2)}, u32[]{:S(2)}) collective-permute-start(bf16[64,512]{1,0:T(8,128)(2,1)S(1)} %get-tuple-element.35), channel_id=1, source_target_pairs={{0,4},{1,5},{2,6},{3,7},{4,0},{5,1},{6,2},{7,3},{8,12},{9,13},{10,... | collective-permute-start | bytes 196616 | tf_op jit(solution)/shard_map/ppermute | solution.py:251
  10.8 1.3 %collective-permute-start.4 = (bf16[64,512]{1,0:T(8,128)(2,1)S(1)}, bf16[64,512]{1,0:T(8,128)(2,1)S(1)}, u32[]{:S(2)}, u32[]{:S(2)}) collective-permute-start(bf16[64,512]{1,0:T(8,128)(2,1)S(1)} %get-tuple-element.36), channel_id=1, source_target_pairs={{0,5},{1,4},{2,7},{3,6},{4,1},{5,0},{6,3},{7,2},{8,13},{9,12},{10,... | collective-permute-start | bytes 196616 | tf_op jit(solution)/shard_map/ppermute | solution.py:251
  14.5 3.7 %collective-permute-start.5 = (bf16[64,512]{1,0:T(8,128)(2,1)S(1)}, bf16[64,512]{1,0:T(8,128)(2,1)S(1)}, u32[]{:S(2)}, u32[]{:S(2)}) collective-permute-start(bf16[64,512]{1,0:T(8,128)(2,1)S(1)} %get-tuple-element.37), channel_id=1, source_target_pairs={{0,6},{1,7},{2,4},{3,5},{4,2},{5,3},{6,0},{7,1},{8,14},{9,15},{10,... | collective-permute-start | bytes 196616 | tf_op jit(solution)/shard_map/ppermute | solution.py:251
  18.4 1.2 %collective-permute-done.4.refs_5_ = bf16[64,512]{1,0:T(8,128)(2,1)S(1)} collective-permute-done((bf16[64,512]{1,0:T(8,128)(2,1)S(1)}, bf16[64,512]{1,0:T(8,128)(2,1)S(1)}, u32[]{:S(2)}, u32[]{:S(2)}) %collective-permute-start.4) | collective-permute-done | bytes 65568 | tf_op jit(solution)/shard_map/ppermute | solution.py:251
  19.6 1.1 collective-permute-done.5.refs_6_
  20.7 4.4 %collective-permute-done.6.refs_7_ = bf16[64,512]{1,0:T(8,128)(2,1)S(1)} collective-permute-done((bf16[64,512]{1,0:T(8,128)(2,1)S(1)}, bf16[64,512]{1,0:T(8,128)(2,1)S(1)}, u32[]{:S(2)}, u32[]{:S(2)}) %collective-permute-start.6) | collective-permute-done | bytes 65568 | tf_op jit(solution)/shard_map/ppermute | solution.py:251
  25.1 1.2 %copy-done.3 = f32[1,512,512]{2,1,0:T(8,128)S(1)} copy-done((f32[1,512,512]{2,1,0:T(8,128)S(1)}, f32[1,512,512]{2,1,0:T(8,128)}, u32[]{:S(2)}) %copy-start.3) | copy-done | bytes 1048600
  26.3 2.7 %shard_map.85 = (f32[512,512]{1,0:T(8,128)}, f32[512,512]{1,0:T(8,128)S(1)}, f32[136,512]{1,0:T(8,128)S(1)}, f32[136,512]{1,0:T(8,128)S(1)}) custom-call(f32[512,512]{1,0:T(8,128)S(1)} %bitcast.18, bf16[64,512]{1,0:T(8,128)(2,1)S(1)} %get-tuple-element.31.refs_0_, bf16[64,512]{1,0:T(8,128)(2,1)S(1)} %collective-permute-done.refs_1_, ...), custom_call_target="tpu_custom_call" | custom-call | flops 1073741824 | bytes 4194304 | tf_op jit(solution)/shard_map/pallas_call | solution.py:141
  29.6 6.0 %collective-permute-done.7 = f32[136,512]{1,0:T(8,128)S(1)} collective-permute-done((f32[136,512]{1,0:T(8,128)S(1)}, f32[136,512]{1,0:T(8,128)S(1)}, u32[]{:S(2)}, u32[]{:S(2)}) %collective-permute-start.7) | collective-permute-done | bytes 278560 | tf_op jit(solution)/shard_map/ppermute | solution.py:34
  35.8 1.3 %collective-permute-done.9 = f32[136,512]{1,0:T(8,128)S(1)} collective-permute-done((f32[136,512]{1,0:T(8,128)S(1)}, f32[136,512]{1,0:T(8,128)S(1)}, u32[]{:S(2)}, u32[]{:S(2)}) %collective-permute-start.9) | collective-permute-done | bytes 278560 | tf_op jit(solution)/shard_map/ppermute | solution.py:34
  37.2 2.9 %collective-permute-start.10 = (f32[136,512]{1,0:T(8,128)S(1)}, f32[136,512]{1,0:T(8,128)S(1)}, u32[]{:S(2)}, u32[]{:S(2)}) collective-permute-start(f32[136,512]{1,0:T(8,128)S(1)} %add.18.b0), channel_id=1, source_target_pairs={{0,1},{1,0},{2,3},{3,2},{4,5},{5,4},{6,7},{7,6},{8,9},{9,8},{10,11... | collective-permute-start | bytes 835592 | tf_op jit(solution)/shard_map/ppermute | solution.py:34
  40.1 2.2 %collective-permute-done.8.a1 = f32[136,512]{1,0:T(8,128)S(1)} collective-permute-done((f32[136,512]{1,0:T(8,128)S(1)}, f32[136,512]{1,0:T(8,128)S(1)}, u32[]{:S(2)}, u32[]{:S(2)}) %collective-permute-start.8) | collective-permute-done | bytes 278560 | tf_op jit(solution)/shard_map/ppermute | solution.py:34
  42.3 2.3 %collective-permute-done.10.b1 = f32[136,512]{1,0:T(8,128)S(1)} collective-permute-done((f32[136,512]{1,0:T(8,128)S(1)}, f32[136,512]{1,0:T(8,128)S(1)}, u32[]{:S(2)}, u32[]{:S(2)}) %collective-permute-start.10) | collective-permute-done | bytes 278560 | tf_op jit(solution)/shard_map/ppermute | solution.py:34
  44.7 15.7 %shard_map.86 = (f32[512,512]{1,0:T(8,128)}, bf16[512,512]{1,0:T(8,128)(2,1)S(1)}, bf16[256,512]{1,0:T(8,128)(2,1)S(1)}, bf16[256,512]{1,0:T(8,128)(2,1)S(1)}) custom-call(f32[136,512]{1,0:T(8,128)S(1)} %add.17.a0, f32[136,512]{1,0:T(8,128)S(1)} %collective-permute-done.8.a1, f32[136,512]{1,0:T(8,128)S(1)} %add.18.b0, ...), custom_call_target="tpu_custom_call" | custom-call | flops 16106127360 | bytes 6291456 | tf_op jit(solution)/shard_map/pallas_call | solution.py:234
  60.4 1.5 %collective-permute-start.14 = (bf16[512,512]{1,0:T(8,128)(2,1)S(1)}, bf16[512,512]{1,0:T(8,128)(2,1)S(1)}, u32[]{:S(2)}, u32[]{:S(2)}) collective-permute-start(bf16[512,512]{1,0:T(8,128)(2,1)S(1)} %get-tuple-element.47.refs_0_), channel_id=1, source_target_pairs={{0,16},{8,24},{16,0},{24,8},{1,17},{9,25},{17,1},{25,9},{2,18},{10... | collective-permute-start | bytes 1572872 | tf_op jit(solution)/shard_map/ppermute | solution.py:251
  62.5 2.3 %collective-permute-start.11 = (bf16[256,512]{1,0:T(8,128)(2,1)S(1)}, bf16[256,512]{1,0:T(8,128)(2,1)S(1)}, u32[]{:S(2)}, u32[]{:S(2)}) collective-permute-start(bf16[256,512]{1,0:T(8,128)(2,1)S(1)} %get-tuple-element.48), channel_id=1, source_target_pairs={{0,4},{1,5},{2,6},{3,7},{4,0},{5,1},{6,2},{7,3},{8,12},{9,13},{10,... | collective-permute-start | bytes 786440 | tf_op jit(solution)/shard_map/ppermute | solution.py:251
  64.8 14.9 %collective-permute-done.21.refs_1_ = bf16[256,512]{1,0:T(8,128)(2,1)S(1)} collective-permute-done((bf16[256,512]{1,0:T(8,128)(2,1)S(1)}, bf16[256,512]{1,0:T(8,128)(2,1)S(1)}, u32[]{:S(2)}, u32[]{:S(2)}) %collective-permute-start.21) | collective-permute-done | bytes 262176 | tf_op jit(solution)/shard_map/ppermute | solution.py:251
  80.3 3.1 %collective-permute-done.11.refs_1_ = bf16[256,512]{1,0:T(8,128)(2,1)S(1)} collective-permute-done((bf16[256,512]{1,0:T(8,128)(2,1)S(1)}, bf16[256,512]{1,0:T(8,128)(2,1)S(1)}, u32[]{:S(2)}, u32[]{:S(2)}) %collective-permute-start.11) | collective-permute-done | bytes 262176 | tf_op jit(solution)/shard_map/ppermute | solution.py:251
  83.9 4.1 %collective-permute-done.23.refs_5_ = bf16[256,512]{1,0:T(8,128)(2,1)S(1)} collective-permute-done((bf16[256,512]{1,0:T(8,128)(2,1)S(1)}, bf16[256,512]{1,0:T(8,128)(2,1)S(1)}, u32[]{:S(2)}, u32[]{:S(2)}) %collective-permute-start.23) | collective-permute-done | bytes 262176 | tf_op jit(solution)/shard_map/ppermute | solution.py:251
  88.5 3.2 %collective-permute-done.15.refs_5_ = bf16[256,512]{1,0:T(8,128)(2,1)S(1)} collective-permute-done((bf16[256,512]{1,0:T(8,128)(2,1)S(1)}, bf16[256,512]{1,0:T(8,128)(2,1)S(1)}, u32[]{:S(2)}, u32[]{:S(2)}) %collective-permute-start.15) | collective-permute-done | bytes 262176 | tf_op jit(solution)/shard_map/ppermute | solution.py:251
  92.6 1.8 %collective-permute-start.25 = (bf16[256,512]{1,0:T(8,128)(2,1)S(1)}, bf16[256,512]{1,0:T(8,128)(2,1)S(1)}, u32[]{:S(2)}, u32[]{:S(2)}) collective-permute-start(bf16[256,512]{1,0:T(8,128)(2,1)S(1)} %get-tuple-element.55), channel_id=1, source_target_pairs={{0,1},{1,0},{2,3},{3,2},{4,5},{5,4},{6,7},{7,6},{8,9},{9,8},{10,11... | collective-permute-start | bytes 786440 | tf_op jit(solution)/shard_map/ppermute | solution.py:251
  94.4 1.7 %collective-permute-start.27 = (bf16[256,512]{1,0:T(8,128)(2,1)S(1)}, bf16[256,512]{1,0:T(8,128)(2,1)S(1)}, u32[]{:S(2)}, u32[]{:S(2)}) collective-permute-start(bf16[256,512]{1,0:T(8,128)(2,1)S(1)} %get-tuple-element.57), channel_id=1, source_target_pairs={{0,3},{1,2},{2,1},{3,0},{4,7},{5,6},{6,5},{7,4},{8,11},{9,10},{10,... | collective-permute-start | bytes 786440 | tf_op jit(solution)/shard_map/ppermute | solution.py:251
  97.0 1.8 %collective-permute-start.18 = (bf16[256,512]{1,0:T(8,128)(2,1)S(1)}, bf16[256,512]{1,0:T(8,128)(2,1)S(1)}, u32[]{:S(2)}, u32[]{:S(2)}) collective-permute-start(bf16[256,512]{1,0:T(8,128)(2,1)S(1)} %get-tuple-element.50), channel_id=1, source_target_pairs={{0,1},{1,0},{2,3},{3,2},{4,5},{5,4},{6,7},{7,6},{8,9},{9,8},{10,11... | collective-permute-start | bytes 786440 | tf_op jit(solution)/shard_map/ppermute | solution.py:251
  98.8 3.0 %collective-permute-done.25.refs_1_ = bf16[256,512]{1,0:T(8,128)(2,1)S(1)} collective-permute-done((bf16[256,512]{1,0:T(8,128)(2,1)S(1)}, bf16[256,512]{1,0:T(8,128)(2,1)S(1)}, u32[]{:S(2)}, u32[]{:S(2)}) %collective-permute-start.25) | collective-permute-done | bytes 262176 | tf_op jit(solution)/shard_map/ppermute | solution.py:251
  101.9 1.2 %subtract_bitcast_fusion = f32[1,512,512]{2,1,0:T(8,128)} fusion(f32[512,512]{1,0:T(8,128)S(1)} %copy-done.4, f32[1,512,512]{2,1,0:T(8,128)S(1)} %copy-done), kind=kLoop, calls=%fused_computation | loop fusion | flops 1048576 | bytes 3145728 | tf_op jit(solution)/shard_map/broadcast_in_dim | solution.py:471
  103.6 5.4 %collective-permute-done.27.refs_3_ = bf16[256,512]{1,0:T(8,128)(2,1)S(1)} collective-permute-done((bf16[256,512]{1,0:T(8,128)(2,1)S(1)}, bf16[256,512]{1,0:T(8,128)(2,1)S(1)}, u32[]{:S(2)}, u32[]{:S(2)}) %collective-permute-start.27) | collective-permute-done | bytes 262176 | tf_op jit(solution)/shard_map/ppermute | solution.py:251
  110.0 2.6 %collective-permute-done.18.refs_1_ = bf16[256,512]{1,0:T(8,128)(2,1)S(1)} collective-permute-done((bf16[256,512]{1,0:T(8,128)(2,1)S(1)}, bf16[256,512]{1,0:T(8,128)(2,1)S(1)}, u32[]{:S(2)}, u32[]{:S(2)}) %collective-permute-start.18) | collective-permute-done | bytes 262176 | tf_op jit(solution)/shard_map/ppermute | solution.py:251
  112.6 2.3 %collective-permute-done.19.refs_2_ = bf16[256,512]{1,0:T(8,128)(2,1)S(1)} collective-permute-done((bf16[256,512]{1,0:T(8,128)(2,1)S(1)}, bf16[256,512]{1,0:T(8,128)(2,1)S(1)}, u32[]{:S(2)}, u32[]{:S(2)}) %collective-permute-start.19) | collective-permute-done | bytes 262176 | tf_op jit(solution)/shard_map/ppermute | solution.py:251
  114.9 4.7 %collective-permute-done.20.refs_3_ = bf16[256,512]{1,0:T(8,128)(2,1)S(1)} collective-permute-done((bf16[256,512]{1,0:T(8,128)(2,1)S(1)}, bf16[256,512]{1,0:T(8,128)(2,1)S(1)}, u32[]{:S(2)}, u32[]{:S(2)}) %collective-permute-start.20) | collective-permute-done | bytes 262176 | tf_op jit(solution)/shard_map/ppermute | solution.py:251
  (51 shorter events, 11.2 us)
Async XLA Ops:
  0.6 1.0 copy-start.1
  3.2 11.3 %collective-permute-start = (bf16[64,512]{1,0:T(8,128)(2,1)S(1)}, bf16[64,512]{1,0:T(8,128)(2,1)S(1)}, u32[]{:S(2)}, u32[]{:S(2)}) collective-permute-start(bf16[64,512]{1,0:T(8,128)(2,1)S(1)} %get-tuple-element.32), channel_id=1, source_target_pairs={{0,1},{1,0},{2,3},{3,2},{4,5},{5,4},{6,7},{7,6},{8,9},{9,8},{10,11... | collective-permute-start | bytes 196616 | tf_op jit(solution)/shard_map/ppermute | solution.py:251
  6.2 11.9 %collective-permute-start.1 = (bf16[64,512]{1,0:T(8,128)(2,1)S(1)}, bf16[64,512]{1,0:T(8,128)(2,1)S(1)}, u32[]{:S(2)}, u32[]{:S(2)}) collective-permute-start(bf16[64,512]{1,0:T(8,128)(2,1)S(1)} %get-tuple-element.33), channel_id=1, source_target_pairs={{0,2},{1,3},{2,0},{3,1},{4,6},{5,7},{6,4},{7,5},{8,10},{9,11},{10,... | collective-permute-start | bytes 196616 | tf_op jit(solution)/shard_map/ppermute | solution.py:251
  7.8 10.6 %collective-permute-start.2 = (bf16[64,512]{1,0:T(8,128)(2,1)S(1)}, bf16[64,512]{1,0:T(8,128)(2,1)S(1)}, u32[]{:S(2)}, u32[]{:S(2)}) collective-permute-start(bf16[64,512]{1,0:T(8,128)(2,1)S(1)} %get-tuple-element.34), channel_id=1, source_target_pairs={{0,3},{1,2},{2,1},{3,0},{4,7},{5,6},{6,5},{7,4},{8,11},{9,10},{10,... | collective-permute-start | bytes 196616 | tf_op jit(solution)/shard_map/ppermute | solution.py:251
  7.8 10.6 %collective-permute-start.3 = (bf16[64,512]{1,0:T(8,128)(2,1)S(1)}, bf16[64,512]{1,0:T(8,128)(2,1)S(1)}, u32[]{:S(2)}, u32[]{:S(2)}) collective-permute-start(bf16[64,512]{1,0:T(8,128)(2,1)S(1)} %get-tuple-element.35), channel_id=1, source_target_pairs={{0,4},{1,5},{2,6},{3,7},{4,0},{5,1},{6,2},{7,3},{8,12},{9,13},{10,... | collective-permute-start | bytes 196616 | tf_op jit(solution)/shard_map/ppermute | solution.py:251
  10.8 8.8 %collective-permute-start.4 = (bf16[64,512]{1,0:T(8,128)(2,1)S(1)}, bf16[64,512]{1,0:T(8,128)(2,1)S(1)}, u32[]{:S(2)}, u32[]{:S(2)}) collective-permute-start(bf16[64,512]{1,0:T(8,128)(2,1)S(1)} %get-tuple-element.36), channel_id=1, source_target_pairs={{0,5},{1,4},{2,7},{3,6},{4,1},{5,0},{6,3},{7,2},{8,13},{9,12},{10,... | collective-permute-start | bytes 196616 | tf_op jit(solution)/shard_map/ppermute | solution.py:251
  14.5 6.2 %collective-permute-start.5 = (bf16[64,512]{1,0:T(8,128)(2,1)S(1)}, bf16[64,512]{1,0:T(8,128)(2,1)S(1)}, u32[]{:S(2)}, u32[]{:S(2)}) collective-permute-start(bf16[64,512]{1,0:T(8,128)(2,1)S(1)} %get-tuple-element.37), channel_id=1, source_target_pairs={{0,6},{1,7},{2,4},{3,5},{4,2},{5,3},{6,0},{7,1},{8,14},{9,15},{10,... | collective-permute-start | bytes 196616 | tf_op jit(solution)/shard_map/ppermute | solution.py:251
  18.2 7.0 %collective-permute-start.6 = (bf16[64,512]{1,0:T(8,128)(2,1)S(1)}, bf16[64,512]{1,0:T(8,128)(2,1)S(1)}, u32[]{:S(2)}, u32[]{:S(2)}) collective-permute-start(bf16[64,512]{1,0:T(8,128)(2,1)S(1)} %get-tuple-element.38), channel_id=1, source_target_pairs={{0,7},{1,6},{2,5},{3,4},{4,3},{5,2},{6,1},{7,0},{8,15},{9,14},{10,... | collective-permute-start | bytes 196616 | tf_op jit(solution)/shard_map/ppermute | solution.py:251
  25.1 1.2 %copy-start.3 = (f32[1,512,512]{2,1,0:T(8,128)S(1)}, f32[1,512,512]{2,1,0:T(8,128)}, u32[]{:S(2)}) copy-start(f32[1,512,512]{2,1,0:T(8,128)} %param.6) | copy-start | bytes 3145732
  26.3 18.3 %copy-start = (f32[1,512,512]{2,1,0:T(8,128)S(1)}, f32[1,512,512]{2,1,0:T(8,128)}, u32[]{:S(2)}) copy-start(f32[1,512,512]{2,1,0:T(8,128)} %param.7) | copy-start | bytes 3145732
  29.1 6.6 %collective-permute-start.7 = (f32[136,512]{1,0:T(8,128)S(1)}, f32[136,512]{1,0:T(8,128)S(1)}, u32[]{:S(2)}, u32[]{:S(2)}) collective-permute-start(f32[136,512]{1,0:T(8,128)S(1)} %get-tuple-element.42), channel_id=1, source_target_pairs={{0,1},{1,0},{2,3},{3,2},{4,5},{5,4},{6,7},{7,6},{8,9},{9,8},{10,11... | collective-permute-start | bytes 835592 | tf_op jit(solution)/shard_map/ppermute | solution.py:34
  29.6 7.5 %collective-permute-start.9 = (f32[136,512]{1,0:T(8,128)S(1)}, f32[136,512]{1,0:T(8,128)S(1)}, u32[]{:S(2)}, u32[]{:S(2)}) collective-permute-start(f32[136,512]{1,0:T(8,128)S(1)} %get-tuple-element.43), channel_id=1, source_target_pairs={{0,2},{2,0},{1,3},{3,1},{4,6},{6,4},{5,7},{7,5},{8,10},{10,8},{9,1... | collective-permute-start | bytes 835592 | tf_op jit(solution)/shard_map/ppermute | solution.py:34
  35.7 6.6 %collective-permute-start.8 = (f32[136,512]{1,0:T(8,128)S(1)}, f32[136,512]{1,0:T(8,128)S(1)}, u32[]{:S(2)}, u32[]{:S(2)}) collective-permute-start(f32[136,512]{1,0:T(8,128)S(1)} %add.17.a0), channel_id=1, source_target_pairs={{0,2},{2,0},{1,3},{3,1},{4,6},{6,4},{5,7},{7,5},{8,10},{10,8},{9,1... | collective-permute-start | bytes 835592 | tf_op jit(solution)/shard_map/ppermute | solution.py:34
  37.2 7.5 %collective-permute-start.10 = (f32[136,512]{1,0:T(8,128)S(1)}, f32[136,512]{1,0:T(8,128)S(1)}, u32[]{:S(2)}, u32[]{:S(2)}) collective-permute-start(f32[136,512]{1,0:T(8,128)S(1)} %add.18.b0), channel_id=1, source_target_pairs={{0,1},{1,0},{2,3},{3,2},{4,5},{5,4},{6,7},{7,6},{8,9},{9,8},{10,11... | collective-permute-start | bytes 835592 | tf_op jit(solution)/shard_map/ppermute | solution.py:34
  60.4 19.9 %collective-permute-start.14 = (bf16[512,512]{1,0:T(8,128)(2,1)S(1)}, bf16[512,512]{1,0:T(8,128)(2,1)S(1)}, u32[]{:S(2)}, u32[]{:S(2)}) collective-permute-start(bf16[512,512]{1,0:T(8,128)(2,1)S(1)} %get-tuple-element.47.refs_0_), channel_id=1, source_target_pairs={{0,16},{8,24},{16,0},{24,8},{1,17},{9,25},{17,1},{25,9},{2,18},{10... | collective-permute-start | bytes 1572872 | tf_op jit(solution)/shard_map/ppermute | solution.py:251
  61.9 17.9 %collective-permute-start.21 = (bf16[256,512]{1,0:T(8,128)(2,1)S(1)}, bf16[256,512]{1,0:T(8,128)(2,1)S(1)}, u32[]{:S(2)}, u32[]{:S(2)}) collective-permute-start(bf16[256,512]{1,0:T(8,128)(2,1)S(1)} %get-tuple-element.53), channel_id=1, source_target_pairs={{0,4},{1,5},{2,6},{3,7},{4,0},{5,1},{6,2},{7,3},{8,12},{9,13},{10,... | collective-permute-start | bytes 786440 | tf_op jit(solution)/shard_map/ppermute | solution.py:251
  62.5 25.5 %collective-permute-start.12 = (bf16[512,512]{1,0:T(8,128)(2,1)S(1)}, bf16[512,512]{1,0:T(8,128)(2,1)S(1)}, u32[]{:S(2)}, u32[]{:S(2)}) collective-permute-start(bf16[512,512]{1,0:T(8,128)(2,1)S(1)} %get-tuple-element.47.refs_0_), channel_id=1, source_target_pairs={{0,8},{8,0},{16,24},{24,16},{1,9},{9,1},{17,25},{25,17},{2,10},{10... | collective-permute-start | bytes 1572872 | tf_op jit(solution)/shard_map/ppermute | solution.py:251
  62.5 20.9 %collective-permute-start.11 = (bf16[256,512]{1,0:T(8,128)(2,1)S(1)}, bf16[256,512]{1,0:T(8,128)(2,1)S(1)}, u32[]{:S(2)}, u32[]{:S(2)}) collective-permute-start(bf16[256,512]{1,0:T(8,128)(2,1)S(1)} %get-tuple-element.48), channel_id=1, source_target_pairs={{0,4},{1,5},{2,6},{3,7},{4,0},{5,1},{6,2},{7,3},{8,12},{9,13},{10,... | collective-permute-start | bytes 786440 | tf_op jit(solution)/shard_map/ppermute | solution.py:251
  79.8 8.3 %collective-permute-start.23 = (bf16[256,512]{1,0:T(8,128)(2,1)S(1)}, bf16[256,512]{1,0:T(8,128)(2,1)S(1)}, u32[]{:S(2)}, u32[]{:S(2)}) collective-permute-start(bf16[256,512]{1,0:T(8,128)(2,1)S(1)} %collective-permute-done.21.refs_1_), channel_id=1, source_target_pairs={{0,16},{8,24},{16,0},{24,8},{1,17},{9,25},{17,1},{25,9},{2,18},{10... | collective-permute-start | bytes 786440 | tf_op jit(solution)/shard_map/ppermute | solution.py:251
  80.3 11.5 %collective-permute-start.16 = (bf16[512,512]{1,0:T(8,128)(2,1)S(1)}, bf16[512,512]{1,0:T(8,128)(2,1)S(1)}, u32[]{:S(2)}, u32[]{:S(2)}) collective-permute-start(bf16[512,512]{1,0:T(8,128)(2,1)S(1)} %collective-permute-done.14.refs_4_), channel_id=1, source_target_pairs={{0,8},{8,0},{16,24},{24,16},{1,9},{9,1},{17,25},{25,17},{2,10},{10... | collective-permute-start | bytes 1572872 | tf_op jit(solution)/shard_map/ppermute | solution.py:251
  83.5 8.3 %collective-permute-start.15 = (bf16[256,512]{1,0:T(8,128)(2,1)S(1)}, bf16[256,512]{1,0:T(8,128)(2,1)S(1)}, u32[]{:S(2)}, u32[]{:S(2)}) collective-permute-start(bf16[256,512]{1,0:T(8,128)(2,1)S(1)} %collective-permute-done.11.refs_1_), channel_id=1, source_target_pairs={{0,16},{8,24},{16,0},{24,8},{1,17},{9,25},{17,1},{25,9},{2,18},{10... | collective-permute-start | bytes 786440 | tf_op jit(solution)/shard_map/ppermute | solution.py:251
  83.9 7.8 %collective-permute-start.22 = (bf16[256,512]{1,0:T(8,128)(2,1)S(1)}, bf16[256,512]{1,0:T(8,128)(2,1)S(1)}, u32[]{:S(2)}, u32[]{:S(2)}) collective-permute-start(bf16[256,512]{1,0:T(8,128)(2,1)S(1)} %collective-permute-done.21.refs_1_), channel_id=1, source_target_pairs={{0,8},{8,0},{16,24},{24,16},{1,9},{9,1},{17,25},{25,17},{2,10},{10... | collective-permute-start | bytes 786440 | tf_op jit(solution)/shard_map/ppermute | solution.py:251
  88.0 3.7 %collective-permute-start.24 = (bf16[256,512]{1,0:T(8,128)(2,1)S(1)}, bf16[256,512]{1,0:T(8,128)(2,1)S(1)}, u32[]{:S(2)}, u32[]{:S(2)}) collective-permute-start(bf16[256,512]{1,0:T(8,128)(2,1)S(1)} %collective-permute-done.23.refs_5_), channel_id=1, source_target_pairs={{0,8},{8,0},{16,24},{24,16},{1,9},{9,1},{17,25},{25,17},{2,10},{10... | collective-permute-start | bytes 786440 | tf_op jit(solution)/shard_map/ppermute | solution.py:251
  88.0 8.2 %collective-permute-start.13 = (bf16[256,512]{1,0:T(8,128)(2,1)S(1)}, bf16[256,512]{1,0:T(8,128)(2,1)S(1)}, u32[]{:S(2)}, u32[]{:S(2)}) collective-permute-start(bf16[256,512]{1,0:T(8,128)(2,1)S(1)} %collective-permute-done.11.refs_1_), channel_id=1, source_target_pairs={{0,8},{8,0},{16,24},{24,16},{1,9},{9,1},{17,25},{25,17},{2,10},{10... | collective-permute-start | bytes 786440 | tf_op jit(solution)/shard_map/ppermute | solution.py:251
  91.7 4.4 %collective-permute-start.17 = (bf16[256,512]{1,0:T(8,128)(2,1)S(1)}, bf16[256,512]{1,0:T(8,128)(2,1)S(1)}, u32[]{:S(2)}, u32[]{:S(2)}) collective-permute-start(bf16[256,512]{1,0:T(8,128)(2,1)S(1)} %collective-permute-done.15.refs_5_), channel_id=1, source_target_pairs={{0,8},{8,0},{16,24},{24,16},{1,9},{9,1},{17,25},{25,17},{2,10},{10... | collective-permute-start | bytes 786440 | tf_op jit(solution)/shard_map/ppermute | solution.py:251
  92.6 9.3 %copy-start.4 = (f32[512,512]{1,0:T(8,128)S(1)}, f32[512,512]{1,0:T(8,128)}, u32[]{:S(2)}) copy-start(f32[512,512]{1,0:T(8,128)} %get-tuple-element.45) | copy-start | bytes 3145732
  92.6 9.2 %collective-permute-start.25 = (bf16[256,512]{1,0:T(8,128)(2,1)S(1)}, bf16[256,512]{1,0:T(8,128)(2,1)S(1)}, u32[]{:S(2)}, u32[]{:S(2)}) collective-permute-start(bf16[256,512]{1,0:T(8,128)(2,1)S(1)} %get-tuple-element.55), channel_id=1, source_target_pairs={{0,1},{1,0},{2,3},{3,2},{4,5},{5,4},{6,7},{7,6},{8,9},{9,8},{10,11... | collective-permute-start | bytes 786440 | tf_op jit(solution)/shard_map/ppermute | solution.py:251
  94.4 9.2 %collective-permute-start.26 = (bf16[256,512]{1,0:T(8,128)(2,1)S(1)}, bf16[256,512]{1,0:T(8,128)(2,1)S(1)}, u32[]{:S(2)}, u32[]{:S(2)}) collective-permute-start(bf16[256,512]{1,0:T(8,128)(2,1)S(1)} %get-tuple-element.56), channel_id=1, source_target_pairs={{0,2},{1,3},{2,0},{3,1},{4,6},{5,7},{6,4},{7,5},{8,10},{9,11},{10,... | collective-permute-start | bytes 786440 | tf_op jit(solution)/shard_map/ppermute | solution.py:251
  94.4 14.6 %collective-permute-start.27 = (bf16[256,512]{1,0:T(8,128)(2,1)S(1)}, bf16[256,512]{1,0:T(8,128)(2,1)S(1)}, u32[]{:S(2)}, u32[]{:S(2)}) collective-permute-start(bf16[256,512]{1,0:T(8,128)(2,1)S(1)} %get-tuple-element.57), channel_id=1, source_target_pairs={{0,3},{1,2},{2,1},{3,0},{4,7},{5,6},{6,5},{7,4},{8,11},{9,10},{10,... | collective-permute-start | bytes 786440 | tf_op jit(solution)/shard_map/ppermute | solution.py:251
  97.0 15.6 %collective-permute-start.18 = (bf16[256,512]{1,0:T(8,128)(2,1)S(1)}, bf16[256,512]{1,0:T(8,128)(2,1)S(1)}, u32[]{:S(2)}, u32[]{:S(2)}) collective-permute-start(bf16[256,512]{1,0:T(8,128)(2,1)S(1)} %get-tuple-element.50), channel_id=1, source_target_pairs={{0,1},{1,0},{2,3},{3,2},{4,5},{5,4},{6,7},{7,6},{8,9},{9,8},{10,11... | collective-permute-start | bytes 786440 | tf_op jit(solution)/shard_map/ppermute | solution.py:251
  98.8 16.1 %collective-permute-start.19 = (bf16[256,512]{1,0:T(8,128)(2,1)S(1)}, bf16[256,512]{1,0:T(8,128)(2,1)S(1)}, u32[]{:S(2)}, u32[]{:S(2)}) collective-permute-start(bf16[256,512]{1,0:T(8,128)(2,1)S(1)} %get-tuple-element.51), channel_id=1, source_target_pairs={{0,2},{1,3},{2,0},{3,1},{4,6},{5,7},{6,4},{7,5},{8,10},{9,11},{10,... | collective-permute-start | bytes 786440 | tf_op jit(solution)/shard_map/ppermute | solution.py:251
  101.9 17.7 %collective-permute-start.20 = (bf16[256,512]{1,0:T(8,128)(2,1)S(1)}, bf16[256,512]{1,0:T(8,128)(2,1)S(1)}, u32[]{:S(2)}, u32[]{:S(2)}) collective-permute-start(bf16[256,512]{1,0:T(8,128)(2,1)S(1)} %get-tuple-element.52), channel_id=1, source_target_pairs={{0,3},{1,2},{2,1},{3,0},{4,7},{5,6},{6,5},{7,4},{8,11},{9,10},{10,... | collective-permute-start | bytes 786440 | tf_op jit(solution)/shard_map/ppermute | solution.py:251
  (1 other events, 0.7 us)
